TPU v7x, 32 devices: a whole 2x2x4 slice. The times are simulated.
32 devices in a mesh: grp: 2 (over y), sp: 4 (over x, core), ch: 4 (over z).
Axes of the slice: x: 2, y: 2, z: 4, core: 2. Of those that a mesh axis runs over, the one named last changes fastest.
Arguments:
- flow: float32 [4, 64, 64, 256], P(None, ('grp', 'sp'), 'ch'), may hold values from -6 to 6
- embed_w: bfloat16 [2048, 512], P(None, 'ch'), may hold values from -0.125 to 0.125
- conv_w: bfloat16 [2, 27, 512, 512], P(None, None, None, 'ch'), may hold values from -0.109375 to 0.109375
- dec_w: bfloat16 [512, 2048], P(None, 'ch'), may hold values from -0.25 to 0.25
- conv_m: float32 [2, 27, 512, 512], P(None, None, ('grp', 'sp'), 'ch'), may hold values from -0.00018 to 0.00018
- conv_v: float32 [2, 27, 512, 512], P(None, None, ('grp', 'sp'), 'ch'), may hold values from 1e-10 to 1e-07
- dec_m: float32 [512, 2048], P(('grp', 'sp'), 'ch'), may hold values from -0.0006 to 0.0006
- dec_v: float32 [512, 2048], P(('grp', 'sp'), 'ch'), may hold values from 1e-09 to 1e-06
- loss_mask: int32 [8, 8, 32], P(('grp', 'sp')), may hold values 0 or 1
Outputs:
- flow_next: float32 [4, 64, 64, 256], P(None, ('grp', 'sp'), 'ch')
- loss: float32 [], replicated
- conv_w_next: bfloat16 [2, 27, 512, 512], P(None, None, None, 'ch')
- dec_w_next: bfloat16 [512, 2048], P(None, 'ch')
- conv_m_next: float32 [2, 27, 512, 512], P(None, None, ('grp', 'sp'), 'ch')
- conv_v_next: float32 [2, 27, 512, 512], P(None, None, ('grp', 'sp'), 'ch')
- dec_m_next: float32 [512, 2048], P(('grp', 'sp'), 'ch')
- dec_v_next: float32 [512, 2048], P(('grp', 'sp'), 'ch')
All inputs are finite; a program needn't handle non-finite values. No bound on the sum of `loss_mask` on one device may be relied on, other than what follows from the above.
Results may differ from a plain program's by a relative error of at most 0.01.
Values may be sent and summed in bfloat16 or wider, within the bound.
No kernel may reach another device: no remote copies, remote signals or barrier semaphores. Data moves between devices by JAX's collectives and lax.ppermute only.
A program may use at most 192 MiB of HBM per device.

v0:
```python
import jax
import jax.numpy as jnp
from jax import lax
from jax.sharding import PartitionSpec as P

PATCH = 8
FLOW_STEPS = 2
OUT = 2048


time_step = 0.1
viscosity = 0.2
beta_one = 0.9
beta_two = 0.95
learn_rate = 0.001
adam_eps = 1e-08
bias_one = 0.9999734386011124
bias_two = 0.994079470779666


def with_halo(block, sides, width):
    for axis, dim in sides:
        count = lax.axis_size(axis)
        forward = [(i, i + 1) for i in range(count - 1)]
        forward.append((count - 1, 0))
        backward = [(target, source) for source, target in forward]
        low = lax.ppermute(
            lax.slice_in_dim(block, block.shape[dim] - width, None, axis=dim), axis, forward
        )
        high = lax.ppermute(lax.slice_in_dim(block, 0, width, axis=dim), axis, backward)
        block = jnp.concatenate([low, block, high], axis=dim)
    return block


def advance(padded):
    center = padded[:, 1:-1, 1:-1]
    east = padded[:, 2:, 1:-1]
    west = padded[:, :-2, 1:-1]
    north = padded[:, 1:-1, 2:]
    south = padded[:, 1:-1, :-2]
    upper = jnp.roll(center, -1, 3)
    lower = jnp.roll(center, 1, 3)
    laplace = east + west + north + south + upper + lower - 6.0 * center
    carried = (
        center[0:1] * (east - west) * 0.5
        + center[1:2] * (north - south) * 0.5
        + center[2:3] * (upper - lower) * 0.5
    )
    return center + time_step * (viscosity * laplace - carried)


def to_patches(field):
    fields, depth, span, length = field.shape
    blocks = field.reshape(fields, PATCH, span // PATCH, PATCH, length // PATCH, PATCH)
    return blocks.transpose(2, 4, 0, 1, 3, 5).reshape(
        span // PATCH * (length // PATCH), fields * PATCH**3
    )


def unfold(planes):
    parts = []
    for plane in range(3):
        for down in (-1, 0, 1):
            for across in (-1, 0, 1):
                parts.append(jnp.roll(planes[plane], (-down, -across), (0, 1)))
    stacked = jnp.concatenate(parts, axis=-1)
    return stacked.reshape(-1, stacked.shape[-1])


def unfold_back(planes):
    parts = []
    for plane in range(3):
        for down in (-1, 0, 1):
            for across in (-1, 0, 1):
                parts.append(jnp.roll(planes[2 - plane], (down, across), (0, 1)))
    stacked = jnp.concatenate(parts, axis=-1)
    return stacked.reshape(-1, stacked.shape[-1])


def spread(act, rows_y, rows_z):
    whole = lax.all_gather(act, "ch", axis=1, tiled=True)
    planes = with_halo(whole.reshape(1, rows_y, rows_z, -1), ((("grp", "sp"), 0),), 1)
    return planes


def conv_layer(act, kernel, rows_y, rows_z):
    planes = spread(act, rows_y, rows_z)
    columns = unfold(planes)
    pre = jnp.dot(columns, kernel.reshape(-1, kernel.shape[-1]), preferred_element_type=jnp.float32)
    out = (act.astype(jnp.float32) + jax.nn.silu(pre)).astype(jnp.bfloat16)
    whole = planes[1].reshape(columns.shape[0], -1)
    return (pre, out, columns, whole)


def silu_slope(value):
    sig = jax.nn.sigmoid(value)
    return sig * (1.0 + value * (1.0 - sig))


def column_grad(columns, error, width):
    grad = lax.dot_general(
        columns, error, (((0,), (0,)), ((), ())), preferred_element_type=jnp.float32
    )
    return grad.reshape(-1, width, error.shape[1])


def adam(weight, moment, second, grad):
    moment_next = beta_one * moment + (1.0 - beta_one) * grad
    second_next = beta_two * second + (1.0 - beta_two) * grad * grad
    weight_next = weight.astype(jnp.float32) - learn_rate * (moment_next / bias_one) / (
        jnp.sqrt(second_next / bias_two) + adam_eps
    )
    return (weight_next.astype(jnp.bfloat16), moment_next, second_next)


def body(flow, embed_w, conv_w, dec_w, conv_m, conv_v, dec_m, dec_v, loss_mask):
    state = with_halo(flow, ((("grp", "sp"), 1), ("ch", 2)), FLOW_STEPS)
    for step in range(FLOW_STEPS):
        state = advance(state)
    rows_y = flow.shape[2] * lax.axis_size("ch") // PATCH
    rows_z = flow.shape[3] // PATCH
    width = conv_w.shape[2]
    inputs = lax.all_gather(to_patches(flow).astype(jnp.bfloat16), "ch", axis=0, tiled=True)
    targets = lax.all_to_all(to_patches(state), "ch", split_axis=1, concat_axis=0, tiled=True)
    embedded = jnp.dot(inputs, embed_w, preferred_element_type=jnp.float32).astype(jnp.bfloat16)
    pre_one, act_one, columns_one, whole_one = conv_layer(embedded, conv_w[0], rows_y, rows_z)
    pre_two, act_two, columns_two, whole_two = conv_layer(act_one, conv_w[1], rows_y, rows_z)
    top = lax.all_gather(act_two, "ch", axis=1, tiled=True)
    block = dec_w.shape[1]
    own_in = lax.dynamic_slice_in_dim(inputs, lax.axis_index("ch") * block, block, 1)
    pred = own_in.astype(jnp.float32) + jnp.dot(top, dec_w, preferred_element_type=jnp.float32)
    weights = loss_mask.reshape(-1).astype(jnp.float32)[:, None]
    resid = pred - targets
    squares, marked = lax.psum(
        (jnp.sum(weights * resid * resid), jnp.sum(weights)), ("grp", "sp", "ch")
    )
    denom = jnp.maximum(marked / lax.axis_size("ch"), 1.0) * OUT
    loss = squares / denom
    d_pred = (2.0 * weights * resid / denom).astype(jnp.bfloat16)
    grad_dec = lax.dot_general(
        top, d_pred, (((0,), (0,)), ((), ())), preferred_element_type=jnp.float32
    )
    back_top = lax.dot_general(
        d_pred, dec_w, (((1,), (1,)), ((), ())), preferred_element_type=jnp.float32
    )
    d_act_two = lax.psum_scatter(back_top, "ch", scatter_dimension=1, tiled=True)
    d_pre_two = (d_act_two * silu_slope(pre_two)).astype(jnp.bfloat16)
    error_planes = with_halo(d_pre_two.reshape(1, rows_y, rows_z, -1), ((("grp", "sp"), 0),), 1)
    turned = jnp.transpose(conv_w[1], (0, 2, 1)).reshape(-1, width)
    back_partial = jnp.dot(unfold_back(error_planes), turned, preferred_element_type=jnp.float32)
    d_act_one = d_act_two + lax.psum_scatter(back_partial, "ch", scatter_dimension=1, tiled=True)
    d_pre_one = (d_act_one * silu_slope(pre_one)).astype(jnp.bfloat16)
    local_conv = jnp.stack(
        [column_grad(columns_one, d_pre_one, width), column_grad(columns_two, d_pre_two, width)]
    )
    grad_conv, grad_lifted = (
        lax.psum_scatter(local_conv, ("grp", "sp"), scatter_dimension=2, tiled=True),
        lax.psum_scatter(grad_dec[None, None], ("grp", "sp"), scatter_dimension=2, tiled=True),
    )
    grad_dec_rows = grad_lifted[0, 0]
    place = lax.axis_index(("grp", "sp"))
    conv_rows = conv_m.shape[2]
    dec_rows = dec_m.shape[0]
    conv_own = lax.dynamic_slice_in_dim(conv_w, place * conv_rows, conv_rows, 2)
    dec_own = lax.dynamic_slice_in_dim(dec_w, place * dec_rows, dec_rows, 0)
    conv_shard, conv_m_next, conv_v_next = adam(conv_own, conv_m, conv_v, grad_conv)
    dec_shard, dec_m_next, dec_v_next = adam(dec_own, dec_m, dec_v, grad_dec_rows)
    conv_next, dec_lifted = (
        lax.all_gather(conv_shard, ("grp", "sp"), axis=2, tiled=True),
        lax.all_gather(dec_shard[None, None], ("grp", "sp"), axis=2, tiled=True),
    )
    return (
        state,
        loss,
        conv_next,
        dec_lifted[0, 0],
        conv_m_next,
        conv_v_next,
        dec_m_next,
        dec_v_next,
    )


def solution(mesh):
    return jax.shard_map(
        body,
        mesh=mesh,
        in_specs=(
            P(None, ("grp", "sp"), "ch", None),
            P(None, "ch"),
            P(None, None, None, "ch"),
            P(None, "ch"),
            P(None, None, ("grp", "sp"), "ch"),
            P(None, None, ("grp", "sp"), "ch"),
            P(("grp", "sp"), "ch"),
            P(("grp", "sp"), "ch"),
            P(("grp", "sp"), None, None),
        ),
        out_specs=(
            P(None, ("grp", "sp"), "ch", None),
            P(),
            P(None, None, None, "ch"),
            P(None, "ch"),
            P(None, None, ("grp", "sp"), "ch"),
            P(None, None, ("grp", "sp"), "ch"),
            P(("grp", "sp"), "ch"),
            P(("grp", "sp"), "ch"),
        ),
        check_vma=False,
    )
```

profile of v0, /device:TPU:0, one launch (start us, length us, event | category | flops | bytes accessed | tf_op | source)
XLA Modules:
  0.0 467.9 jit_solution(15508353446523864724)
XLA Ops:
  7.2 1.0 fusion.90
  8.8 2.9 collective-permute-start.1
  12.5 8.0 %slice_bitcast_fusion.36 = (bf16[27,128,512]{1,2,0:T(8,128)(2,1)}, bf16[1,27,512,128]{3,2,1,0:T(8,128)(2,1)}, bf16[1,27,512,128]{3,2,1,0:T(8,128)(2,1)}) fusion(bf16[2,27,512,128]{3,2,1,0:T(8,128)(2,1)} %param.11), kind=kLoop, calls=%fused_computation.412 | loop fusion | bytes 17694720 | tf_op jit(solution)/shard_map/transpose | solution.py:149
  20.8 4.3 collective-permute-start.3
  25.7 5.9 %convert_element_type.68 = bf16[4,8,2,8,32,8]{5,4,3,2,1,0:T(8,128)(2,1)} reshape(bf16[4,8,16,256]{3,2,1,0:T(8,128)(2,1)S(1)} %get-tuple-element.35) | data formatting | bytes 524288 | tf_op jit(solution)/shard_map/convert_element_type | solution.py:123
  31.6 5.2 %copy.35 = bf16[2,32,4,8,8,8]{1,0,5,4,3,2:T(2,128)(2,1)S(1)} copy(bf16[2,32,4,8,8,8]{5,1,4,0,3,2:T(8,128)(2,1)} %bitcast.230) | data formatting | bytes 524288 | tf_op jit(solution)/shard_map/convert_element_type | solution.py:123
  37.3 0.9 copy.36
  39.0 1.1 multiply_add_fusion.1
  41.1 6.2 %reshape.195 = f32[4,8,2,8,32,8]{5,4,3,2,1,0:T(8,128)} reshape(f32[4,8,16,256]{3,2,1,0:T(8,128)S(1)} %multiply_add_fusion.2) | data formatting | bytes 1048576 | tf_op jit(solution)/shard_map/reshape | solution.py:54
  47.3 6.8 %copy.37 = f32[2,32,4,8,8,8]{1,0,5,4,3,2:T(2,128)S(1)} copy(f32[2,32,4,8,8,8]{5,1,4,0,3,2:T(8,128)} %bitcast.227) | data formatting | bytes 1048576 | tf_op jit(solution)/shard_map/transpose | solution.py:55
  54.1 2.1 all_to_all.14
  56.3 2.3 copy.38
  58.6 5.1 %all-to-all-start = ((f32[64,4,512]{2,0,1:T(8,128)}), f32[64,4,512]{2,0,1:T(8,128)S(1)}, u32[]{:S(2)}, u32[]{:S(2)}) async-start(f32[64,4,512]{2,0,1:T(8,128)} %copy.38), calls=%async_computation | async-start | bytes 1048576 | tf_op jit(solution)/shard_map/all_to_all | solution.py:124
  63.7 4.3 all-gather.4.cloned.1.call-done
  68.0 1.6 convolution_convert_fusion
  69.6 15.1 %all_gather.19 = bf16[256,512]{1,0:T(8,128)(2,1)S(1)} all-gather(bf16[256,128]{1,0:T(8,128)(2,1)S(1)} %convolution_convert_fusion), channel_id=1, replica_groups=mesh['grp'=2,'sp'=4,'ch'=4] {'ch'}, dimensions={1}, use_global_device_ids=true | all-gather | bytes 327680 | tf_op jit(solution)/shard_map/all_gather | solution.py:81
  85.2 2.6 collective-permute-start.5
  88.3 4.4 collective-permute-done.4
  95.2 1.1 copy-done.5
  96.3 2.2 add_convert_fusion.1
  98.5 13.3 %all_gather.20 = bf16[256,512]{1,0:T(8,128)(2,1)S(1)} all-gather(bf16[256,128]{1,0:T(8,128)(2,1)S(1)} %get-tuple-element.183), channel_id=1, replica_groups=mesh['grp'=2,'sp'=4,'ch'=4] {'ch'}, dimensions={1}, use_global_device_ids=true | all-gather | bytes 327680 | tf_op jit(solution)/shard_map/all_gather | solution.py:81
  112.3 2.6 collective-permute-start.7
  115.4 5.1 %collective-permute-done.6 = bf16[1,8,32,512]{3,2,1,0:T(8,128)(2,1)S(1)} collective-permute-done((bf16[1,8,32,512]{3,2,1,0:T(8,128)(2,1)S(1)}, bf16[1,8,32,512]{3,2,1,0:T(8,128)(2,1)S(1)}, u32[]{:S(2)}, u32[]{:S(2)}) %collective-permute-start.6) | collective-permute-done | bytes 262176 | tf_op jit(solution)/shard_map/ppermute | solution.py:27
  123.1 3.0 copy-done.3
  126.1 2.2 add_convert_fusion
  128.2 13.5 %all_gather.21 = bf16[256,512]{1,0:T(8,128)(2,1)S(1)} all-gather(bf16[256,128]{1,0:T(8,128)(2,1)S(1)} %get-tuple-element.185), channel_id=1, replica_groups=mesh['grp'=2,'sp'=4,'ch'=4] {'ch'}, dimensions={1}, use_global_device_ids=true | all-gather | bytes 327680 | tf_op jit(solution)/shard_map/all_gather | solution.py:128
  141.8 1.9 fusion.2
  143.7 38.9 %all-reduce = (f32[]{:T(128)}, f32[]{:T(128)}) all-reduce(f32[]{:T(128)} %get-tuple-element.187, f32[]{:T(128)} %convert_reduce_fusion), channel_id=1, replica_groups=mesh['grp'=2,'sp'=4,'ch'=4] {'grp','sp','ch'}, use_global_device_ids=true, to_apply=%region_1.2 | all-reduce | flops 2 | bytes 16 | tf_op jit(solution)/shard_map/psum | solution.py:134
  183.2 1.1 fusion.80
  184.7 5.7 %copy.40 = bf16[27,128,512]{2,1,0:T(8,128)(2,1)} copy(bf16[27,128,512]{1,2,0:T(8,128)(2,1)} %get-tuple-element.16) | data formatting | bytes 7077888 | tf_op jit(solution)/shard_map/transpose | solution.py:149
  190.4 17.3 %reduce-scatter.5.cloned.1.call-done = f32[256,128]{1,0:T(8,128)} async-done(((f32[256,512]{1,0:T(8,128)}), f32[256,128]{1,0:T(8,128)}) %reduce-scatter.5.cloned.1.call-update) | async-done | bytes 131088 | tf_op jit(solution)/shard_map/reduce_scatter | solution.py:146
  207.7 1.1 multiply_convert_fusion.1
  209.8 1.4 collective-permute-done.8
  211.4 2.9 collective-permute-done.9
  215.7 1.9 fusion.112
  217.7 9.8 %copy.39 = bf16[13824,256]{1,0:T(8,128)(2,1)} copy(bf16[13824,256]{0,1:T(8,128)(2,1)} %bitcast.228) | data formatting | bytes 14155776 | tf_op jit(solution)/shard_map/dot_general | solution.py:101
  227.4 10.3 %copy.41 = bf16[13824,256]{1,0:T(8,128)(2,1)} copy(bf16[13824,256]{0,1:T(8,128)(2,1)} %bitcast.229) | data formatting | bytes 14155776 | tf_op jit(solution)/shard_map/dot_general | solution.py:101
  237.8 8.0 %convolution_bitcast_fusion = f32[1,27,512,128]{3,2,1,0:T(8,128)} fusion(bf16[27,512,256]{2,1,0:T(8,128)(2,1)} %bitcast.225, bf16[256,128]{1,0:T(8,128)(2,1)S(1)} %multiply_convert_fusion.1), kind=kOutput, calls=%fused_computation.1 | convolution fusion | flops 905969664 | bytes 14221312 | tf_op jit(solution)/shard_map/dot_general | solution.py:101
  245.8 7.9 %convolution_bitcast_fusion.1 = f32[1,27,512,128]{3,2,1,0:T(8,128)} fusion(bf16[27,512,256]{2,1,0:T(8,128)(2,1)} %bitcast.226, f32[256,128]{1,0:T(8,128)S(1)} %get-tuple-element.184, f32[256,128]{1,0:T(8,128)S(1)} %copy-done.11, f32[256,128]{1,0:T(8,128)} %reduce-scatter.7.cloned.1.call-done), kind=kOutput, calls=%fused_computation.2 | convolution fusion | flops 906297344 | bytes 14548992 | tf_op jit(solution)/shard_map/dot_general | solution.py:101
  253.7 11.7 %pad_maximum_fusion = f32[2,27,512,128]{3,2,1,0:T(8,128)} fusion(f32[1,27,512,128]{3,2,1,0:T(8,128)} %convolution_bitcast_fusion, f32[1,27,512,128]{3,2,1,0:T(8,128)} %convolution_bitcast_fusion.1), kind=kLoop, calls=%fused_computation | loop fusion | flops 3538944 | bytes 28311552 | tf_op jit(solution)/shard_map/stack | solution.py:153
  265.5 1.4 convolution_bitcast_fusion.2
  266.9 95.3 %reduce-scatter.9.cloned.1.call-done = f32[2,27,64,128]{3,2,1,0:T(8,128)} async-done(((f32[2,27,512,128]{3,2,1,0:T(8,128)}), f32[2,27,64,128]{3,2,1,0:T(8,128)}) %reduce-scatter.9.cloned.1.call-update) | async-done | bytes 1769488 | tf_op jit(solution)/shard_map/reduce_scatter | solution.py:157
  362.2 5.5 %subtract_convert_fusion = (bf16[2,27,64,128]{3,2,1,0:T(8,128)(2,1)}, f32[2,27,64,128]{3,2,1,0:T(8,128)}, f32[2,27,64,128]{3,2,1,0:T(8,128)}) fusion(bf16[2,27,512,128]{3,2,1,0:T(8,128)(2,1)} %param.11, s32[]{:T(128)S(6)} %select_n.8, f32[2,27,64,128]{3,2,1,0:T(8,128)} %reduce-scatter.9.cloned.1.call-done, f32[2,27,64,128]{3,2,1,0:T(8,128)S(1)} %copy-done.8, ...), kind=kLoop, calls=%fused_computation.5 | loop fusion | flops 6193152 | bytes 10616836 | tf_op jit(solution)/shard_map/convert_element_type | solution.py:113
  368.4 33.4 %reduce-scatter.11.cloned.1.call-done = f32[1,1,64,512]{3,2,1,0:T(8,128)} async-done(((f32[1,1,512,512]{3,2,1,0:T(8,128)}), f32[1,1,64,512]{3,2,1,0:T(8,128)}) %reduce-scatter.11.cloned.1.call-update) | async-done | bytes 131088 | tf_op jit(solution)/shard_map/reduce_scatter | solution.py:158
  401.8 1.7 subtract_convert_fusion.1
  403.5 9.8 %all-gather = bf16[512,512]{1,0:T(8,128)(2,1)S(1)} all-gather(bf16[64,512]{1,0:T(8,128)(2,1)S(1)} %get-tuple-element.10), channel_id=2, replica_groups=mesh['grp'=2,'sp'=4,'ch'=4] {'grp','sp'}, dimensions={0}, use_global_device_ids=true | all-gather | bytes 589824 | tf_op jit(solution)/shard_map/all_gather | solution.py:170
  413.3 39.0 %all-gather.6.cloned.1.call-done = bf16[2,27,512,128]{3,2,1,0:T(8,128)(2,1)} async-done(((bf16[2,27,64,128]{3,2,1,0:T(8,128)(2,1)}), bf16[2,27,512,128]{3,2,1,0:T(8,128)(2,1)}) %all-gather.6.cloned.1.call-update) | async-done | bytes 7077904 | tf_op jit(solution)/shard_map/all_gather | solution.py:169
  452.3 6.8 %copy.124 = bf16[2,27,512,128]{3,2,1,0:T(8,128)(2,1)} copy(bf16[2,27,512,128]{3,2,1,0:T(8,128)(2,1)} %all-gather.6.cloned.1.call-done) | data formatting | bytes 14155776
  (285 shorter events, 13.6 us)
Async XLA Ops:
  7.2 60.8 %copy-start = (bf16[2048,128]{1,0:T(8,128)(2,1)S(1)}, bf16[2048,128]{1,0:T(8,128)(2,1)}, u32[]{:S(2)}) copy-start(bf16[2048,128]{1,0:T(8,128)(2,1)} %param.10) | copy-start | bytes 1572868
  7.2 60.8 %all-gather.4.cloned.1.call-start = ((), (), s32[]{:S(2)}) async-start(), calls=%async_computation.5 | async-start | bytes 1310720 | tf_op jit(solution)/shard_map/all_gather | solution.py:123
  8.3 12.3 %collective-permute-start = (f32[4,2,16,256]{3,2,1,0:T(8,128)S(1)}, f32[4,2,16,256]{3,2,1,0:T(8,128)S(1)}, u32[]{:S(2)}, u32[]{:S(2)}) collective-permute-start(f32[4,2,16,256]{3,2,1,0:T(8,128)S(1)} %get-tuple-element.38), channel_id=1, source_target_pairs={{0,4},{4,8},{8,12},{12,16},{16,20},{20,24},{24,28},{28,0},{1,5},{5... | collective-permute-start | bytes 393224 | tf_op jit(solution)/shard_map/ppermute | solution.py:27
  8.8 11.8 %collective-permute-start.1 = (f32[4,2,16,256]{3,2,1,0:T(8,128)S(1)}, f32[4,2,16,256]{3,2,1,0:T(8,128)S(1)}, u32[]{:S(2)}, u32[]{:S(2)}) collective-permute-start(f32[4,2,16,256]{3,2,1,0:T(8,128)S(1)} %get-tuple-element.37), channel_id=1, source_target_pairs={{4,0},{8,4},{12,8},{16,12},{20,16},{24,20},{28,24},{0,28},{5,1},{9... | collective-permute-start | bytes 393224 | tf_op jit(solution)/shard_map/ppermute | solution.py:30
  12.5 8.0 %copy-start.9 = (f32[4,8,16,256]{3,2,1,0:T(8,128)S(1)}, f32[4,8,16,256]{3,2,1,0:T(8,128)}, u32[]{:S(2)}) copy-start(f32[4,8,16,256]{3,2,1,0:T(8,128)} %param.9) | copy-start | bytes 1572868
  12.5 12.6 %copy-start.14 = (s32[1,8,32]{2,1,0:T(8,128)S(1)}, s32[1,8,32]{2,1,0:T(8,128)}, u32[]{:S(2)}) copy-start(s32[1,8,32]{2,1,0:T(8,128)} %param.17) | copy-start | bytes 3076
  20.8 17.4 %collective-permute-start.3 = (f32[4,12,2,256]{3,2,1,0:T(2,128)S(1)}, f32[4,12,2,256]{3,2,1,0:T(2,128)S(1)}, u32[]{:S(2)}, u32[]{:S(2)}) collective-permute-start(f32[4,12,2,256]{3,2,1,0:T(2,128)S(1)} %get-tuple-element.34), channel_id=1, source_target_pairs={{1,0},{2,1},{3,2},{0,3},{5,4},{6,5},{7,6},{4,7},{9,8},{10,9},{11,1... | collective-permute-start | bytes 294920 | tf_op jit(solution)/shard_map/ppermute | solution.py:30
  25.1 13.1 %collective-permute-start.2 = (f32[4,12,2,256]{3,2,1,0:T(2,128)S(1)}, f32[4,12,2,256]{3,2,1,0:T(2,128)S(1)}, u32[]{:S(2)}, u32[]{:S(2)}) collective-permute-start(f32[4,12,2,256]{3,2,1,0:T(2,128)S(1)} %get-tuple-element.33), channel_id=1, source_target_pairs={{0,1},{1,2},{2,3},{3,0},{4,5},{5,6},{6,7},{7,4},{8,9},{9,10},{10,1... | collective-permute-start | bytes 294920 | tf_op jit(solution)/shard_map/ppermute | solution.py:27
  41.1 13.0 %copy-start.7 = (f32[4,8,16,256]{3,2,1,0:T(8,128)}, f32[4,8,16,256]{3,2,1,0:T(8,128)S(1)}, u32[]{:S(2)}) copy-start(f32[4,8,16,256]{3,2,1,0:T(8,128)S(1)} %multiply_add_fusion.2) | copy-start | bytes 1572868
  58.6 83.1 %all-to-all-start = ((f32[64,4,512]{2,0,1:T(8,128)}), f32[64,4,512]{2,0,1:T(8,128)S(1)}, u32[]{:S(2)}, u32[]{:S(2)}) async-start(f32[64,4,512]{2,0,1:T(8,128)} %copy.38), calls=%async_computation | async-start | bytes 1048576 | tf_op jit(solution)/shard_map/all_to_all | solution.py:124
  63.7 144.0 %reduce-scatter.5.cloned.1.call-start = ((), (), s32[]{:S(2)}) async-start(), calls=%async_computation.6 | async-start | bytes 655360 | tf_op jit(solution)/shard_map/reduce_scatter | solution.py:146
  85.1 7.6 %collective-permute-start.4 = (bf16[1,8,32,512]{3,2,1,0:T(8,128)(2,1)S(1)}, bf16[1,8,32,512]{3,2,1,0:T(8,128)(2,1)S(1)}, u32[]{:S(2)}, u32[]{:S(2)}) collective-permute-start(bf16[1,8,32,512]{3,2,1,0:T(8,128)(2,1)S(1)} %bitcast.239), channel_id=1, source_target_pairs={{0,4},{4,8},{8,12},{12,16},{16,20},{20,24},{24,28},{28,0},{1,5},{5... | collective-permute-start | bytes 786440 | tf_op jit(solution)/shard_map/ppermute | solution.py:27
  85.2 8.0 %collective-permute-start.5 = (bf16[1,8,32,512]{3,2,1,0:T(8,128)(2,1)S(1)}, bf16[1,8,32,512]{3,2,1,0:T(8,128)(2,1)S(1)}, u32[]{:S(2)}, u32[]{:S(2)}) collective-permute-start(bf16[1,8,32,512]{3,2,1,0:T(8,128)(2,1)S(1)} %bitcast.240), channel_id=1, source_target_pairs={{4,0},{8,4},{12,8},{16,12},{20,16},{24,20},{28,24},{0,28},{5,1},{9... | collective-permute-start | bytes 786440 | tf_op jit(solution)/shard_map/ppermute | solution.py:30
  94.2 2.1 copy-start.5
  95.2 16.9 %copy-start.2 = (bf16[256,13824]{1,0:T(8,128)(2,1)}, bf16[256,13824]{1,0:T(8,128)(2,1)S(1)}, u32[]{:S(2)}) copy-start(bf16[256,13824]{1,0:T(8,128)(2,1)S(1)} %constant_dynamic-update-slice_fusion.3) | copy-start | bytes 21233668
  112.3 8.2 %collective-permute-start.6 = (bf16[1,8,32,512]{3,2,1,0:T(8,128)(2,1)S(1)}, bf16[1,8,32,512]{3,2,1,0:T(8,128)(2,1)S(1)}, u32[]{:S(2)}, u32[]{:S(2)}) collective-permute-start(bf16[1,8,32,512]{3,2,1,0:T(8,128)(2,1)S(1)} %bitcast.235), channel_id=1, source_target_pairs={{0,4},{4,8},{8,12},{12,16},{16,20},{20,24},{24,28},{28,0},{1,5},{5... | collective-permute-start | bytes 786440 | tf_op jit(solution)/shard_map/ppermute | solution.py:27
  112.3 8.6 %collective-permute-start.7 = (bf16[1,8,32,512]{3,2,1,0:T(8,128)(2,1)S(1)}, bf16[1,8,32,512]{3,2,1,0:T(8,128)(2,1)S(1)}, u32[]{:S(2)}, u32[]{:S(2)}) collective-permute-start(bf16[1,8,32,512]{3,2,1,0:T(8,128)(2,1)S(1)} %bitcast.236), channel_id=1, source_target_pairs={{4,0},{8,4},{12,8},{16,12},{20,16},{24,20},{28,24},{0,28},{5,1},{9... | collective-permute-start | bytes 786440 | tf_op jit(solution)/shard_map/ppermute | solution.py:30
  122.1 4.0 copy-start.4
  122.8 18.9 %copy-start.10 = (bf16[512,512]{1,0:T(8,128)(2,1)S(1)}, bf16[512,512]{1,0:T(8,128)(2,1)}, u32[]{:S(2)}) copy-start(bf16[512,512]{1,0:T(8,128)(2,1)} %param.12) | copy-start | bytes 1572868
  123.1 3.0 copy-start.3
  184.4 61.4 %reduce-scatter.7.cloned.1.call-start = ((), (), s32[]{:S(2)}) async-start(), calls=%async_computation.7 | async-start | bytes 655360 | tf_op jit(solution)/shard_map/reduce_scatter | solution.py:151
  207.7 8.0 %copy-start.6 = (bf16[27,128,512]{2,1,0:T(8,128)(2,1)S(1)}, bf16[27,128,512]{2,1,0:T(8,128)(2,1)}, u32[]{:S(2)}) copy-start(bf16[27,128,512]{2,1,0:T(8,128)(2,1)} %copy.40) | copy-start | bytes 10616836
  209.0 2.2 collective-permute-start.8
  209.3 5.1 %collective-permute-start.9 = (bf16[1,8,32,128]{3,2,1,0:T(8,128)(2,1)S(1)}, bf16[1,8,32,128]{3,2,1,0:T(8,128)(2,1)S(1)}, u32[]{:S(2)}, u32[]{:S(2)}) collective-permute-start(bf16[1,8,32,128]{3,2,1,0:T(8,128)(2,1)S(1)} %bitcast.269), channel_id=1, source_target_pairs={{0,4},{4,8},{8,12},{12,16},{16,20},{20,24},{24,28},{28,0},{1,5},{5... | collective-permute-start | bytes 196616 | tf_op jit(solution)/shard_map/ppermute | solution.py:27
  217.6 144.6 %reduce-scatter.9.cloned.1.call-start = ((), (), s32[]{:S(2)}) async-start(), calls=%async_computation.8 | async-start | bytes 15925248 | tf_op jit(solution)/shard_map/reduce_scatter | solution.py:157
  237.8 8.0 %copy-start.11 = (f32[256,128]{1,0:T(8,128)S(1)}, f32[256,128]{1,0:T(8,128)}, u32[]{:S(2)}) copy-start(f32[256,128]{1,0:T(8,128)} %reduce-scatter.5.cloned.1.call-done) | copy-start | bytes 393220
  265.4 96.8 %copy-start.8 = (f32[2,27,64,128]{3,2,1,0:T(8,128)S(1)}, f32[2,27,64,128]{3,2,1,0:T(8,128)}, u32[]{:S(2)}) copy-start(f32[2,27,64,128]{3,2,1,0:T(8,128)} %param.13) | copy-start | bytes 5308420
  265.4 136.4 %copy-start.12 = (f32[64,512]{1,0:T(8,128)S(1)}, f32[64,512]{1,0:T(8,128)}, u32[]{:S(2)}) copy-start(f32[64,512]{1,0:T(8,128)} %param.15) | copy-start | bytes 393220
  265.4 136.4 %copy-start.13 = (f32[64,512]{1,0:T(8,128)S(1)}, f32[64,512]{1,0:T(8,128)}, u32[]{:S(2)}) copy-start(f32[64,512]{1,0:T(8,128)} %param.16) | copy-start | bytes 393220
  265.4 136.3 %reduce-scatter.11.cloned.1.call-start = ((), (), s32[]{:S(2)}) async-start(), calls=%async_computation.10 | async-start | bytes 1179648 | tf_op jit(solution)/shard_map/reduce_scatter | solution.py:158
  266.8 185.4 %all-gather.6.cloned.1.call-start = ((), (), s32[]{:S(2)}) async-start(), calls=%async_computation.9 | async-start | bytes 7962624 | tf_op jit(solution)/shard_map/all_gather | solution.py:169
  452.3 7.6 %copy-start.1 = (bf16[2048,128]{1,0:T(8,128)(2,1)S(1)}, bf16[2048,128]{1,0:T(8,128)(2,1)}, u32[]{:S(2)}) copy-start(bf16[2048,128]{1,0:T(8,128)(2,1)} %param.10) | copy-start | bytes 1572868
Sparse Core Ops, SparseCore 0:
  38.3 29.6 all-gather.3
  184.5 23.1 reduce-scatter.4
  217.7 18.5 reduce-scatter.6
  265.5 96.6 reduce-scatter.8
  365.8 35.9 reduce-scatter.10
  403.5 48.7 all-gather.5
where the time goes:
time: 469 us; the launch traced here: 468 us
  waiting for transfers between devices  203 us (43%)
  blocking collectives  90.6 us (19%)
  local copies, waits for them, and re-layouts  80.3 us (17%)
  matrix products  28.2 us (6%)
  other arithmetic  27.9 us (6%)
  starting transfers between devices  19.3 us (4%)
  between operations  18.4 us (4%)
    reduce_scatter x1, waiting for transfers between devices, body(): lax.psum_scatter(local_conv, ('grp', 'sp'), scatter_dimension=2, tiled=True)  95.3 us
    all_gather x1, waiting for transfers between devices, body(): lax.all_gather(conv_shard, ('grp', 'sp'), axis=2, tiled=True)  39 us
    psum x1, blocking collectives, body(): lax.psum((jnp.sum(weights * resid * resid), jnp.sum(weights)), ('grp', 's...  38.9 us
    reduce_scatter x1, waiting for transfers between devices, body(): lax.psum_scatter(grad_dec[None, None], ('grp', 'sp'), scatter_dimension=2...  33.4 us
    all_gather x2, blocking collectives, spread(): whole = lax.all_gather(act, 'ch', axis=1, tiled=True)  28.4 us
    dot_general x2, local copies, waits for them, and re-layouts, column_grad(): lax.dot_general(columns, error, (((0,), (0,)), ((), ())), preferred_eleme...  20.1 us
    reduce_scatter x1, waiting for transfers between devices, body(): lax.psum_scatter(back_top, 'ch', scatter_dimension=1, tiled=True)  17.3 us
    dot_general x2, matrix products, column_grad(): lax.dot_general(columns, error, (((0,), (0,)), ((), ())), preferred_eleme...  15.9 us
  transfers between devices with their start and end apart: 17, of which 9 were waited for; matrix products, arithmetic and copies ran while one was open for 20% of the time, Pallas kernels for 0%

commit v1 on v0

v1 whole, which is shorter than its diff:
```python
import jax
import jax.numpy as jnp
from jax import lax
from jax.experimental import pallas as pl
from jax.experimental.pallas import tpu as pltpu
from jax.sharding import PartitionSpec as P

PATCH = 8
FLOW_STEPS = 2
OUT = 2048
SPLIT = ("grp", "sp")


time_step = 0.1
viscosity = 0.2
beta_one = 0.9
beta_two = 0.95
learn_rate = 0.001
adam_eps = 1e-08
bias_one = 0.9999734386011124
bias_two = 0.994079470779666


def shift(block, axis, by):
    count = lax.axis_size(axis)
    return lax.ppermute(block, axis, [(i, (i + by) % count) for i in range(count)])


def with_halo(block, sides, width):
    for axis, dim in sides:
        low = shift(
            lax.slice_in_dim(block, block.shape[dim] - width, None, axis=dim), axis, 1
        )
        high = shift(lax.slice_in_dim(block, 0, width, axis=dim), axis, -1)
        block = jnp.concatenate([low, block, high], axis=dim)
    return block


def advance(padded):
    center = padded[:, 1:-1, 1:-1]
    east = padded[:, 2:, 1:-1]
    west = padded[:, :-2, 1:-1]
    north = padded[:, 1:-1, 2:]
    south = padded[:, 1:-1, :-2]
    upper = jnp.roll(center, -1, 3)
    lower = jnp.roll(center, 1, 3)
    laplace = east + west + north + south + upper + lower - 6.0 * center
    carried = (
        center[0:1] * (east - west) * 0.5
        + center[1:2] * (north - south) * 0.5
        + center[2:3] * (upper - lower) * 0.5
    )
    return center + time_step * (viscosity * laplace - carried)


def rotations(block, axis):
    return [block] + [shift(block, axis, by) for by in range(1, lax.axis_size(axis))]


def scattered(pieces_of, axis):
    count, own = lax.axis_size(axis), lax.axis_index(axis)
    parts = [pieces_of(own)]
    for by in range(1, count):
        parts.append(shift(pieces_of((own + by) % count), axis, by))
    return parts


BIG = pltpu.CompilerParams(vmem_limit_bytes=48 * 1024 * 1024)
FLOAT = jnp.float32
HALF = jnp.bfloat16


def like(shape, dtype):
    return jax.ShapeDtypeStruct(shape, dtype)


def whole_spec(shape):
    return pl.BlockSpec(shape, lambda *_: (0,) * len(shape))


def turn(block, by, groups):
    rows = block.shape[0] // groups
    cube = block.astype(FLOAT).reshape(groups, rows, block.shape[1])
    return pltpu.roll(cube, by % rows, 1).reshape(block.shape)


def to_patches(field):
    fields, depth, span, length = field.shape
    high, long = span // PATCH, length // PATCH
    flat = PATCH * PATCH
    cells = flat * PATCH

    def kernel(field_ref, out_ref):
        row = lax.broadcasted_iota(jnp.int32, (length, length), 0)
        col = lax.broadcasted_iota(jnp.int32, (length, length), 1)
        pick = (col == (row % long) * PATCH + row // long).astype(HALF)
        row = lax.broadcasted_iota(jnp.int32, (flat, cells), 0)
        col = lax.broadcasted_iota(jnp.int32, (flat, cells), 1)
        inside, deep = row == col // PATCH, col % PATCH
        grids = []
        for part in range(high):
            for index in range(fields):
                brick = field_ref[index, :, part * PATCH : (part + 1) * PATCH, :]
                brick = brick.reshape(flat, length).astype(HALF)
                grids.append(
                    lax.dot_general(
                        pick, brick, (((1,), (1,)), ((), ())), preferred_element_type=FLOAT
                    ).astype(HALF)
                )
        total = jnp.zeros((high * fields * long, cells), FLOAT)
        for step in range(PATCH):
            rows = jnp.concatenate(
                [grid[step * long : (step + 1) * long] for grid in grids], axis=0
            )
            place = (inside & (deep == step)).astype(HALF)
            total = total + jnp.dot(rows, place, preferred_element_type=FLOAT)
        for part in range(high):
            for index in range(fields):
                at = (part * fields + index) * long
                out_ref[
                    part * long : (part + 1) * long, index * cells : (index + 1) * cells
                ] = total[at : at + long].astype(HALF)

    return pl.pallas_call(
        kernel, out_shape=like((high * long, fields * cells), HALF), compiler_params=BIG
    )(field)


def axis_word(axis):
    return lax.axis_index(axis).astype(jnp.int32).reshape(1)


def embed(parts, weight):
    count, rows, cols = len(parts), parts[0].shape[0], weight.shape[1]

    def kernel(own_ref, *refs):
        weight_ref, out_ref = refs[count], refs[count + 1]
        for by in range(count):
            source = lax.rem(own_ref[0] - by + count, count)
            out_ref[pl.ds(pl.multiple_of(source * rows, rows), rows), :] = jnp.dot(
                refs[by][...], weight_ref[...], preferred_element_type=FLOAT
            ).astype(HALF)

    return pl.pallas_call(
        kernel,
        out_shape=like((count * rows, cols), HALF),
        in_specs=[pl.BlockSpec(memory_space=pltpu.SMEM)]
        + [pl.BlockSpec(memory_space=pltpu.VMEM)] * (count + 1),
        compiler_params=BIG,
    )(axis_word("ch"), *parts, weight)


def conv_layer(act, kernels, layer, rows_y, rows_z):
    near = jnp.stack(rotations(act, "ch"))
    below = shift(near, SPLIT, 1)
    above = shift(near, SPLIT, -1)
    count, rows, cols = near.shape
    width = count * cols

    def kernel(own_ref, below_ref, near_ref, above_ref, act_ref, taps_ref, pre_ref, out_ref, planes, total):
        step = pl.program_id(0)

        @pl.when(step == 0)
        def _():
            for plane, source in enumerate((below_ref, near_ref, above_ref)):
                for by in range(count):
                    place = lax.rem(own_ref[0] - by + count, count)
                    at = pl.ds(pl.multiple_of(place * cols, cols), cols)
                    planes[plane, rows_z : rows_z + rows, at] = source[by]
                    planes[plane, :rows_z, at] = source[by, rows - rows_z :]
                    planes[plane, rows_z + rows :, at] = source[by, :rows_z]
            total[...] = jnp.zeros_like(total)

        first = pl.multiple_of(lax.rem(step, 3) * rows_z, rows_z)
        left = planes[step // 3, pl.ds(first, rows), :]
        right = jnp.concatenate([taps_ref[0, index] for index in range(3)], axis=1)
        total[...] += jnp.dot(left, right, preferred_element_type=FLOAT)

        @pl.when(step == 8)
        def _():
            pre = (
                turn(total[:, :cols], 1, rows_y)
                + total[:, cols : 2 * cols]
                + turn(total[:, 2 * cols :], -1, rows_y)
            )
            pre_ref[...] = pre
            out_ref[...] = (act_ref[...].astype(FLOAT) + pre / (1.0 + jnp.exp(-pre))).astype(HALF)

    pre, out = pl.pallas_call(
        kernel,
        grid=(9,),
        out_shape=(like((rows, cols), FLOAT), like((rows, cols), HALF)),
        in_specs=[pl.BlockSpec(memory_space=pltpu.SMEM)]
        + [whole_spec(near.shape)] * 3
        + [
            whole_spec(act.shape),
            pl.BlockSpec((1, 3, width, cols), lambda step: (layer, step, 0, 0)),
        ],
        out_specs=(whole_spec((rows, cols)), whole_spec((rows, cols))),
        scratch_shapes=[
            pltpu.VMEM((3, rows + 2 * rows_z, width), HALF),
            pltpu.VMEM((rows, 3 * cols), FLOAT),
        ],
        compiler_params=BIG,
    )(axis_word("ch"), below, near, above, act, kernels)
    return (pre, out, near)


def give(own_ref, total, cols, count, first_ref, piece_refs):
    for by in range(count):
        place = lax.rem(own_ref[0] + by, count)
        part = total[:, pl.ds(pl.multiple_of(place * cols, cols), cols)]
        if by == 0:
            first_ref[...] = part
        else:
            piece_refs[by - 1][...] = part.astype(HALF)


def conv_back(errors, kernels, layer, rows_y, rows_z, count):
    planes, rows, cols = errors.shape
    width = count * cols

    def kernel(own_ref, *refs):
        error_refs, taps_ref, first_ref = refs[:3], refs[3], refs[4]
        piece_refs, sides, total = refs[5 : 4 + count], refs[4 + count], refs[5 + count]
        step = pl.program_id(0)

        @pl.when(step == 0)
        def _():
            for plane in range(3):
                source = error_refs[plane][0]
                wide = jnp.concatenate(
                    [
                        turn(source, -1, rows_y).astype(HALF),
                        source,
                        turn(source, 1, rows_y).astype(HALF),
                    ],
                    axis=1,
                )
                sides[plane, rows_z : rows_z + rows] = wide
                sides[plane, :rows_z] = wide[rows - rows_z :]
                sides[plane, rows_z + rows :] = wide[:rows_z]
            total[...] = jnp.zeros_like(total)

        first = pl.multiple_of((2 - lax.rem(step, 3)) * rows_z, rows_z)
        left = sides[step // 3, pl.ds(first, rows), :]
        right = jnp.concatenate([taps_ref[0, index] for index in range(3)], axis=1)
        total[...] += lax.dot_general(
            left, right, (((1,), (1,)), ((), ())), preferred_element_type=FLOAT
        )

        @pl.when(step == 8)
        def _():
            give(own_ref, total, cols, count, first_ref, piece_refs)

    def plane_spec(offset):
        return pl.BlockSpec(
            (1, rows, cols), lambda step, word: (lax.rem(word[1] + offset + planes, planes), 0, 0)
        )

    word = jnp.concatenate([axis_word("ch"), axis_word(SPLIT)])
    return pl.pallas_call(
        kernel,
        grid_spec=pltpu.PrefetchScalarGridSpec(
            num_scalar_prefetch=1,
            grid=(9,),
            in_specs=[
                plane_spec(1),
                plane_spec(0),
                plane_spec(-1),
                pl.BlockSpec((1, 3, width, cols), lambda step, word: (layer, step, 0, 0)),
            ],
            out_specs=[whole_spec((rows, cols))] * count,
            scratch_shapes=[
                pltpu.VMEM((3, rows + 2 * rows_z, 3 * cols), HALF),
                pltpu.VMEM((rows, width), FLOAT),
            ],
        ),
        out_shape=[like((rows, cols), FLOAT)] + [like((rows, cols), HALF)] * (count - 1),
        compiler_params=BIG,
    )(word, errors, errors, errors, kernels)


def predict(parts, changes, weight, mask, channels):
    count = len(parts)
    rows, cols = parts[0].shape
    short, block = changes[0].shape
    width = count * cols

    def kernel(own_ref, *refs):
        part_refs, change_refs = refs[:count], refs[count : 2 * count]
        weight_ref, mask_ref = refs[2 * count], refs[2 * count + 1]
        outs = refs[2 * count + 2 :]
        top_ref, error_ref, sums_ref, first_ref = outs[:4]
        piece_refs, held = outs[4 : 3 + count], outs[3 + count]
        for by in range(count):
            place = lax.rem(own_ref[0] - by + count, count)
            top_ref[:, pl.ds(pl.multiple_of(place * cols, cols), cols)] = part_refs[by][...]
            held[pl.ds(pl.multiple_of(place * short, short), short), :] = change_refs[by][...]
        pred = jnp.dot(top_ref[...], weight_ref[...], preferred_element_type=FLOAT)
        resid = held[...].astype(FLOAT) + pred
        mask = mask_ref[...]
        marked = mask * resid
        error = marked.astype(HALF)
        error_ref[...] = error
        sums_ref[0] = jnp.full((8, 128), jnp.sum(marked * resid), FLOAT)
        sums_ref[1] = jnp.full((8, 128), jnp.sum(mask), FLOAT)
        total = refs[-1]
        total[...] = lax.dot_general(
            error, weight_ref[...], (((1,), (1,)), ((), ())), preferred_element_type=FLOAT
        )
        give(own_ref, total, cols, count, first_ref, piece_refs)

    return pl.pallas_call(
        kernel,
        in_specs=[pl.BlockSpec(memory_space=pltpu.SMEM)]
        + [pl.BlockSpec(memory_space=pltpu.VMEM)] * (2 * count + 2),
        out_shape=[
            like((rows, width), HALF),
            like((rows, block), HALF),
            like((2, 8, 128), FLOAT),
            like((rows, cols), FLOAT),
        ]
        + [like((rows, cols), HALF)] * (count - 1),
        scratch_shapes=[pltpu.VMEM((rows, block), HALF), pltpu.VMEM((rows, width), FLOAT)],
        compiler_params=BIG,
    )(axis_word("ch"), *parts, *changes, weight, mask)


def kernel_step(every, errors, scale, kernels, moments, seconds, layer, kept, rows_y, rows_z):
    planes, count, points, lane = every.shape
    cols = errors.shape[2]
    rows = moments.shape[2]
    each = lane // rows
    blocks = -(-9 // each)

    def kernel(word_ref, scale_ref, every_ref, errors_ref, w_ref, m_ref, v_ref, *refs):
        new_w, new_m, new_v, slots, total = refs[-5:]
        offset = lax.rem(word_ref[0] * rows, lane)
        lanes = lax.broadcasted_iota(jnp.int32, (points, lane), 1)

        def prepare(plane, carry):
            own = every_ref[plane, 0].astype(FLOAT)
            for slot in range(each):
                moved = pltpu.roll(own, lax.rem(slot * rows - offset + lane, lane), 1)
                inside = (lanes >= slot * rows) & (lanes < (slot + 1) * rows)
                moved = jnp.where(inside, moved, 0.0).astype(HALF)
                slots[slot, plane, rows_z : rows_z + points] = moved
                slots[slot, plane, :rows_z] = moved[points - rows_z :]
                slots[slot, plane, rows_z + points :] = moved[:rows_z]
            return carry

        lax.fori_loop(0, planes, prepare, 0)
        total[...] = jnp.zeros_like(total)

        def gather(plane, carry):
            left = []
            for block in range(blocks):
                value = None
                for slot in range(each):
                    pair = block * each + slot
                    if pair < 9:
                        source = lax.rem(plane + pair // 3 - 1 + planes, planes)
                        part = slots[slot, source, pl.ds((pair % 3) * rows_z, points), :]
                        value = part if value is None else value + part
                left.append(value)
            left = jnp.concatenate(left, axis=1)
            error = errors_ref[plane]
            right = jnp.concatenate(
                [
                    turn(error, -1, rows_y).astype(HALF),
                    error,
                    turn(error, 1, rows_y).astype(HALF),
                ],
                axis=1,
            )
            total[...] += lax.dot_general(
                left, right, (((0,), (0,)), ((), ())), preferred_element_type=FLOAT
            )
            return carry

        lax.fori_loop(0, planes, gather, 0)
        for tap in range(27):
            at = (tap // 3) * rows
            grad = total[at : at + rows, (tap % 3) * cols : (tap % 3 + 1) * cols] * scale_ref[0]
            weight_next, moment_next, second_next = adam(
                w_ref[0, tap], m_ref[0, tap], v_ref[0, tap], grad
            )
            new_w[tap] = weight_next
            new_m[0, tap] = moment_next
            new_v[0, tap] = second_next

    state_spec = pl.BlockSpec((1, 27, rows, cols), lambda step, word: (layer, 0, 0, 0))
    extra = list(kept)
    place = axis_word(SPLIT)
    word = jnp.concatenate([place, (axis_word("ch") - place * rows // lane + count) % count])
    return pl.pallas_call(
        kernel,
        grid_spec=pltpu.PrefetchScalarGridSpec(
            num_scalar_prefetch=1,
            grid=(1,),
            in_specs=[
                pl.BlockSpec(memory_space=pltpu.SMEM),
                pl.BlockSpec((planes, 1, points, lane), lambda step, word: (0, word[1], 0, 0)),
                whole_spec(errors.shape),
                pl.BlockSpec((1, 27, rows, cols), lambda step, word: (layer, 0, word[0], 0)),
                state_spec,
                state_spec,
            ]
            + [pl.BlockSpec(memory_space=pl.ANY)] * len(extra),
            out_specs=[whole_spec((27, rows, cols)), state_spec, state_spec],
            scratch_shapes=[
                pltpu.VMEM((each, planes, points + 2 * rows_z, lane), HALF),
                pltpu.VMEM((blocks * lane, 3 * cols), FLOAT),
            ],
        ),
        out_shape=[
            like((27, rows, cols), HALF),
            like(moments.shape, FLOAT),
            like(seconds.shape, FLOAT),
        ],
        input_output_aliases={7: 1, 8: 2} if extra else {},
        compiler_params=BIG,
    )(word, scale.reshape(1), every, errors, kernels, moments, seconds, *extra)


def settle(gathered, shape, layer, kept):
    count, taps, rows, cols = gathered.shape

    def kernel(*refs):
        refs[-1][0] = refs[0][0]

    extra = list(kept)
    return pl.pallas_call(
        kernel,
        grid=(count,),
        in_specs=[pl.BlockSpec((1, taps, rows, cols), lambda step: (step, 0, 0, 0))]
        + [pl.BlockSpec(memory_space=pl.ANY)] * len(extra),
        out_specs=pl.BlockSpec((1, taps, rows, cols), lambda step: (layer, 0, step, 0)),
        out_shape=like(shape, HALF),
        input_output_aliases={1: 0} if extra else {},
        compiler_params=BIG,
    )(gathered, *extra)


def silu_slope(value):
    sig = jax.nn.sigmoid(value)
    return sig * (1.0 + value * (1.0 - sig))


def adam(weight, moment, second, grad):
    moment_next = beta_one * moment + (1.0 - beta_one) * grad
    second_next = beta_two * second + (1.0 - beta_two) * grad * grad
    weight_next = weight.astype(jnp.float32) - learn_rate * (moment_next / bias_one) / (
        jnp.sqrt(second_next / bias_two) + adam_eps
    )
    return (weight_next.astype(jnp.bfloat16), moment_next, second_next)


def total_of(block, axis):
    by = 1
    while by < lax.axis_size(axis):
        block = block + shift(block, axis, by)
        by *= 2
    return block


def body(flow, embed_w, conv_w, dec_w, conv_m, conv_v, dec_m, dec_v, loss_mask):
    rows_y = flow.shape[2] * lax.axis_size("ch") // PATCH
    rows_z = flow.shape[3] // PATCH
    width = conv_w.shape[2]
    channels = conv_w.shape[3]
    block = dec_w.shape[1]
    place = lax.axis_index(SPLIT)
    dec_rows = dec_m.shape[0]

    rounded = flow.astype(HALF).astype(FLOAT)
    patches = to_patches(flow)
    every_patch = lax.all_gather(patches, "ch", axis=0)
    count = lax.axis_size("ch")
    embedded = jnp.dot(
        every_patch.reshape(-1, patches.shape[1]), embed_w, preferred_element_type=FLOAT
    ).astype(HALF)

    state = with_halo(flow, ((SPLIT, 1), ("ch", 2)), FLOW_STEPS)
    for step in range(FLOW_STEPS):
        state = advance(state)
    change = to_patches(rounded - state)
    changes = scattered(
        lambda k: lax.dynamic_slice_in_dim(change, k * block, block, 1), "ch"
    )

    pre_one, act_one, near_one = conv_layer(embedded, conv_w, 0, rows_y, rows_z)
    pre_two, act_two, near_two = conv_layer(act_one, conv_w, 1, rows_y, rows_z)

    mask = loss_mask.reshape(-1, 1).astype(FLOAT)
    top, d_pred, sums, d_act_two, *pieces = predict(
        rotations(act_two, "ch"), changes, dec_w, mask, channels
    )
    sums = total_of(total_of(sums, "ch"), SPLIT)[:, 0, 0]
    denom = jnp.maximum(sums[1] / count, 1.0) * OUT
    loss = sums[0] / denom
    scale = 2.0 / denom

    def reduced(own, pieces):
        for by, piece in enumerate(pieces):
            own = own + shift(piece, "ch", by + 1).astype(FLOAT)
        return own

    d_act_two = reduced(d_act_two, pieces)
    d_pre_two = (d_act_two * silu_slope(pre_two)).astype(HALF)
    errors_two = lax.all_gather(d_pre_two, SPLIT, axis=0)
    own_back, *pieces = conv_back(errors_two, conv_w, 1, rows_y, rows_z, count)
    d_act_one = d_act_two + reduced(own_back, pieces)
    d_pre_one = (d_act_one * silu_slope(pre_one)).astype(HALF)
    errors_one = lax.all_gather(d_pre_one, SPLIT, axis=0)

    grad_dec = lax.dot_general(top, d_pred, (((0,), (0,)), ((), ())), preferred_element_type=FLOAT)
    grad_dec = lax.all_to_all(
        grad_dec.astype(HALF).reshape(-1, dec_rows, block), SPLIT, 0, 0, tiled=False
    )
    grad_dec = jnp.sum(grad_dec.astype(FLOAT), axis=0) * scale
    dec_own = lax.dynamic_slice_in_dim(dec_w, place * dec_rows, dec_rows, 0)
    dec_shard, dec_m_next, dec_v_next = adam(dec_own, dec_m, dec_v, grad_dec)
    dec_next = lax.all_gather(dec_shard, SPLIT, axis=0, tiled=True)

    rows_two = lax.all_gather(near_two, SPLIT, axis=0)
    rows_one = lax.all_gather(near_one, SPLIT, axis=0)
    two_shard, *moments = kernel_step(
        rows_two, errors_two, scale, conv_w, conv_m, conv_v, 1, (), rows_y, rows_z
    )
    one_shard, *moments = kernel_step(
        rows_one, errors_one, scale, conv_w, conv_m, conv_v, 0, moments, rows_y, rows_z
    )
    conv_next = settle(lax.all_gather(two_shard, SPLIT, axis=0), conv_w.shape, 1, ())
    conv_next = settle(lax.all_gather(one_shard, SPLIT, axis=0), conv_w.shape, 0, (conv_next,))
    return (
        state,
        loss,
        conv_next,
        dec_next,
        *moments,
        dec_m_next,
        dec_v_next,
    )


def solution(mesh):
    return jax.shard_map(
        body,
        mesh=mesh,
        in_specs=(
            P(None, ("grp", "sp"), "ch", None),
            P(None, "ch"),
            P(None, None, None, "ch"),
            P(None, "ch"),
            P(None, None, ("grp", "sp"), "ch"),
            P(None, None, ("grp", "sp"), "ch"),
            P(("grp", "sp"), "ch"),
            P(("grp", "sp"), "ch"),
            P(("grp", "sp"), None, None),
        ),
        out_specs=(
            P(None, ("grp", "sp"), "ch", None),
            P(),
            P(None, None, None, "ch"),
            P(None, "ch"),
            P(None, None, ("grp", "sp"), "ch"),
            P(None, None, ("grp", "sp"), "ch"),
            P(("grp", "sp"), "ch"),
            P(("grp", "sp"), "ch"),
        ),
        check_vma=False,
    )
```

time: 469 us -> 271 us (0.58)
  waiting for transfers between devices: 203 us -> 105 us
  blocking collectives: 90.6 us -> 32.9 us
  local copies, waits for them, and re-layouts: 80.3 us -> 23.5 us
  Pallas kernels: 0 us -> 46.6 us
  matrix products: 28.2 us -> 2.76 us
  other arithmetic: 27.9 us -> 6.33 us
  starting transfers between devices: 19.3 us -> 35.8 us
    reduce_scatter x4 -> x0, waiting for transfers between devices: 146 us -> none  [the longest x1 95.3 us: body(): lax.psum_scatter(local_conv, ('grp', 'sp'), scatter_dimension=2, tiled=True)]
    ppermute x10 -> x31, waiting for transfers between devices: 13.9 us -> 60.6 us  [shift(): lax.ppermute(block, axis, [(i, (i + by) % count) for i in range(count)])]
    pallas_call x0 -> x10, Pallas kernels: none -> 46.6 us  [the longest x2 14.6 us: kernel_step(): pl.pallas_call(kernel, grid_spec=pltpu.PrefetchScalarGridSpec(num_scalar_...]
    psum x1 -> x0, blocking collectives: 38.9 us -> none  [body(): lax.psum((jnp.sum(weights * resid * resid), jnp.sum(weights)), ('grp', 's...]
    dot_general x8 -> x1, matrix products: 26.9 us -> 1.64 us  [body(): jnp.dot(every_patch.reshape(-1, patches.shape[1]), embed_w, preferred_ele...]
    transpose x3 -> x0, local copies, waits for them, and re-layouts: 20.5 us -> none  [the longest x2 13.7 us: body(): turned = jnp.transpose(conv_w[1], (0, 2, 1)).reshape(-1, width)]
    dot_general x2 -> x0, local copies, waits for them, and re-layouts: 20.1 us -> none  [column_grad(): lax.dot_general(columns, error, (((0,), (0,)), ((), ())), preferred_eleme...]
    all_gather x4 -> x3, blocking collectives: 51.7 us -> 32.9 us  [the longest x1 11.7 us: body(): errors_one = lax.all_gather(d_pre_one, SPLIT, axis=0)]
  transfers between devices with their start and end apart: 17 -> 37, of which waited for: 9 -> 23; matrix products, arithmetic and copies ran while one was open for 20% -> 3% of each run, Pallas kernels for 0% -> 13%
where the time goes in v1:
time: 271 us; the launch traced here: 270 us
  waiting for transfers between devices  105 us (39%)
  Pallas kernels  46.6 us (17%)
  starting transfers between devices  35.8 us (13%)
  blocking collectives  32.9 us (12%)
  local copies, waits for them, and re-layouts  23.5 us (9%)
  between operations  16.6 us (6%)
  other arithmetic  6.33 us (2%)
  matrix products  2.76 us (1%)
    ppermute x31, waiting for transfers between devices, shift(): lax.ppermute(block, axis, [(i, (i + by) % count) for i in range(count)])  60.6 us
    ppermute x31, starting transfers between devices, shift(): lax.ppermute(block, axis, [(i, (i + by) % count) for i in range(count)])  32.1 us
    all_gather x1, waiting for transfers between devices, body(): every_patch = lax.all_gather(patches, 'ch', axis=0)  30.8 us
    unnamed x75, local copies, waits for them, and re-layouts  21 us
    pallas_call x2, Pallas kernels, kernel_step(): pl.pallas_call(kernel, grid_spec=pltpu.PrefetchScalarGridSpec(num_scalar_...  14.6 us
    all_to_all x1, waiting for transfers between devices, body(): lax.all_to_all(grad_dec.astype(HALF).reshape(-1, dec_rows, block), SPLIT,...  13.8 us
    pallas_call x2, Pallas kernels, conv_layer(): pl.pallas_call(kernel, grid=(9,), out_shape=(like((rows, cols), FLOAT), l...  13.7 us
    all_gather x1, blocking collectives, body(): errors_one = lax.all_gather(d_pre_one, SPLIT, axis=0)  11.7 us
  transfers between devices with their start and end apart: 37, of which 23 were waited for; matrix products, arithmetic and copies ran while one was open for 3% of the time, Pallas kernels for 13%

profile of v1, /device:TPU:0, one launch (start us, length us, event | category | flops | bytes accessed | tf_op | source)
XLA Modules:
  0.0 269.7 jit_solution(17584934402238279285)
XLA Ops:
  8.3 1.7 shard_map.152
  10.1 30.8 %all-gather.13.cloned.1.call-done = bf16[256,2048]{1,0:T(8,128)(2,1)} async-done(((bf16[64,2048]{1,0:T(8,128)(2,1)}), bf16[256,2048]{1,0:T(8,128)(2,1)}) %all-gather.13.cloned.1.call-update) | async-done | bytes 1048592 | tf_op jit(solution)/shard_map/all_gather | solution.py:479
  40.9 1.6 convolution_convert_fusion.1.act_ref
  42.5 1.8 collective-permute-start.6
  46.9 4.0 %collective-permute-done.5 = bf16[256,128]{1,0:T(8,128)(2,1)S(1)} collective-permute-done((bf16[256,128]{1,0:T(8,128)(2,1)S(1)}, bf16[256,128]{1,0:T(8,128)(2,1)S(1)}, u32[]{:S(2)}, u32[]{:S(2)}) %collective-permute-start.5) | collective-permute-done | bytes 65568 | tf_op jit(solution)/shard_map/ppermute | solution.py:26
  51.7 2.6 collective-permute-start.8
  54.3 5.1 %collective-permute-done.7.below_ref = bf16[4,256,128]{2,1,0:T(8,128)(2,1)S(1)} collective-permute-done((bf16[4,256,128]{2,1,0:T(8,128)(2,1)S(1)}, bf16[4,256,128]{2,1,0:T(8,128)(2,1)S(1)}, u32[]{:S(2)}, u32[]{:S(2)}) %collective-permute-start.7) | collective-permute-done | bytes 262176 | tf_op jit(solution)/shard_map/ppermute | solution.py:26
  59.4 6.9 %shard_map.153 = (f32[256,128]{1,0:T(8,128)S(1)}, bf16[256,128]{1,0:T(8,128)(2,1)S(1)}) custom-call(s32[1]{0:T(128)} %bitcast.6.own_ref, bf16[4,256,128]{2,1,0:T(8,128)(2,1)S(1)} %collective-permute-done.7.below_ref, bf16[4,256,128]{2,1,0:T(8,128)(2,1)S(1)} %pad_maximum_fusion.7.near_ref, bf16[4,256,128]{2,1,0:T(8,128)(2,1)S(1)} %collective-permute-done.8.above_ref, ...), custom_call_target="tpu_custom_call" | custom-call | tf_op jit(solution)/shard_map/pallas_call | solution.py:189
  66.3 1.4 collective-permute-start.11
  68.0 1.9 collective-permute-start.9
  70.7 5.3 %collective-permute-done.10 = bf16[256,128]{1,0:T(8,128)(2,1)S(1)} collective-permute-done((bf16[256,128]{1,0:T(8,128)(2,1)S(1)}, bf16[256,128]{1,0:T(8,128)(2,1)S(1)}, u32[]{:S(2)}, u32[]{:S(2)}) %collective-permute-start.10) | collective-permute-done | bytes 65568 | tf_op jit(solution)/shard_map/ppermute | solution.py:26
  77.1 2.5 collective-permute-start.1
  79.6 2.9 %collective-permute-done = f32[4,2,16,256]{3,2,1,0:T(8,128)S(1)} collective-permute-done((f32[4,2,16,256]{3,2,1,0:T(8,128)S(1)}, f32[4,2,16,256]{3,2,1,0:T(8,128)S(1)}, u32[]{:S(2)}, u32[]{:S(2)}) %collective-permute-start) | collective-permute-done | bytes 131104 | tf_op jit(solution)/shard_map/ppermute | solution.py:26
  82.7 1.8 collective-permute-start.3
  84.8 3.6 %collective-permute-done.3 = f32[4,12,2,256]{3,2,1,0:T(2,128)S(1)} collective-permute-done((f32[4,12,2,256]{3,2,1,0:T(2,128)S(1)}, f32[4,12,2,256]{3,2,1,0:T(2,128)S(1)}, u32[]{:S(2)}, u32[]{:S(2)}) %collective-permute-start.3) | collective-permute-done | bytes 98336 | tf_op jit(solution)/shard_map/ppermute | solution.py:26
  88.4 3.2 %collective-permute-done.2 = f32[4,12,2,256]{3,2,1,0:T(2,128)S(1)} collective-permute-done((f32[4,12,2,256]{3,2,1,0:T(2,128)S(1)}, f32[4,12,2,256]{3,2,1,0:T(2,128)S(1)}, u32[]{:S(2)}, u32[]{:S(2)}) %collective-permute-start.2) | collective-permute-done | bytes 98336 | tf_op jit(solution)/shard_map/ppermute | solution.py:26
  94.5 2.6 collective-permute-start.13
  97.2 1.3 convert_subtract_fusion
  100.3 2.1 collective-permute-start.18
  102.4 1.6 collective-permute-start.19
  104.0 4.3 %collective-permute-done.12.below_ref = bf16[4,256,128]{2,1,0:T(8,128)(2,1)S(1)} collective-permute-done((bf16[4,256,128]{2,1,0:T(8,128)(2,1)S(1)}, bf16[4,256,128]{2,1,0:T(8,128)(2,1)S(1)}, u32[]{:S(2)}, u32[]{:S(2)}) %collective-permute-start.12) | collective-permute-done | bytes 262176 | tf_op jit(solution)/shard_map/ppermute | solution.py:26
  108.2 6.8 %shard_map.154 = (f32[256,128]{1,0:T(8,128)S(1)}, bf16[256,128]{1,0:T(8,128)(2,1)S(1)}) custom-call(s32[1]{0:T(128)} %bitcast.6.own_ref, bf16[4,256,128]{2,1,0:T(8,128)(2,1)S(1)} %collective-permute-done.12.below_ref, bf16[4,256,128]{2,1,0:T(8,128)(2,1)S(1)} %copy-done.9, bf16[4,256,128]{2,1,0:T(8,128)(2,1)S(1)} %collective-permute-done.13.above_ref, ...), custom_call_target="tpu_custom_call" | custom-call | tf_op jit(solution)/shard_map/pallas_call | solution.py:189
  116.4 2.4 collective-permute-start.15
  121.1 1.5 collective-permute-done.14.refs_1_
  129.7 1.5 shard_map.156
  134.9 4.4 %collective-permute-done.20 = f32[2,8,128]{2,1,0:T(8,128)S(1)} collective-permute-done((f32[2,8,128]{2,1,0:T(8,128)S(1)}, f32[2,8,128]{2,1,0:T(8,128)S(1)}, u32[]{:S(2)}, u32[]{:S(2)}) %collective-permute-start.20) | collective-permute-done | bytes 8224 | tf_op jit(solution)/shard_map/ppermute | solution.py:26
  139.3 4.5 %collective-permute-done.21 = f32[2,8,128]{2,1,0:T(8,128)S(1)} collective-permute-done((f32[2,8,128]{2,1,0:T(8,128)S(1)}, f32[2,8,128]{2,1,0:T(8,128)S(1)}, u32[]{:S(2)}, u32[]{:S(2)}) %collective-permute-start.21) | collective-permute-done | bytes 8224 | tf_op jit(solution)/shard_map/ppermute | solution.py:26
  143.9 4.0 %collective-permute-done.22 = f32[2,8,128]{2,1,0:T(8,128)S(1)} collective-permute-done((f32[2,8,128]{2,1,0:T(8,128)S(1)}, f32[2,8,128]{2,1,0:T(8,128)S(1)}, u32[]{:S(2)}, u32[]{:S(2)}) %collective-permute-start.22) | collective-permute-done | bytes 8224 | tf_op jit(solution)/shard_map/ppermute | solution.py:26
  147.8 4.5 %collective-permute-done.23 = f32[2,8,128]{2,1,0:T(8,128)S(1)} collective-permute-done((f32[2,8,128]{2,1,0:T(8,128)S(1)}, f32[2,8,128]{2,1,0:T(8,128)S(1)}, u32[]{:S(2)}, u32[]{:S(2)}) %collective-permute-start.23) | collective-permute-done | bytes 8224 | tf_op jit(solution)/shard_map/ppermute | solution.py:26
  157.9 3.2 %collective-permute-done.26 = bf16[256,128]{1,0:T(8,128)(2,1)S(1)} collective-permute-done((bf16[256,128]{1,0:T(8,128)(2,1)}, bf16[256,128]{1,0:T(8,128)(2,1)S(1)}, u32[]{:S(2)}, u32[]{:S(2)}) %collective-permute-start.26) | collective-permute-done | bytes 65568 | tf_op jit(solution)/shard_map/ppermute | solution.py:26
  162.7 9.7 %all-gather.2 = bf16[2048,128]{1,0:T(8,128)(2,1)S(1)} all-gather(bf16[256,128]{1,0:T(8,128)(2,1)S(1)} %multiply_convert_fusion.1), channel_id=4, replica_groups=mesh['grp'=2,'sp'=4,'ch'=4] {'grp','sp'}, dimensions={0}, use_global_device_ids=true | all-gather | bytes 589824 | tf_op jit(solution)/shard_map/all_gather | solution.py:512
  172.4 1.5 copy-done.2
  173.9 7.3 %shard_map.158 = (bf16[27,64,128]{2,1,0:T(8,128)(2,1)}, f32[2,27,64,128]{3,2,1,0:T(8,128)}, f32[2,27,64,128]{3,2,1,0:T(8,128)}) custom-call(s32[2]{0:T(128)S(1)} %pad_add_fusion.word_ref, f32[1]{0:T(128)} %bitcast.17.scale_ref, bf16[8,4,256,128]{3,2,1,0:T(8,128)(2,1)} %bitcast.46, bf16[8,256,128]{2,1,0:T(8,128)(2,1)S(1)} %bitcast.36, ...), custom_call_target="tpu_custom_call" | custom-call | tf_op jit(solution)/shard_map/pallas_call | solution.py:397
  181.3 7.5 %shard_map.157 = (f32[256,128]{1,0:T(8,128)S(1)}, bf16[256,128]{1,0:T(8,128)(2,1)S(1)}, bf16[256,128]{1,0:T(8,128)(2,1)S(1)}, bf16[256,128]{1,0:T(8,128)(2,1)S(1)}) custom-call(s32[2]{0:T(128)S(1)} %pad_add_fusion.1.own_ref, bf16[8,256,128]{2,1,0:T(8,128)(2,1)S(1)} %bitcast.37, bf16[8,256,128]{2,1,0:T(8,128)(2,1)S(1)} %bitcast.38, ...), custom_call_target="tpu_custom_call" | custom-call | tf_op jit(solution)/shard_map/pallas_call | solution.py:262
  190.1 1.4 collective-permute-start.28
  191.5 1.7 collective-permute-done.30
  193.3 4.6 %collective-permute-done.29 = bf16[256,128]{1,0:T(8,128)(2,1)S(1)} collective-permute-done((bf16[256,128]{1,0:T(8,128)(2,1)S(1)}, bf16[256,128]{1,0:T(8,128)(2,1)S(1)}, u32[]{:S(2)}, u32[]{:S(2)}) %collective-permute-start.29) | collective-permute-done | bytes 65568 | tf_op jit(solution)/shard_map/ppermute | solution.py:26
  198.0 11.7 %all-gather.3 = bf16[2048,128]{1,0:T(8,128)(2,1)S(1)} all-gather(bf16[256,128]{1,0:T(8,128)(2,1)S(1)} %multiply_convert_fusion), channel_id=5, replica_groups=mesh['grp'=2,'sp'=4,'ch'=4] {'grp','sp'}, dimensions={0}, use_global_device_ids=true | all-gather | bytes 589824 | tf_op jit(solution)/shard_map/all_gather | solution.py:516
  209.6 1.5 copy-done.3
  211.1 7.3 %shard_map.159 = (bf16[27,64,128]{2,1,0:T(8,128)(2,1)}, f32[2,27,64,128]{3,2,1,0:T(8,128)}, f32[2,27,64,128]{3,2,1,0:T(8,128)}) custom-call(s32[2]{0:T(128)S(1)} %pad_add_fusion.word_ref, f32[1]{0:T(128)} %bitcast.17.scale_ref, bf16[8,4,256,128]{3,2,1,0:T(8,128)(2,1)} %bitcast.45, ...), custom_call_target="tpu_custom_call", output_to_operand_aliasing={{1}: (7, {}), {2}: (8, {})} | custom-call | tf_op jit(solution)/shard_map/pallas_call | solution.py:397
  219.6 3.5 %all-to-all-start = ((bf16[8,64,512]{2,1,0:T(8,128)(2,1)}), bf16[8,64,512]{2,1,0:T(8,128)(2,1)S(1)}, u32[]{:S(2)}, u32[]{:S(2)}) async-start(bf16[8,64,512]{2,1,0:T(8,128)(2,1)} %bitcast.24), calls=%async_computation | async-start | bytes 1048576 | tf_op jit(solution)/shard_map/all_to_all | solution.py:519
  223.7 13.8 %all-to-all-done = bf16[8,64,512]{2,1,0:T(8,128)(2,1)S(1)} async-done(((bf16[8,64,512]{2,1,0:T(8,128)(2,1)}), bf16[8,64,512]{2,1,0:T(8,128)(2,1)S(1)}, u32[]{:S(2)}, u32[]{:S(2)}) %all-to-all-start) | async-done | bytes 524320 | tf_op jit(solution)/shard_map/all_to_all | solution.py:519
  237.6 1.6 subtract_convert_fusion
  239.2 11.5 %all_gather.59 = bf16[512,512]{1,0:T(8,128)(2,1)S(1)} all-gather(bf16[64,512]{1,0:T(8,128)(2,1)S(1)} %get-tuple-element.50), channel_id=1, replica_groups=mesh['grp'=2,'sp'=4,'ch'=4] {'grp','sp'}, dimensions={0}, use_global_device_ids=true | all-gather | bytes 589824 | tf_op jit(solution)/shard_map/all_gather | solution.py:525
  250.7 2.0 copy-done.6
  252.7 3.3 %shard_map.160.refs_1_ = bf16[2,27,512,128]{3,2,1,0:T(8,128)(2,1)} custom-call(bf16[8,27,64,128]{3,2,1,0:T(8,128)(2,1)S(1)} %bitcast.40), custom_call_target="tpu_custom_call" | custom-call | tf_op jit(solution)/shard_map/pallas_call | solution.py:434
  256.0 2.0 copy-done.7
  258.0 3.3 %shard_map.161 = bf16[2,27,512,128]{3,2,1,0:T(8,128)(2,1)} custom-call(bf16[8,27,64,128]{3,2,1,0:T(8,128)(2,1)S(1)} %bitcast.41, bf16[2,27,512,128]{3,2,1,0:T(8,128)(2,1)} %shard_map.160.refs_1_), custom_call_target="tpu_custom_call", output_to_operand_aliasing={{}: (1, {})} | custom-call | tf_op jit(solution)/shard_map/pallas_call | solution.py:434
  (150 shorter events, 36.0 us)
Async XLA Ops:
  7.2 33.7 %copy-start = (bf16[2048,128]{1,0:T(8,128)(2,1)S(1)}, bf16[2048,128]{1,0:T(8,128)(2,1)}, u32[]{:S(2)}) copy-start(bf16[2048,128]{1,0:T(8,128)(2,1)} %param.10) | copy-start | bytes 1572868
  7.2 33.7 %all-gather.13.cloned.1.call-start = ((), (), s32[]{:S(2)}) async-start(), calls=%async_computation.1 | async-start | bytes 1310720 | tf_op jit(solution)/shard_map/all_gather | solution.py:479
  10.0 162.4 %all-gather.17.cloned.1.call-start = ((), (), s32[]{:S(2)}) async-start(), calls=%async_computation.3 | async-start | bytes 2359296 | tf_op jit(solution)/shard_map/all_gather | solution.py:527
  42.5 4.3 %collective-permute-start.6 = (bf16[256,128]{1,0:T(8,128)(2,1)S(1)}, bf16[256,128]{1,0:T(8,128)(2,1)S(1)}, u32[]{:S(2)}, u32[]{:S(2)}) collective-permute-start(bf16[256,128]{1,0:T(8,128)(2,1)S(1)} %convolution_convert_fusion.1.act_ref), channel_id=1, source_target_pairs={{0,3},{1,0},{2,1},{3,2},{4,7},{5,4},{6,5},{7,6},{8,11},{9,8},{10,9... | collective-permute-start | bytes 196616 | tf_op jit(solution)/shard_map/ppermute | solution.py:26
  44.4 6.5 %collective-permute-start.5 = (bf16[256,128]{1,0:T(8,128)(2,1)S(1)}, bf16[256,128]{1,0:T(8,128)(2,1)S(1)}, u32[]{:S(2)}, u32[]{:S(2)}) collective-permute-start(bf16[256,128]{1,0:T(8,128)(2,1)S(1)} %convolution_convert_fusion.1.act_ref), channel_id=1, source_target_pairs={{0,2},{1,3},{2,0},{3,1},{4,6},{5,7},{6,4},{7,5},{8,10},{9,11},{10,... | collective-permute-start | bytes 196616 | tf_op jit(solution)/shard_map/ppermute | solution.py:26
  45.5 6.1 %collective-permute-start.4 = (bf16[256,128]{1,0:T(8,128)(2,1)S(1)}, bf16[256,128]{1,0:T(8,128)(2,1)S(1)}, u32[]{:S(2)}, u32[]{:S(2)}) collective-permute-start(bf16[256,128]{1,0:T(8,128)(2,1)S(1)} %convolution_convert_fusion.1.act_ref), channel_id=1, source_target_pairs={{0,1},{1,2},{2,3},{3,0},{4,5},{5,6},{6,7},{7,4},{8,9},{9,10},{10,1... | collective-permute-start | bytes 196616 | tf_op jit(solution)/shard_map/ppermute | solution.py:26
  51.6 14.7 %copy-start.8 = (bf16[4,256,128]{2,1,0:T(8,128)(2,1)}, bf16[4,256,128]{2,1,0:T(8,128)(2,1)S(1)}, u32[]{:S(2)}) copy-start(bf16[4,256,128]{2,1,0:T(8,128)(2,1)S(1)} %pad_maximum_fusion.7.near_ref) | copy-start | bytes 786436
  51.6 7.8 %collective-permute-start.7 = (bf16[4,256,128]{2,1,0:T(8,128)(2,1)S(1)}, bf16[4,256,128]{2,1,0:T(8,128)(2,1)S(1)}, u32[]{:S(2)}, u32[]{:S(2)}) collective-permute-start(bf16[4,256,128]{2,1,0:T(8,128)(2,1)S(1)} %pad_maximum_fusion.7.near_ref), channel_id=1, source_target_pairs={{0,4},{4,8},{8,12},{12,16},{16,20},{20,24},{24,28},{28,0},{1,5},{5... | collective-permute-start | bytes 786440 | tf_op jit(solution)/shard_map/ppermute | solution.py:26
  51.7 7.7 %collective-permute-start.8 = (bf16[4,256,128]{2,1,0:T(8,128)(2,1)S(1)}, bf16[4,256,128]{2,1,0:T(8,128)(2,1)S(1)}, u32[]{:S(2)}, u32[]{:S(2)}) collective-permute-start(bf16[4,256,128]{2,1,0:T(8,128)(2,1)S(1)} %pad_maximum_fusion.7.near_ref), channel_id=1, source_target_pairs={{0,28},{4,0},{8,4},{12,8},{16,12},{20,16},{24,20},{28,24},{1,29},{... | collective-permute-start | bytes 786440 | tf_op jit(solution)/shard_map/ppermute | solution.py:26
  59.4 17.4 %copy-start.5 = (f32[4,8,16,256]{3,2,1,0:T(8,128)S(1)}, f32[4,8,16,256]{3,2,1,0:T(8,128)}, u32[]{:S(2)}) copy-start(f32[4,8,16,256]{3,2,1,0:T(8,128)} %field_ref.1) | copy-start | bytes 1572868
  66.3 4.4 %collective-permute-start.11 = (bf16[256,128]{1,0:T(8,128)(2,1)S(1)}, bf16[256,128]{1,0:T(8,128)(2,1)S(1)}, u32[]{:S(2)}, u32[]{:S(2)}) collective-permute-start(bf16[256,128]{1,0:T(8,128)(2,1)S(1)} %get-tuple-element.29.act_ref), channel_id=1, source_target_pairs={{0,3},{1,0},{2,1},{3,2},{4,7},{5,4},{6,5},{7,6},{8,11},{9,8},{10,9... | collective-permute-start | bytes 196616 | tf_op jit(solution)/shard_map/ppermute | solution.py:26
  67.7 8.3 %collective-permute-start.10 = (bf16[256,128]{1,0:T(8,128)(2,1)S(1)}, bf16[256,128]{1,0:T(8,128)(2,1)S(1)}, u32[]{:S(2)}, u32[]{:S(2)}) collective-permute-start(bf16[256,128]{1,0:T(8,128)(2,1)S(1)} %get-tuple-element.29.act_ref), channel_id=1, source_target_pairs={{0,2},{1,3},{2,0},{3,1},{4,6},{5,7},{6,4},{7,5},{8,10},{9,11},{10,... | collective-permute-start | bytes 196616 | tf_op jit(solution)/shard_map/ppermute | solution.py:26
  68.0 8.0 %collective-permute-start.9 = (bf16[256,128]{1,0:T(8,128)(2,1)S(1)}, bf16[256,128]{1,0:T(8,128)(2,1)S(1)}, u32[]{:S(2)}, u32[]{:S(2)}) collective-permute-start(bf16[256,128]{1,0:T(8,128)(2,1)S(1)} %get-tuple-element.29.act_ref), channel_id=1, source_target_pairs={{0,1},{1,2},{2,3},{3,0},{4,5},{5,6},{6,7},{7,4},{8,9},{9,10},{10,1... | collective-permute-start | bytes 196616 | tf_op jit(solution)/shard_map/ppermute | solution.py:26
  76.8 132.8 %all-gather.15.cloned.1.call-start = ((), (), s32[]{:S(2)}) async-start(), calls=%async_computation.2 | async-start | bytes 2359296 | tf_op jit(solution)/shard_map/all_gather | solution.py:528
  76.9 5.6 %collective-permute-start = (f32[4,2,16,256]{3,2,1,0:T(8,128)S(1)}, f32[4,2,16,256]{3,2,1,0:T(8,128)S(1)}, u32[]{:S(2)}, u32[]{:S(2)}) collective-permute-start(f32[4,2,16,256]{3,2,1,0:T(8,128)S(1)} %get-tuple-element.72), channel_id=1, source_target_pairs={{0,4},{4,8},{8,12},{12,16},{16,20},{20,24},{24,28},{28,0},{1,5},{5... | collective-permute-start | bytes 393224 | tf_op jit(solution)/shard_map/ppermute | solution.py:26
  77.1 5.5 %collective-permute-start.1 = (f32[4,2,16,256]{3,2,1,0:T(8,128)S(1)}, f32[4,2,16,256]{3,2,1,0:T(8,128)S(1)}, u32[]{:S(2)}, u32[]{:S(2)}) collective-permute-start(f32[4,2,16,256]{3,2,1,0:T(8,128)S(1)} %get-tuple-element.71), channel_id=1, source_target_pairs={{0,28},{4,0},{8,4},{12,8},{16,12},{20,16},{24,20},{28,24},{1,29},{... | collective-permute-start | bytes 393224 | tf_op jit(solution)/shard_map/ppermute | solution.py:26
  82.5 168.1 %all-gather.21.cloned.1.call-start = ((), (), s32[]{:S(2)}) async-start(), calls=%async_computation.5 | async-start | bytes 3981312 | tf_op jit(solution)/shard_map/all_gather | solution.py:535
  82.7 5.7 %collective-permute-start.3 = (f32[4,12,2,256]{3,2,1,0:T(2,128)S(1)}, f32[4,12,2,256]{3,2,1,0:T(2,128)S(1)}, u32[]{:S(2)}, u32[]{:S(2)}) collective-permute-start(f32[4,12,2,256]{3,2,1,0:T(2,128)S(1)} %get-tuple-element.70), channel_id=1, source_target_pairs={{0,3},{1,0},{2,1},{3,2},{4,7},{5,4},{6,5},{7,6},{8,11},{9,8},{10,9... | collective-permute-start | bytes 294920 | tf_op jit(solution)/shard_map/ppermute | solution.py:26
  84.5 7.1 %collective-permute-start.2 = (f32[4,12,2,256]{3,2,1,0:T(2,128)S(1)}, f32[4,12,2,256]{3,2,1,0:T(2,128)S(1)}, u32[]{:S(2)}, u32[]{:S(2)}) collective-permute-start(f32[4,12,2,256]{3,2,1,0:T(2,128)S(1)} %get-tuple-element.69), channel_id=1, source_target_pairs={{0,1},{1,2},{2,3},{3,0},{4,5},{5,6},{6,7},{7,4},{8,9},{9,10},{10,1... | collective-permute-start | bytes 294920 | tf_op jit(solution)/shard_map/ppermute | solution.py:26
  94.5 13.7 %collective-permute-start.12 = (bf16[4,256,128]{2,1,0:T(8,128)(2,1)S(1)}, bf16[4,256,128]{2,1,0:T(8,128)(2,1)S(1)}, u32[]{:S(2)}, u32[]{:S(2)}) collective-permute-start(bf16[4,256,128]{2,1,0:T(8,128)(2,1)S(1)} %copy-done.9), channel_id=1, source_target_pairs={{0,4},{4,8},{8,12},{12,16},{16,20},{20,24},{24,28},{28,0},{1,5},{5... | collective-permute-start | bytes 786440 | tf_op jit(solution)/shard_map/ppermute | solution.py:26
  94.5 13.7 %collective-permute-start.13 = (bf16[4,256,128]{2,1,0:T(8,128)(2,1)S(1)}, bf16[4,256,128]{2,1,0:T(8,128)(2,1)S(1)}, u32[]{:S(2)}, u32[]{:S(2)}) collective-permute-start(bf16[4,256,128]{2,1,0:T(8,128)(2,1)S(1)} %copy-done.9), channel_id=1, source_target_pairs={{0,28},{4,0},{8,4},{12,8},{16,12},{20,16},{24,20},{28,24},{1,29},{... | collective-permute-start | bytes 786440 | tf_op jit(solution)/shard_map/ppermute | solution.py:26
  100.2 18.6 %collective-permute-start.17 = (bf16[64,512]{1,0:T(8,128)(2,1)S(1)}, bf16[64,512]{1,0:T(8,128)(2,1)S(1)}, u32[]{:S(2)}, u32[]{:S(2)}) collective-permute-start(bf16[64,512]{1,0:T(8,128)(2,1)S(1)} %get-tuple-element.75), channel_id=1, source_target_pairs={{0,1},{1,2},{2,3},{3,0},{4,5},{5,6},{6,7},{7,4},{8,9},{9,10},{10,1... | collective-permute-start | bytes 196616 | tf_op jit(solution)/shard_map/ppermute | solution.py:26
  100.3 19.5 %collective-permute-start.18 = (bf16[64,512]{1,0:T(8,128)(2,1)}, bf16[64,512]{1,0:T(8,128)(2,1)S(1)}, u32[]{:S(2)}, u32[]{:S(2)}) collective-permute-start(bf16[64,512]{1,0:T(8,128)(2,1)} %get-tuple-element.74), channel_id=1, source_target_pairs={{0,2},{1,3},{2,0},{3,1},{4,6},{5,7},{6,4},{7,5},{8,10},{9,11},{10,... | collective-permute-start | bytes 196616 | tf_op jit(solution)/shard_map/ppermute | solution.py:26
  102.4 17.3 %copy-start.35 = (s32[1,8,32]{2,1,0:T(8,128)S(1)}, s32[1,8,32]{2,1,0:T(8,128)}, u32[]{:S(2)}) copy-start(s32[1,8,32]{2,1,0:T(8,128)} %param.17) | copy-start | bytes 3076
  102.4 22.3 %copy-start.10 = (bf16[512,512]{1,0:T(8,128)(2,1)S(1)}, bf16[512,512]{1,0:T(8,128)(2,1)}, u32[]{:S(2)}) copy-start(bf16[512,512]{1,0:T(8,128)(2,1)} %refs_8_.1) | copy-start | bytes 1572868
  102.4 18.0 %collective-permute-start.19 = (bf16[64,512]{1,0:T(8,128)(2,1)}, bf16[64,512]{1,0:T(8,128)(2,1)S(1)}, u32[]{:S(2)}, u32[]{:S(2)}) collective-permute-start(bf16[64,512]{1,0:T(8,128)(2,1)} %get-tuple-element.73), channel_id=1, source_target_pairs={{0,3},{1,0},{2,1},{3,2},{4,7},{5,4},{6,5},{7,6},{8,11},{9,8},{10,9... | collective-permute-start | bytes 196616 | tf_op jit(solution)/shard_map/ppermute | solution.py:26
  115.8 56.7 %copy-start.1 = (f32[2,27,64,128]{3,2,1,0:T(8,128)S(1)}, f32[2,27,64,128]{3,2,1,0:T(8,128)}, u32[]{:S(2)}) copy-start(f32[2,27,64,128]{3,2,1,0:T(8,128)} %m_ref.3) | copy-start | bytes 5308420
  115.8 6.8 %collective-permute-start.14 = (bf16[256,128]{1,0:T(8,128)(2,1)S(1)}, bf16[256,128]{1,0:T(8,128)(2,1)S(1)}, u32[]{:S(2)}, u32[]{:S(2)}) collective-permute-start(bf16[256,128]{1,0:T(8,128)(2,1)S(1)} %get-tuple-element.30.refs_0_), channel_id=1, source_target_pairs={{0,1},{1,2},{2,3},{3,0},{4,5},{5,6},{6,7},{7,4},{8,9},{9,10},{10,1... | collective-permute-start | bytes 196616 | tf_op jit(solution)/shard_map/ppermute | solution.py:26
  116.4 7.6 %collective-permute-start.15 = (bf16[256,128]{1,0:T(8,128)(2,1)S(1)}, bf16[256,128]{1,0:T(8,128)(2,1)S(1)}, u32[]{:S(2)}, u32[]{:S(2)}) collective-permute-start(bf16[256,128]{1,0:T(8,128)(2,1)S(1)} %get-tuple-element.30.refs_0_), channel_id=1, source_target_pairs={{0,2},{1,3},{2,0},{3,1},{4,6},{5,7},{6,4},{7,5},{8,10},{9,11},{10,... | collective-permute-start | bytes 196616 | tf_op jit(solution)/shard_map/ppermute | solution.py:26
  118.8 5.9 %collective-permute-start.16 = (bf16[256,128]{1,0:T(8,128)(2,1)S(1)}, bf16[256,128]{1,0:T(8,128)(2,1)}, u32[]{:S(2)}, u32[]{:S(2)}) collective-permute-start(bf16[256,128]{1,0:T(8,128)(2,1)S(1)} %get-tuple-element.30.refs_0_), channel_id=1, source_target_pairs={{0,3},{1,0},{2,1},{3,2},{4,7},{5,4},{6,5},{7,6},{8,11},{9,8},{10,9... | collective-permute-start | bytes 196616 | tf_op jit(solution)/shard_map/ppermute | solution.py:26
  133.8 5.4 %collective-permute-start.20 = (f32[2,8,128]{2,1,0:T(8,128)S(1)}, f32[2,8,128]{2,1,0:T(8,128)S(1)}, u32[]{:S(2)}, u32[]{:S(2)}) collective-permute-start(f32[2,8,128]{2,1,0:T(8,128)S(1)} %get-tuple-element.31), channel_id=1, source_target_pairs={{0,1},{1,2},{2,3},{3,0},{4,5},{5,6},{6,7},{7,4},{8,9},{9,10},{10,1... | collective-permute-start | bytes 24584 | tf_op jit(solution)/shard_map/ppermute | solution.py:26
  139.3 4.5 %collective-permute-start.21 = (f32[2,8,128]{2,1,0:T(8,128)S(1)}, f32[2,8,128]{2,1,0:T(8,128)S(1)}, u32[]{:S(2)}, u32[]{:S(2)}) collective-permute-start(f32[2,8,128]{2,1,0:T(8,128)S(1)} %add.191), channel_id=1, source_target_pairs={{0,2},{1,3},{2,0},{3,1},{4,6},{5,7},{6,4},{7,5},{8,10},{9,11},{10,... | collective-permute-start | bytes 24584 | tf_op jit(solution)/shard_map/ppermute | solution.py:26
  143.9 4.0 %collective-permute-start.22 = (f32[2,8,128]{2,1,0:T(8,128)S(1)}, f32[2,8,128]{2,1,0:T(8,128)S(1)}, u32[]{:S(2)}, u32[]{:S(2)}) collective-permute-start(f32[2,8,128]{2,1,0:T(8,128)S(1)} %add.192), channel_id=1, source_target_pairs={{0,4},{4,8},{8,12},{12,16},{16,20},{20,24},{24,28},{28,0},{1,5},{5... | collective-permute-start | bytes 24584 | tf_op jit(solution)/shard_map/ppermute | solution.py:26
  147.8 4.5 %collective-permute-start.23 = (f32[2,8,128]{2,1,0:T(8,128)S(1)}, f32[2,8,128]{2,1,0:T(8,128)S(1)}, u32[]{:S(2)}, u32[]{:S(2)}) collective-permute-start(f32[2,8,128]{2,1,0:T(8,128)S(1)} %add.193), channel_id=1, source_target_pairs={{0,8},{4,12},{8,16},{12,20},{16,24},{20,28},{24,0},{28,4},{1,9},{5... | collective-permute-start | bytes 24584 | tf_op jit(solution)/shard_map/ppermute | solution.py:26
  152.4 3.7 %collective-permute-start.24 = (f32[2,8,128]{2,1,0:T(8,128)S(1)}, f32[2,8,128]{2,1,0:T(8,128)S(1)}, u32[]{:S(2)}, u32[]{:S(2)}) collective-permute-start(f32[2,8,128]{2,1,0:T(8,128)S(1)} %add.194), channel_id=1, source_target_pairs={{0,16},{4,20},{8,24},{12,28},{16,0},{20,4},{24,8},{28,12},{1,17},{... | collective-permute-start | bytes 24584 | tf_op jit(solution)/shard_map/ppermute | solution.py:26
  153.4 4.5 %collective-permute-start.27 = (bf16[256,128]{1,0:T(8,128)(2,1)}, bf16[256,128]{1,0:T(8,128)(2,1)S(1)}, u32[]{:S(2)}, u32[]{:S(2)}) collective-permute-start(bf16[256,128]{1,0:T(8,128)(2,1)} %copy-done.28), channel_id=1, source_target_pairs={{0,3},{1,0},{2,1},{3,2},{4,7},{5,4},{6,5},{7,6},{8,11},{9,8},{10,9... | collective-permute-start | bytes 196616 | tf_op jit(solution)/shard_map/ppermute | solution.py:26
  154.3 6.8 %collective-permute-start.26 = (bf16[256,128]{1,0:T(8,128)(2,1)}, bf16[256,128]{1,0:T(8,128)(2,1)S(1)}, u32[]{:S(2)}, u32[]{:S(2)}) collective-permute-start(bf16[256,128]{1,0:T(8,128)(2,1)} %copy-done.27), channel_id=1, source_target_pairs={{0,2},{1,3},{2,0},{3,1},{4,6},{5,7},{6,4},{7,5},{8,10},{9,11},{10,... | collective-permute-start | bytes 196616 | tf_op jit(solution)/shard_map/ppermute | solution.py:26
  154.4 6.7 %collective-permute-start.25 = (bf16[256,128]{1,0:T(8,128)(2,1)}, bf16[256,128]{1,0:T(8,128)(2,1)S(1)}, u32[]{:S(2)}, u32[]{:S(2)}) collective-permute-start(bf16[256,128]{1,0:T(8,128)(2,1)} %copy-done.26), channel_id=1, source_target_pairs={{0,1},{1,2},{2,3},{3,0},{4,5},{5,6},{6,7},{7,4},{8,9},{9,10},{10,1... | collective-permute-start | bytes 196616 | tf_op jit(solution)/shard_map/ppermute | solution.py:26
  161.1 20.1 %copy-start.29 = (bf16[256,128]{1,0:T(8,128)(2,1)}, bf16[256,128]{1,0:T(8,128)(2,1)S(1)}, u32[]{:S(2)}) copy-start(bf16[256,128]{1,0:T(8,128)(2,1)S(1)} %collective-permute-done.26) | copy-start | bytes 196612
  181.2 74.8 %all-gather.19.cloned.1.call-start = ((), (), s32[]{:S(2)}) async-start(), calls=%async_computation.4 | async-start | bytes 3981312 | tf_op jit(solution)/shard_map/all_gather | solution.py:536
  181.3 16.5 %copy-start.30 = (bf16[256,128]{1,0:T(8,128)(2,1)S(1)}, bf16[256,128]{1,0:T(8,128)(2,1)}, u32[]{:S(2)}) copy-start(bf16[256,128]{1,0:T(8,128)(2,1)} %copy-done.29) | copy-start | bytes 196612
  181.3 16.5 %copy-start.32 = (bf16[256,128]{1,0:T(8,128)(2,1)S(1)}, bf16[256,128]{1,0:T(8,128)(2,1)}, u32[]{:S(2)}) copy-start(bf16[256,128]{1,0:T(8,128)(2,1)} %copy-done.31) | copy-start | bytes 196612
  188.9 4.4 %collective-permute-start.30 = (bf16[256,128]{1,0:T(8,128)(2,1)S(1)}, bf16[256,128]{1,0:T(8,128)(2,1)S(1)}, u32[]{:S(2)}, u32[]{:S(2)}) collective-permute-start(bf16[256,128]{1,0:T(8,128)(2,1)S(1)} %get-tuple-element.40), channel_id=1, source_target_pairs={{0,3},{1,0},{2,1},{3,2},{4,7},{5,4},{6,5},{7,6},{8,11},{9,8},{10,9... | collective-permute-start | bytes 196616 | tf_op jit(solution)/shard_map/ppermute | solution.py:26
  190.0 7.8 %collective-permute-start.29 = (bf16[256,128]{1,0:T(8,128)(2,1)S(1)}, bf16[256,128]{1,0:T(8,128)(2,1)S(1)}, u32[]{:S(2)}, u32[]{:S(2)}) collective-permute-start(bf16[256,128]{1,0:T(8,128)(2,1)S(1)} %get-tuple-element.39), channel_id=1, source_target_pairs={{0,2},{1,3},{2,0},{3,1},{4,6},{5,7},{6,4},{7,5},{8,10},{9,11},{10,... | collective-permute-start | bytes 196616 | tf_op jit(solution)/shard_map/ppermute | solution.py:26
  190.1 7.8 %collective-permute-start.28 = (bf16[256,128]{1,0:T(8,128)(2,1)S(1)}, bf16[256,128]{1,0:T(8,128)(2,1)S(1)}, u32[]{:S(2)}, u32[]{:S(2)}) collective-permute-start(bf16[256,128]{1,0:T(8,128)(2,1)S(1)} %get-tuple-element.38), channel_id=1, source_target_pairs={{0,1},{1,2},{2,3},{3,0},{4,5},{5,6},{6,7},{7,4},{8,9},{9,10},{10,1... | collective-permute-start | bytes 196616 | tf_op jit(solution)/shard_map/ppermute | solution.py:26
  218.4 19.1 %copy-start.33 = (f32[64,512]{1,0:T(8,128)S(1)}, f32[64,512]{1,0:T(8,128)}, u32[]{:S(2)}) copy-start(f32[64,512]{1,0:T(8,128)} %param.15) | copy-start | bytes 393220
  218.4 19.1 %copy-start.34 = (f32[64,512]{1,0:T(8,128)S(1)}, f32[64,512]{1,0:T(8,128)}, u32[]{:S(2)}) copy-start(f32[64,512]{1,0:T(8,128)} %param.16) | copy-start | bytes 393220
  219.6 17.9 %all-to-all-start = ((bf16[8,64,512]{2,1,0:T(8,128)(2,1)}), bf16[8,64,512]{2,1,0:T(8,128)(2,1)S(1)}, u32[]{:S(2)}, u32[]{:S(2)}) async-start(bf16[8,64,512]{2,1,0:T(8,128)(2,1)} %bitcast.24), calls=%async_computation | async-start | bytes 1048576 | tf_op jit(solution)/shard_map/all_to_all | solution.py:519
  (25 other events, 42.6 us)
Sparse Core Ops, SparseCore 0:
  10.1 30.6 all-gather.12
  76.9 30.4 all-gather.16
  109.3 28.8 all-gather.14
  181.3 33.4 all-gather.20
  218.6 36.4 all-gather.18

commit v2 on v1

v2 whole, which is shorter than its diff:
```python
import jax
import jax.numpy as jnp
from jax import lax
from jax.experimental import pallas as pl
from jax.experimental.pallas import tpu as pltpu
from jax.sharding import PartitionSpec as P

PATCH = 8
FLOW_STEPS = 2
OUT = 2048
SPLIT = ("grp", "sp")


time_step = 0.1
viscosity = 0.2
beta_one = 0.9
beta_two = 0.95
learn_rate = 0.001
adam_eps = 1e-08
bias_one = 0.9999734386011124
bias_two = 0.994079470779666


def shift(block, axis, by):
    count = lax.axis_size(axis)
    return lax.ppermute(block, axis, [(i, (i + by) % count) for i in range(count)])


def with_halo(block, sides, width, hold):
    for axis, dim in sides:
        low = lax.slice_in_dim(block, block.shape[dim] - width, None, axis=dim)
        high = lax.slice_in_dim(block, 0, width, axis=dim)
        low, high, hold = lax.optimization_barrier((low, high, hold))
        low, high = shift(low, axis, 1), shift(high, axis, -1)
        block = jnp.concatenate([low, block, high], axis=dim)
    return block


def advance(padded):
    center = padded[:, 1:-1, 1:-1]
    east = padded[:, 2:, 1:-1]
    west = padded[:, :-2, 1:-1]
    north = padded[:, 1:-1, 2:]
    south = padded[:, 1:-1, :-2]
    upper = jnp.roll(center, -1, 3)
    lower = jnp.roll(center, 1, 3)
    laplace = east + west + north + south + upper + lower - 6.0 * center
    carried = (
        center[0:1] * (east - west) * 0.5
        + center[1:2] * (north - south) * 0.5
        + center[2:3] * (upper - lower) * 0.5
    )
    return center + time_step * (viscosity * laplace - carried)


def rotations(block, axis):
    return [block] + [shift(block, axis, by) for by in range(1, lax.axis_size(axis))]


def scattered(pieces_of, axis):
    count, own = lax.axis_size(axis), lax.axis_index(axis)
    parts = [pieces_of(own)]
    for by in range(1, count):
        parts.append(shift(pieces_of((own + by) % count), axis, by))
    return parts


BIG = pltpu.CompilerParams(vmem_limit_bytes=48 * 1024 * 1024)
FULL = pltpu.CompilerParams(vmem_limit_bytes=60 * 1024 * 1024)
FLOAT = jnp.float32
HALF = jnp.bfloat16


def like(shape, dtype):
    return jax.ShapeDtypeStruct(shape, dtype)


def whole_spec(shape):
    return pl.BlockSpec(shape, lambda *_: (0,) * len(shape))


def turn(block, by, groups):
    rows = block.shape[0] // groups
    cube = block.astype(FLOAT).reshape(groups, rows, block.shape[1])
    return pltpu.roll(cube, by % rows, 1).reshape(block.shape)


def to_patches(field):
    fields, depth, span, length = field.shape
    high, long = span // PATCH, length // PATCH
    flat = PATCH * PATCH
    cells = flat * PATCH

    def kernel(field_ref, out_ref):
        row = lax.broadcasted_iota(jnp.int32, (length, length), 0)
        col = lax.broadcasted_iota(jnp.int32, (length, length), 1)
        pick = (col == (row % long) * PATCH + row // long).astype(HALF)
        row = lax.broadcasted_iota(jnp.int32, (flat, cells), 0)
        col = lax.broadcasted_iota(jnp.int32, (flat, cells), 1)
        inside, deep = row == col // PATCH, col % PATCH
        grids = []
        for part in range(high):
            for index in range(fields):
                brick = field_ref[index, :, part * PATCH : (part + 1) * PATCH, :]
                brick = brick.reshape(flat, length).astype(HALF)
                grids.append(
                    lax.dot_general(
                        pick, brick, (((1,), (1,)), ((), ())), preferred_element_type=FLOAT
                    ).astype(HALF)
                )
        total = jnp.zeros((high * fields * long, cells), FLOAT)
        for step in range(PATCH):
            rows = jnp.concatenate(
                [grid[step * long : (step + 1) * long] for grid in grids], axis=0
            )
            place = (inside & (deep == step)).astype(HALF)
            total = total + jnp.dot(rows, place, preferred_element_type=FLOAT)
        for part in range(high):
            for index in range(fields):
                at = (part * fields + index) * long
                out_ref[
                    part * long : (part + 1) * long, index * cells : (index + 1) * cells
                ] = total[at : at + long].astype(HALF)

    return pl.pallas_call(
        kernel, out_shape=like((high * long, fields * cells), HALF), compiler_params=BIG
    )(field)


def axis_word(axis):
    return lax.axis_index(axis).astype(jnp.int32).reshape(1)


def after(value, *others):
    return lax.optimization_barrier((value, others))[0]


def ring_pieces(block, axis):
    count, rows = lax.axis_size(axis), block.shape[0]
    pieces, up, down = [(0, 0, block)], block, block
    for by in range(1, (count + 1) // 2):
        up, down = shift(up, axis, 1), shift(down, axis, -1)
        pieces += [(by, 0, up), (count - by, 0, down)]
    if count % 2 == 0:
        half = rows // 2
        pieces.append((count // 2, 0, shift(up[:half], axis, 1)))
        pieces.append((count // 2, half, shift(down[half:], axis, -1)))
    return pieces


def embed(pieces, rows, weight):
    count, cols = lax.axis_size("ch"), weight.shape[1]
    marks = [(by, first, piece.shape[0]) for by, first, piece in pieces]

    def kernel(own_ref, *refs):
        weight_ref, out_ref = refs[-2:]
        for (by, first, long), piece_ref in zip(marks, refs):
            at = lax.rem(own_ref[0] - by + count, count) * rows + first
            out_ref[pl.ds(pl.multiple_of(at, long), long), :] = jnp.dot(
                piece_ref[...], weight_ref[...], preferred_element_type=FLOAT
            ).astype(HALF)

    arrays = [piece for _, _, piece in pieces] + [weight]
    return pl.pallas_call(
        kernel,
        grid=(1,),
        out_shape=like((count * rows, cols), HALF),
        in_specs=[pl.BlockSpec(memory_space=pltpu.SMEM)] + [whole_spec(a.shape) for a in arrays],
        out_specs=whole_spec((count * rows, cols)),
        compiler_params=BIG,
    )(axis_word("ch"), *arrays)


def fetch(taps_ref, layer, held, sems, pairs):
    copies = {}
    for slot, pair in enumerate(pairs):
        copies[pair] = pltpu.make_async_copy(
            taps_ref.at[layer, pl.ds(3 * pair, 3)], held.at[slot], sems.at[slot]
        )
        copies[pair].start()
    return copies


def conv_planes(sources, kernels, layer, rows_y, rows_z, planes, tail):
    count, rows, cols = sources[0].shape
    width = count * cols
    pairs = [3 * plane + down for plane in planes for down in range(3)]

    def kernel(own_ref, *refs):
        source_refs, taps_ref = refs[: len(planes)], refs[len(planes)]
        grids, held, sems = refs[-3:]
        copies = fetch(taps_ref, layer, held, sems, pairs)
        for plane, source in enumerate(source_refs):
            for by in range(count):
                place = lax.rem(own_ref[0] - by + count, count)
                at = pl.ds(pl.multiple_of(place * cols, cols), cols)
                grids[plane, rows_z : rows_z + rows, at] = source[by]
                grids[plane, :rows_z, at] = source[by, rows - rows_z :]
                grids[plane, rows_z + rows :, at] = source[by, :rows_z]
        total = None
        for slot, pair in enumerate(pairs):
            copies[pair].wait()
            left = grids[slot // 3, pl.ds((slot % 3) * rows_z, rows), :]
            right = jnp.concatenate([held[slot, index] for index in range(3)], axis=1)
            part = jnp.dot(left, right, preferred_element_type=FLOAT)
            total = part if total is None else total + part
        if not tail:
            refs[-4][...] = total
            return
        act_ref, other_ref, pre_ref, out_ref = refs[len(planes) + 1 : len(planes) + 5]
        total = total + other_ref[...]
        pre = (
            turn(total[:, :cols], 1, rows_y)
            + total[:, cols : 2 * cols]
            + turn(total[:, 2 * cols :], -1, rows_y)
        )
        pre_ref[...] = pre
        out_ref[...] = (act_ref[...].astype(FLOAT) + pre / (1.0 + jnp.exp(-pre))).astype(HALF)

    outs = [like((rows, 3 * cols), FLOAT)]
    if tail:
        outs = [like((rows, cols), FLOAT), like((rows, cols), HALF)]
    return pl.pallas_call(
        kernel,
        grid=(1,),
        out_shape=outs,
        in_specs=[pl.BlockSpec(memory_space=pltpu.SMEM)]
        + [whole_spec(source.shape) for source in sources]
        + [pl.BlockSpec(memory_space=pl.ANY)]
        + [whole_spec(array.shape) for array in tail],
        out_specs=[whole_spec(out.shape) for out in outs],
        scratch_shapes=[
            pltpu.VMEM((len(planes), rows + 2 * rows_z, width), HALF),
            pltpu.VMEM((len(pairs), 3, width, cols), HALF),
            pltpu.SemaphoreType.DMA((len(pairs),)),
        ],
        compiler_params=BIG,
    )(axis_word("ch"), *sources, kernels, *tail)


def conv_layer(act, kernels, layer, rows_y, rows_z, hold):
    near = jnp.stack(rotations(act, "ch"))
    below, above = shift(near, SPLIT, 1), shift(near, SPLIT, -1)
    (middle,) = conv_planes((near,), kernels, layer, rows_y, rows_z, (1,), ())
    below = after(below, middle, *hold)
    pre, out = conv_planes(
        (below, above), kernels, layer, rows_y, rows_z, (0, 2), (act, middle)
    )
    return (pre, out, near)


def split_up(value):
    high = value.astype(HALF)
    rest = value - high.astype(FLOAT)
    middle = rest.astype(HALF)
    return [high, middle, (rest - middle.astype(FLOAT)).astype(HALF)]


def give(own_ref, total, cols, count, first_ref, piece_refs):
    for by in range(count):
        place = lax.rem(own_ref[0] + by, count)
        part = total[:, pl.ds(pl.multiple_of(place * cols, cols), cols)]
        if by == 0:
            first_ref[...] = part
        else:
            piece_refs[by - 1][: part.shape[0]] = part.astype(HALF)


def conv_back(errors, kernels, layer, rows_y, rows_z, count):
    planes, _, cols = errors.shape
    rows, width = rows_y * rows_z, count * cols
    pairs = list(range(9))

    def kernel(own_ref, *refs):
        error_refs, taps_ref, first_ref = refs[:3], refs[3], refs[4]
        piece_refs, sides, held, sems, total = refs[5 : 4 + count], *refs[4 + count :]
        copies = fetch(taps_ref, layer, held, sems, pairs)
        for plane in range(3):
            source = error_refs[plane][0]
            wide = jnp.concatenate(
                [
                    turn(source, -1, rows_y).astype(HALF),
                    source,
                    turn(source, 1, rows_y).astype(HALF),
                ],
                axis=1,
            )
            sides[plane, rows_z : rows_z + rows] = wide
            sides[plane, :rows_z] = wide[rows - rows_z :]
            sides[plane, rows_z + rows :] = wide[:rows_z]
        value = None
        for pair in pairs:
            copies[pair].wait()
            left = sides[pair // 3, pl.ds((2 - pair % 3) * rows_z, rows), :]
            right = jnp.concatenate([held[pair, index] for index in range(3)], axis=1)
            part = lax.dot_general(
                left, right, (((1,), (1,)), ((), ())), preferred_element_type=FLOAT
            )
            value = part if value is None else value + part
        total[...] = value
        give(own_ref, total, cols, count, first_ref, piece_refs)

    def plane_spec(offset):
        return pl.BlockSpec(
            (1, rows, cols), lambda step, word: (lax.rem(word[1] + offset + planes, planes), 0, 0)
        )

    word = jnp.concatenate([axis_word("ch"), axis_word(SPLIT)])
    return pl.pallas_call(
        kernel,
        grid_spec=pltpu.PrefetchScalarGridSpec(
            num_scalar_prefetch=1,
            grid=(1,),
            in_specs=[
                plane_spec(1),
                plane_spec(0),
                plane_spec(-1),
                pl.BlockSpec(memory_space=pl.ANY),
            ],
            out_specs=[whole_spec((rows, cols))] * count,
            scratch_shapes=[
                pltpu.VMEM((3, rows + 2 * rows_z, 3 * cols), HALF),
                pltpu.VMEM((9, 3, width, cols), HALF),
                pltpu.SemaphoreType.DMA((9,)),
                pltpu.VMEM((rows, width), FLOAT),
            ],
        ),
        out_shape=[like((rows, cols), FLOAT)] + [like((rows, cols), HALF)] * (count - 1),
        compiler_params=BIG,
    )(word, errors, errors, errors, kernels)


def step_back(own, pieces, pre, extra):
    rows, cols = own.shape
    stats = extra.shape[0] != rows

    def kernel(own_ref, *refs):
        piece_refs, pre_ref, extra_ref = refs[: len(pieces)], refs[-4], refs[-3]
        error_ref, send_ref = refs[-2:]
        error = own_ref[...]
        for ref in piece_refs:
            error = error + ref[:rows].astype(FLOAT)
        if not stats:
            error = error + extra_ref[...]
        error_ref[...] = error
        send_ref[:rows] = (error * silu_slope(pre_ref[...])).astype(HALF)
        if stats:
            squares = extra_ref[:1]
            for ref in piece_refs:
                for term in range(3):
                    squares = squares + ref[rows + term : rows + term + 1].astype(FLOAT)
            marked = extra_ref[1:2]
            coarse = jnp.floor(marked / 128.0)
            terms = split_up(squares) + [coarse.astype(HALF), (marked - 128.0 * coarse).astype(HALF)]
            terms.append(jnp.zeros((11, cols), HALF))
            send_ref[rows:] = jnp.concatenate([term.astype(FLOAT) for term in terms]).astype(HALF)

    arrays = [own, *pieces, pre, extra]
    outs = [like((rows, cols), FLOAT), like((rows + 16 * stats, cols), HALF)]
    return pl.pallas_call(
        kernel,
        grid=(1,),
        in_specs=[whole_spec(array.shape) for array in arrays],
        out_specs=[whole_spec(out.shape) for out in outs],
        out_shape=outs,
        compiler_params=BIG,
    )(*arrays)


def predict(parts, changes, weight, mask, channels):
    count = len(parts)
    rows, cols = parts[0].shape
    short, block = changes[0].shape
    width = count * cols

    def kernel(own_ref, *refs):
        part_refs, change_refs = refs[:count], refs[count : 2 * count]
        weight_ref, mask_ref = refs[2 * count], refs[2 * count + 1]
        outs = refs[2 * count + 2 :]
        top_ref, error_ref, sums_ref, first_ref = outs[:4]
        piece_refs, held = outs[4 : 3 + count], outs[3 + count]
        for by in range(count):
            place = lax.rem(own_ref[0] - by + count, count)
            top_ref[:, pl.ds(pl.multiple_of(place * cols, cols), cols)] = part_refs[by][...]
            held[pl.ds(pl.multiple_of(place * short, short), short), :] = change_refs[by][...]
        pred = jnp.dot(top_ref[...], weight_ref[...], preferred_element_type=FLOAT)
        resid = held[...].astype(FLOAT) + pred
        mask = mask_ref[...]
        marked = mask * resid
        error = marked.astype(HALF)
        error_ref[...] = error
        squares = jnp.full((1, cols), jnp.sum(marked * resid), FLOAT)
        marks = jnp.full((1, cols), jnp.sum(mask), FLOAT)
        sums_ref[...] = jnp.concatenate([squares, marks, jnp.zeros((6, cols), FLOAT)])
        terms = [term.astype(FLOAT) for term in split_up(squares)]
        terms = jnp.concatenate(terms + [jnp.zeros((13, cols), FLOAT)]).astype(HALF)
        for piece_ref in piece_refs:
            piece_ref[rows:] = terms
        total = refs[-1]
        total[...] = lax.dot_general(
            error, weight_ref[...], (((1,), (1,)), ((), ())), preferred_element_type=FLOAT
        )
        give(own_ref, total, cols, count, first_ref, piece_refs)

    arrays = [*parts, *changes, weight, mask]
    outs = [
        like((rows, width), HALF),
        like((rows, block), HALF),
        like((8, cols), FLOAT),
        like((rows, cols), FLOAT),
    ] + [like((rows + 16, cols), HALF)] * (count - 1)
    return pl.pallas_call(
        kernel,
        grid=(1,),
        in_specs=[pl.BlockSpec(memory_space=pltpu.SMEM)] + [whole_spec(a.shape) for a in arrays],
        out_specs=[whole_spec(out.shape) for out in outs],
        out_shape=outs,
        scratch_shapes=[pltpu.VMEM((rows, block), HALF), pltpu.VMEM((rows, width), FLOAT)],
        compiler_params=BIG,
    )(axis_word("ch"), *arrays)


def spread_slots(every, rows, rows_y, rows_z):
    planes, count, points, lane = every.shape
    each = lane // rows

    def kernel(word_ref, every_ref, slots, held, sem):
        read = pltpu.make_async_copy(every_ref.at[:, word_ref[1]], held, sem)
        read.start()
        offset = lax.rem(word_ref[0] * rows, lane)
        lanes = lax.broadcasted_iota(jnp.int32, (points, lane), 1)
        read.wait()

        def prepare(plane, carry):
            own = held[plane].astype(FLOAT)
            for slot in range(each):
                moved = pltpu.roll(own, lax.rem(slot * rows - offset + lane, lane), 1)
                inside = (lanes >= slot * rows) & (lanes < (slot + 1) * rows)
                moved = jnp.where(inside, moved, 0.0).astype(HALF)
                slots[slot, plane, rows_z : rows_z + points] = moved
                slots[slot, plane, :rows_z] = moved[points - rows_z :]
                slots[slot, plane, rows_z + points :] = moved[:rows_z]
            return carry

        lax.fori_loop(0, planes, prepare, 0)

    shape = (each, planes, points + 2 * rows_z, lane)
    place = axis_word(SPLIT)
    word = jnp.concatenate([place, (axis_word("ch") - place * rows // lane + count) % count])
    return pl.pallas_call(
        kernel,
        grid=(1,),
        in_specs=[pl.BlockSpec(memory_space=pltpu.SMEM), pl.BlockSpec(memory_space=pltpu.HBM)],
        out_specs=whole_spec(shape),
        out_shape=like(shape, HALF),
        scratch_shapes=[pltpu.VMEM((planes, points, lane), HALF), pltpu.SemaphoreType.DMA],
        compiler_params=FULL,
    )(word, every)


def kernel_step(slots, errors, counted, states, layer, kept, dec, rows_y, rows_z):
    each, planes, _, lane = slots.shape
    points, cols = rows_y * rows_z, errors.shape[2]
    rows = states[1].shape[2]
    blocks = -(-9 // each)
    solo = 2 * bool(dec)
    more = dec[1].shape[1] // cols if dec else 0
    chunk = 9

    def kernel(word_ref, slots_ref, errors_ref, counted_ref, w_hbm, m_hbm, v_hbm, *refs):
        dec_refs = refs[: len(dec)]
        refs = refs[len(dec) + len(kept) :]
        new_w, m_out, v_out, loss_ref, *dec_outs = refs[: 4 + solo]
        w_ref, m_ref, v_ref, new_m, new_v, total, sems, out_sems = refs[4 + solo :]
        reads = [
            pltpu.make_async_copy(
                w_hbm.at[layer, :, pl.ds(pl.multiple_of(word_ref[0] * rows, rows), rows)],
                w_ref,
                sems.at[0],
            ),
            pltpu.make_async_copy(m_hbm.at[layer], m_ref, sems.at[1]),
            pltpu.make_async_copy(v_hbm.at[layer], v_ref, sems.at[2]),
        ]
        for read in reads:
            read.start()
        total[...] = jnp.zeros_like(total)

        def gather(plane, carry):
            left = []
            for block in range(blocks):
                value = None
                for slot in range(each):
                    pair = block * each + slot
                    if pair < 9:
                        source = lax.rem(plane + pair // 3 - 1 + planes, planes)
                        part = slots_ref[slot, source, pl.ds((pair % 3) * rows_z, points), :]
                        value = part if value is None else value + part
                left.append(value)
            left = jnp.concatenate(left, axis=1)
            error = errors_ref[plane, :points]
            right = jnp.concatenate(
                [
                    turn(error, -1, rows_y).astype(HALF),
                    error,
                    turn(error, 1, rows_y).astype(HALF),
                ],
                axis=1,
            )
            total[...] += lax.dot_general(
                left, right, (((0,), (0,)), ((), ())), preferred_element_type=FLOAT
            )
            return carry

        lax.fori_loop(0, planes, gather, 0)
        stats = jnp.sum(counted_ref[...].astype(FLOAT), axis=0)
        denom = jnp.maximum(128.0 * stats[3:4, :1] + stats[4:5, :1], 1.0) * OUT
        scale = 2.0 / denom
        squares = (stats[0:1, :1] + stats[1:2, :1]) + stats[2:3, :1]
        loss_ref[...] = jnp.broadcast_to(squares / denom, (8, 128))
        for read in reads:
            read.wait()
        writes = []
        for tap in range(27):
            at = (tap // 3) * rows
            grad = total[at : at + rows, (tap % 3) * cols : (tap % 3 + 1) * cols] * scale
            weight_next, moment_next, second_next = adam(w_ref[tap], m_ref[tap], v_ref[tap], grad)
            new_w[tap] = weight_next
            new_m[tap] = moment_next
            new_v[tap] = second_next
            if tap % chunk == chunk - 1:
                part = pl.ds(tap + 1 - chunk, chunk)
                for source, out, side in ((new_m, m_out, 0), (new_v, v_out, 1)):
                    writes.append(
                        pltpu.make_async_copy(
                            source.at[part],
                            out.at[layer, part],
                            out_sems.at[2 * (tap // chunk) + side],
                        )
                    )
                    writes[-1].start()
        if dec:
            grad_ref, dec_w_ref, dec_m_ref, dec_v_ref = dec_refs
            weight_next, moment_next, second_next = adam(
                dec_w_ref[...], dec_m_ref[...], dec_v_ref[...], grad_ref[...] * scale
            )
            dec_outs[0][...] = moment_next
            dec_outs[1][...] = second_next
            for index in range(more):
                new_w[27 + index] = weight_next[:, index * cols : (index + 1) * cols]
        for write in writes:
            write.wait()

    any_spec = pl.BlockSpec(memory_space=pl.ANY)
    hbm_spec = pl.BlockSpec(memory_space=pltpu.HBM)
    dec_specs = []
    if dec:
        flat = whole_spec(dec[2].shape)
        dec_specs = [flat, pl.BlockSpec(dec[2].shape, lambda step, word: (word[0], 0)), flat, flat]
    outs = [
        like((27 + more, rows, cols), HALF),
        like(states[1].shape, FLOAT),
        like(states[2].shape, FLOAT),
        like((8, 128), FLOAT),
    ] + [like(array.shape, FLOAT) for array in dec[2:]]
    first = 7 + len(dec)
    return pl.pallas_call(
        kernel,
        grid_spec=pltpu.PrefetchScalarGridSpec(
            num_scalar_prefetch=1,
            grid=(1,),
            in_specs=[
                whole_spec(slots.shape),
                whole_spec(errors.shape),
                pl.BlockSpec((planes, 16, cols), lambda step, word: (0, points // 16, 0)),
                hbm_spec,
                hbm_spec,
                hbm_spec,
            ]
            + dec_specs
            + [any_spec] * len(kept),
            out_specs=[
                whole_spec((27 + more, rows, cols)),
                any_spec,
                any_spec,
                whole_spec((8, 128)),
            ]
            + [whole_spec(array.shape) for array in dec[2:]],
            scratch_shapes=[
                pltpu.VMEM((27, rows, cols), HALF),
                pltpu.VMEM((27, rows, cols), FLOAT),
                pltpu.VMEM((27, rows, cols), FLOAT),
                pltpu.VMEM((27, rows, cols), FLOAT),
                pltpu.VMEM((27, rows, cols), FLOAT),
                pltpu.VMEM((blocks * lane, 3 * cols), FLOAT),
                pltpu.SemaphoreType.DMA((3,)),
                pltpu.SemaphoreType.DMA((2 * 27 // chunk,)),
            ],
        ),
        out_shape=outs,
        input_output_aliases={first: 1, first + 1: 2} if kept else {},
        compiler_params=BIG,
    )(axis_word(SPLIT), slots, errors, counted, *states, *dec, *kept)


def settle(gathered, shape, layer):
    count, taps, rows, cols = gathered.shape

    def kernel(from_ref, out_ref):
        out_ref[0] = from_ref[0]

    return pl.pallas_call(
        kernel,
        grid=(count,),
        in_specs=[pl.BlockSpec((1, taps, rows, cols), lambda step: (step, 0, 0, 0))],
        out_specs=pl.BlockSpec((1, taps, rows, cols), lambda step: (layer, 0, step, 0)),
        out_shape=like(shape, HALF),
        compiler_params=BIG,
    )(gathered)


def cross(block, mask):
    count = lax.axis_size(SPLIT)
    return lax.ppermute(block, SPLIT, [(i, i ^ mask) for i in range(count)])


def with_partner(pieces):
    return pieces + [(mask + 1, first, cross(piece, 1)) for mask, first, piece in pieces]


def cube_pieces(block, hold):
    count, long = lax.axis_size(SPLIT), block.shape[0]
    outer = [1 << bit for bit in range(1, (count - 1).bit_length())]
    pieces, last = [(0, 0, block)], []
    if len(outer) == 2:
        one, two = outer
        half = long // 2
        by_one, by_two = cross(block, one), cross(block, two)
        by_one, by_two, _ = lax.optimization_barrier((by_one, by_two, hold))
        pieces += [(one, 0, by_one), (two, 0, by_two)]
        last.append((one + two, 0, cross(by_two[:half], one)))
        last.append((one + two, half, cross(by_one[half:], two)))
    else:
        for bit in outer:
            pieces += [(mask + bit, first, cross(piece, bit)) for mask, first, piece in pieces]
    return pieces, last


def settle_pieces(pieces, layer, kept, dec_shape, dec_kept):
    marks = [(mask, first, piece.shape[0]) for mask, first, piece in pieces]
    count, taps = len(pieces), kept.shape[1]
    _, rows, cols = pieces[0][2].shape
    every = sum(1 + max(0, first + long - taps) for _, first, long in marks)

    def kernel(place_ref, *refs):
        out_ref, dec_ref, sems = refs[-3:]
        copies = []

        def copy(source, target):
            copies.append(pltpu.make_async_copy(source, target, sems.at[len(copies)]))
            copies[-1].start()

        for ref, (mask, first, long) in zip(refs, marks):
            at = pl.ds(pl.multiple_of((place_ref[0] ^ mask) * rows, rows), rows)
            own = min(long, taps - first)
            copy(ref.at[pl.ds(0, own)], out_ref.at[layer, pl.ds(first, own), at])
            for index in range(own, long):
                column = (first + index - taps) * cols
                copy(ref.at[index], dec_ref.at[at, pl.ds(column, cols)])
        for started in copies:
            started.wait()

    any_spec = pl.BlockSpec(memory_space=pl.ANY)
    return pl.pallas_call(
        kernel,
        grid=(1,),
        in_specs=[pl.BlockSpec(memory_space=pltpu.SMEM)]
        + [whole_spec(piece.shape) for _, _, piece in pieces]
        + [any_spec] * (1 + len(dec_kept)),
        out_specs=[any_spec, any_spec],
        out_shape=[like(kept.shape, HALF), like(dec_shape, HALF)],
        scratch_shapes=[pltpu.SemaphoreType.DMA((every,))],
        input_output_aliases={count + 1 + index: index for index in range(1 + len(dec_kept))},
        compiler_params=BIG,
    )(axis_word(SPLIT), *[piece for _, _, piece in pieces], kept, *dec_kept)


def halves(block, bit):
    pairs = block.reshape(block.shape[0] // 2, 2, *block.shape[1:])
    mine = (lax.axis_index(SPLIT) // bit) % 2
    keep = lax.dynamic_index_in_dim(pairs, mine, 1, keepdims=False)
    send = lax.dynamic_index_in_dim(pairs, 1 - mine, 1, keepdims=False)
    return keep, send.astype(HALF)


def halved(keep, send, holds):
    bit, turn_at = 1, 0
    while True:
        sent = after(cross(send, bit), holds[min(turn_at, len(holds) - 1)])
        block = keep.astype(FLOAT) + sent.astype(FLOAT)
        bit, turn_at = 2 * bit, turn_at + 1
        if bit == lax.axis_size(SPLIT):
            return block[0]
        keep, send = halves(block, bit)


def silu_slope(value):
    sig = jax.nn.sigmoid(value)
    return sig * (1.0 + value * (1.0 - sig))


def adam(weight, moment, second, grad):
    moment_next = beta_one * moment + (1.0 - beta_one) * grad
    second_next = beta_two * second + (1.0 - beta_two) * grad * grad
    weight_next = weight.astype(jnp.float32) - learn_rate * (moment_next / bias_one) / (
        jnp.sqrt(second_next / bias_two) + adam_eps
    )
    return (weight_next.astype(jnp.bfloat16), moment_next, second_next)


def body(flow, embed_w, conv_w, dec_w, conv_m, conv_v, dec_m, dec_v, loss_mask):
    rows_y = flow.shape[2] * lax.axis_size("ch") // PATCH
    rows_z = flow.shape[3] // PATCH
    width = conv_w.shape[2]
    channels = conv_w.shape[3]
    block = dec_w.shape[1]
    dec_rows = dec_m.shape[0]
    conv_rows = conv_m.shape[2]

    count = lax.axis_size("ch")
    patches = to_patches(flow)
    pieces = ring_pieces(patches, "ch")
    padded = with_halo(flow, ((SPLIT, 1), ("ch", 2)), FLOW_STEPS, patches)
    by, first, piece = pieces[-1]
    pieces[-1] = (by, first, after(piece, padded))
    embedded = embed(pieces, patches.shape[0], embed_w)

    state = padded
    for step in range(FLOW_STEPS):
        state = advance(state)
    change = to_patches(flow.astype(HALF).astype(FLOAT) - state)
    pre_one, act_one, near_one = conv_layer(embedded, conv_w, 0, rows_y, rows_z, (change,))
    changes = scattered(
        lambda k: lax.dynamic_slice_in_dim(change, k * block, block, 1), "ch"
    )
    rows_one = lax.all_gather(near_one, SPLIT, axis=0)
    pre_two, act_two, near_two = conv_layer(
        act_one, conv_w, 1, rows_y, rows_z, (rows_one, *changes)
    )
    rows_two = lax.all_gather(near_two, SPLIT, axis=0)

    mask = loss_mask.reshape(-1, 1).astype(FLOAT)
    slots_one = spread_slots(rows_one, conv_rows, rows_y, rows_z)
    parts = rotations(act_two, "ch")
    parts[-1] = after(parts[-1], slots_one)
    top, d_pred, sums, back, *pieces = predict(parts, changes, dec_w, mask, channels)

    def sent(pieces):
        return [shift(piece, "ch", by + 1) for by, piece in enumerate(pieces)]

    grad_dec = lax.dot_general(top, d_pred, (((0,), (0,)), ((), ())), preferred_element_type=FLOAT)
    keep, send = halves(grad_dec.astype(HALF).reshape(-1, dec_rows, block), 1)
    pieces = sent(pieces)
    pieces[-1] = after(pieces[-1], send)
    d_act_two, d_pre_two = step_back(back, pieces, pre_two, sums)
    slots_two = spread_slots(rows_two, conv_rows, rows_y, rows_z)
    errors_two = lax.all_gather(d_pre_two, SPLIT, axis=0)
    back, *pieces = conv_back(errors_two, conv_w, 1, rows_y, rows_z, count)
    _, d_pre_one = step_back(back, sent(pieces), pre_one, d_act_two)
    errors_one = lax.all_gather(d_pre_one, SPLIT, axis=0)

    grad_dec = halved(keep, send, (back, d_pre_one, errors_one))
    states = (conv_w, conv_m, conv_v)
    dec = (grad_dec, dec_w, dec_m, dec_v)
    two_shard, m_next, v_next, loss = kernel_step(
        slots_two, errors_two, errors_two, states, 1, (), (), rows_y, rows_z
    )
    one_shard, m_next, v_next, _, dec_m_next, dec_v_next = kernel_step(
        slots_one, errors_one, errors_two, states, 0, (m_next, v_next), dec, rows_y, rows_z
    )
    conv_next = settle(lax.all_gather(two_shard, SPLIT, axis=0), conv_w.shape, 1)
    pieces, last = cube_pieces(one_shard, conv_next)
    conv_next, dec_next = settle_pieces(with_partner(pieces), 0, conv_next, dec_w.shape, ())
    if last:
        last = [(mask, first, after(piece, conv_next)) for mask, first, piece in last]
        conv_next, dec_next = settle_pieces(
            with_partner(last), 0, conv_next, dec_w.shape, (dec_next,)
        )
    return (
        state,
        loss[0, 0],
        conv_next,
        dec_next,
        m_next,
        v_next,
        dec_m_next,
        dec_v_next,
    )


def solution(mesh):
    return jax.shard_map(
        body,
        mesh=mesh,
        in_specs=(
            P(None, ("grp", "sp"), "ch", None),
            P(None, "ch"),
            P(None, None, None, "ch"),
            P(None, "ch"),
            P(None, None, ("grp", "sp"), "ch"),
            P(None, None, ("grp", "sp"), "ch"),
            P(("grp", "sp"), "ch"),
            P(("grp", "sp"), "ch"),
            P(("grp", "sp"), None, None),
        ),
        out_specs=(
            P(None, ("grp", "sp"), "ch", None),
            P(),
            P(None, None, None, "ch"),
            P(None, "ch"),
            P(None, None, ("grp", "sp"), "ch"),
            P(None, None, ("grp", "sp"), "ch"),
            P(("grp", "sp"), "ch"),
            P(("grp", "sp"), "ch"),
        ),
        check_vma=False,
    )
```

time: 271 us -> 205 us (0.76)
  waiting for transfers between devices: 105 us -> 50.3 us
  starting transfers between devices: 35.8 us -> 52.6 us
  blocking collectives: 32.9 us -> 22.4 us
  local copies, waits for them, and re-layouts: 23.5 us -> 13.1 us
  Pallas kernels: 46.6 us -> 43.6 us
    all_gather x2 -> x0, waiting for transfers between devices: 30.8 us -> none  [the longest x1 30.8 us: body(): every_patch = lax.all_gather(patches, 'ch', axis=0)]
    ppermute x31 -> x30, waiting for transfers between devices: 60.6 us -> 38 us  [shift(): lax.ppermute(block, axis, [(i, (i + by) % count) for i in range(count)])]
    all_to_all x1 -> x0, waiting for transfers between devices: 13.8 us -> none  [body(): lax.all_to_all(grad_dec.astype(HALF).reshape(-1, dec_rows, block), SPLIT,...]
    ppermute x31 -> x30, starting transfers between devices: 32.1 us -> 45.4 us  [shift(): lax.ppermute(block, axis, [(i, (i + by) % count) for i in range(count)])]
    ppermute x0 -> x12, waiting for transfers between devices: none -> 12.2 us  [cross(): return lax.ppermute(block, SPLIT, [(i, i ^ mask) for i in range(count)])]
    unnamed x75 -> x36, local copies, waits for them, and re-layouts: 21 us -> 8.86 us
    all_gather x1 -> x0, blocking collectives: 11.5 us -> none  [body(): dec_next = lax.all_gather(dec_shard, SPLIT, axis=0, tiled=True)]
    pallas_call x3 -> x12, Pallas kernels: 15.3 us -> 22.4 us  [the longest x4 9.34 us: conv_planes(): pl.pallas_call(kernel, grid=(1,), out_shape=outs, in_specs=[pl.BlockSpec(...]
  transfers between devices with their start and end apart: 37 -> 45, of which waited for: 23 -> 25; matrix products, arithmetic and copies ran while one was open for 3% -> 6% of each run, Pallas kernels for 13% -> 15%
where the time goes in v2:
time: 205 us; the launch traced here: 204 us
  starting transfers between devices  52.6 us (26%)
  waiting for transfers between devices  50.3 us (25%)
  Pallas kernels  43.6 us (21%)
  blocking collectives  22.4 us (11%)
  between operations  14.3 us (7%)
  local copies, waits for them, and re-layouts  13.1 us (6%)
  other arithmetic  7.69 us (4%)
    ppermute x30, starting transfers between devices, shift(): lax.ppermute(block, axis, [(i, (i + by) % count) for i in range(count)])  45.4 us
    ppermute x30, waiting for transfers between devices, shift(): lax.ppermute(block, axis, [(i, (i + by) % count) for i in range(count)])  38 us
    ppermute x12, waiting for transfers between devices, cross(): return lax.ppermute(block, SPLIT, [(i, i ^ mask) for i in range(count)])  12.2 us
    all_gather x1, blocking collectives, body(): errors_one = lax.all_gather(d_pre_one, SPLIT, axis=0)  11.7 us
    pallas_call x2, Pallas kernels, kernel_step(): pl.pallas_call(kernel, grid_spec=pltpu.PrefetchScalarGridSpec(num_scalar_...  11.4 us
    all_gather x1, blocking collectives, body(): errors_two = lax.all_gather(d_pre_two, SPLIT, axis=0)  10.7 us
    pallas_call x4, Pallas kernels, conv_planes(): pl.pallas_call(kernel, grid=(1,), out_shape=outs, in_specs=[pl.BlockSpec(...  9.34 us
    unnamed x36, local copies, waits for them, and re-layouts  8.86 us
  transfers between devices with their start and end apart: 45, of which 25 were waited for; matrix products, arithmetic and copies ran while one was open for 6% of the time, Pallas kernels for 15%

profile of v2, /device:TPU:0, one launch (start us, length us, event | category | flops | bytes accessed | tf_op | source)
XLA Modules:
  0.0 204.2 jit_solution(3627483552827145588)
XLA Ops:
  9.8 4.7 %collective-permute-start.5 = (bf16[64,2048]{1,0:T(8,128)(2,1)S(1)}, bf16[64,2048]{1,0:T(8,128)(2,1)S(1)}, u32[]{:S(2)}, u32[]{:S(2)}) collective-permute-start(bf16[64,2048]{1,0:T(8,128)(2,1)S(1)} %shard_map.152.refs_0_), channel_id=1, source_target_pairs={{0,3},{1,0},{2,1},{3,2},{4,7},{5,4},{6,5},{7,6},{8,11},{9,8},{10,9... | collective-permute-start | bytes 786440 | tf_op jit(solution)/shard_map/ppermute | solution.py:26
  14.5 2.3 %collective-permute-start.1 = (f32[4,2,16,256]{3,2,1,0:T(8,128)S(1)}, f32[4,2,16,256]{3,2,1,0:T(8,128)S(1)}, u32[]{:S(2)}, u32[]{:S(2)}) collective-permute-start(f32[4,2,16,256]{3,2,1,0:T(8,128)S(1)} %get-tuple-element.56), channel_id=1, source_target_pairs={{0,28},{4,0},{8,4},{12,8},{16,12},{20,16},{24,20},{28,24},{1,29},{... | collective-permute-start | bytes 393224 | tf_op jit(solution)/shard_map/ppermute | solution.py:26
  16.8 2.4 %collective-permute-done.1 = f32[4,2,16,256]{3,2,1,0:T(8,128)S(1)} collective-permute-done((f32[4,2,16,256]{3,2,1,0:T(8,128)S(1)}, f32[4,2,16,256]{3,2,1,0:T(8,128)S(1)}, u32[]{:S(2)}, u32[]{:S(2)}) %collective-permute-start.1) | collective-permute-done | bytes 131104 | tf_op jit(solution)/shard_map/ppermute | solution.py:26
  19.4 3.8 %collective-permute-start.3 = (f32[4,12,2,256]{3,2,1,0:T(2,128)S(1)}, f32[4,12,2,256]{3,2,1,0:T(2,128)S(1)}, u32[]{:S(2)}, u32[]{:S(2)}) collective-permute-start(f32[4,12,2,256]{3,2,1,0:T(2,128)S(1)} %get-tuple-element.58), channel_id=1, source_target_pairs={{0,3},{1,0},{2,1},{3,2},{4,7},{5,4},{6,5},{7,6},{8,11},{9,8},{10,9... | collective-permute-start | bytes 294920 | tf_op jit(solution)/shard_map/ppermute | solution.py:26
  23.3 1.8 collective-permute-start.7
  25.1 2.2 %collective-permute-done.4.refs_1_ = bf16[64,2048]{1,0:T(8,128)(2,1)S(1)} collective-permute-done((bf16[64,2048]{1,0:T(8,128)(2,1)S(1)}, bf16[64,2048]{1,0:T(8,128)(2,1)S(1)}, u32[]{:S(2)}, u32[]{:S(2)}) %collective-permute-start.4) | collective-permute-done | bytes 262176 | tf_op jit(solution)/shard_map/ppermute | solution.py:26
  27.3 1.5 collective-permute-start.6
  29.4 2.5 %collective-permute-done.3 = f32[4,12,2,256]{3,2,1,0:T(2,128)S(1)} collective-permute-done((f32[4,12,2,256]{3,2,1,0:T(2,128)S(1)}, f32[4,12,2,256]{3,2,1,0:T(2,128)S(1)}, u32[]{:S(2)}, u32[]{:S(2)}) %collective-permute-start.3) | collective-permute-done | bytes 98336 | tf_op jit(solution)/shard_map/ppermute | solution.py:26
  32.1 3.1 %collective-permute-done.7.refs_4_ = bf16[32,2048]{1,0:T(8,128)(2,1)S(1)} collective-permute-done((bf16[32,2048]{1,0:T(8,128)(2,1)S(1)}, bf16[32,2048]{1,0:T(8,128)(2,1)S(1)}, u32[]{:S(2)}, u32[]{:S(2)}) %collective-permute-start.7) | collective-permute-done | bytes 131104 | tf_op jit(solution)/shard_map/ppermute | solution.py:26
  35.2 1.8 collective-permute-done.6.refs_3_
  37.5 2.5 %collective-permute-start.9 = (bf16[256,128]{1,0:T(8,128)(2,1)S(1)}, bf16[256,128]{1,0:T(8,128)(2,1)S(1)}, u32[]{:S(2)}, u32[]{:S(2)}) collective-permute-start(bf16[256,128]{1,0:T(8,128)(2,1)S(1)} %shard_map.153.refs_3_), channel_id=1, source_target_pairs={{0,2},{1,3},{2,0},{3,1},{4,6},{5,7},{6,4},{7,5},{8,10},{9,11},{10,... | collective-permute-start | bytes 196616 | tf_op jit(solution)/shard_map/ppermute | solution.py:26
  40.0 1.5 collective-permute-start.10
  42.0 2.5 %collective-permute-done.9 = bf16[256,128]{1,0:T(8,128)(2,1)S(1)} collective-permute-done((bf16[256,128]{1,0:T(8,128)(2,1)S(1)}, bf16[256,128]{1,0:T(8,128)(2,1)S(1)}, u32[]{:S(2)}, u32[]{:S(2)}) %collective-permute-start.9) | collective-permute-done | bytes 65568 | tf_op jit(solution)/shard_map/ppermute | solution.py:26
  44.6 3.0 %collective-permute-done.8 = bf16[256,128]{1,0:T(8,128)(2,1)S(1)} collective-permute-done((bf16[256,128]{1,0:T(8,128)(2,1)S(1)}, bf16[256,128]{1,0:T(8,128)(2,1)S(1)}, u32[]{:S(2)}, u32[]{:S(2)}) %collective-permute-start.8) | collective-permute-done | bytes 65568 | tf_op jit(solution)/shard_map/ppermute | solution.py:26
  51.1 2.6 %collective-permute-start.12 = (bf16[4,256,128]{2,1,0:T(8,128)(2,1)S(1)}, bf16[4,256,128]{2,1,0:T(8,128)(2,1)S(1)}, u32[]{:S(2)}, u32[]{:S(2)}) collective-permute-start(bf16[4,256,128]{2,1,0:T(8,128)(2,1)S(1)} %copy-done.7), channel_id=1, source_target_pairs={{0,28},{4,0},{8,4},{12,8},{16,12},{20,16},{24,20},{28,24},{1,29},{... | collective-permute-start | bytes 786440 | tf_op jit(solution)/shard_map/ppermute | solution.py:26
  56.1 1.9 shard_map.154.refs_4_
  59.2 2.3 %collective-permute-done.12.refs_1_ = bf16[4,256,128]{2,1,0:T(8,128)(2,1)S(1)} collective-permute-done((bf16[4,256,128]{2,1,0:T(8,128)(2,1)S(1)}, bf16[4,256,128]{2,1,0:T(8,128)(2,1)S(1)}, u32[]{:S(2)}, u32[]{:S(2)}) %collective-permute-start.12) | collective-permute-done | bytes 262176 | tf_op jit(solution)/shard_map/ppermute | solution.py:26
  61.5 2.8 %shard_map.156 = (f32[256,128]{1,0:T(8,128)S(1)}, bf16[256,128]{1,0:T(8,128)(2,1)S(1)}) custom-call(s32[1]{0:T(128)} %bitcast.7.own_ref, bf16[4,256,128]{2,1,0:T(8,128)(2,1)S(1)} %collective-permute-done.11.refs_0_, bf16[4,256,128]{2,1,0:T(8,128)(2,1)S(1)} %collective-permute-done.12.refs_1_, bf16[2,27,512,128]{3,2,1,0:T(8,128)(2,1)} %w_hbm.3, ...), custom_call_target="tpu_custom_call" | custom-call | tf_op jit(solution)/shard_map/pallas_call | solution.py:223
  64.4 2.3 %collective-permute-start.14 = (bf16[256,128]{1,0:T(8,128)(2,1)S(1)}, bf16[256,128]{1,0:T(8,128)(2,1)S(1)}, u32[]{:S(2)}, u32[]{:S(2)}) collective-permute-start(bf16[256,128]{1,0:T(8,128)(2,1)S(1)} %get-tuple-element.61.refs_3_), channel_id=1, source_target_pairs={{0,2},{1,3},{2,0},{3,1},{4,6},{5,7},{6,4},{7,5},{8,10},{9,11},{10,... | collective-permute-start | bytes 196616 | tf_op jit(solution)/shard_map/ppermute | solution.py:26
  66.7 2.8 %collective-permute-start.15 = (bf16[256,128]{1,0:T(8,128)(2,1)S(1)}, bf16[256,128]{1,0:T(8,128)(2,1)S(1)}, u32[]{:S(2)}, u32[]{:S(2)}) collective-permute-start(bf16[256,128]{1,0:T(8,128)(2,1)S(1)} %get-tuple-element.61.refs_3_), channel_id=1, source_target_pairs={{0,3},{1,0},{2,1},{3,2},{4,7},{5,4},{6,5},{7,6},{8,11},{9,8},{10,9... | collective-permute-start | bytes 196616 | tf_op jit(solution)/shard_map/ppermute | solution.py:26
  70.5 2.1 %collective-permute-done.15 = bf16[256,128]{1,0:T(8,128)(2,1)S(1)} collective-permute-done((bf16[256,128]{1,0:T(8,128)(2,1)S(1)}, bf16[256,128]{1,0:T(8,128)(2,1)S(1)}, u32[]{:S(2)}, u32[]{:S(2)}) %collective-permute-start.15) | collective-permute-done | bytes 65568 | tf_op jit(solution)/shard_map/ppermute | solution.py:26
  74.5 1.6 collective-permute-start.20
  76.1 2.0 collective-permute-start.17
  78.2 2.3 %collective-permute-start.18 = (bf16[64,512]{1,0:T(8,128)(2,1)S(1)}, bf16[64,512]{1,0:T(8,128)(2,1)S(1)}, u32[]{:S(2)}, u32[]{:S(2)}) collective-permute-start(bf16[64,512]{1,0:T(8,128)(2,1)S(1)} %get-tuple-element.123), channel_id=1, source_target_pairs={{0,2},{1,3},{2,0},{3,1},{4,6},{5,7},{6,4},{7,5},{8,10},{9,11},{10,... | collective-permute-start | bytes 196616 | tf_op jit(solution)/shard_map/ppermute | solution.py:26
  82.0 1.9 shard_map.158.refs_4_
  85.1 2.8 %shard_map.159 = (f32[256,128]{1,0:T(8,128)S(1)}, bf16[256,128]{1,0:T(8,128)(2,1)S(1)}) custom-call(s32[1]{0:T(128)} %bitcast.7.own_ref, bf16[4,256,128]{2,1,0:T(8,128)(2,1)S(1)} %collective-permute-done.16.refs_0_, bf16[4,256,128]{2,1,0:T(8,128)(2,1)S(1)} %collective-permute-done.20.refs_1_, bf16[2,27,512,128]{3,2,1,0:T(8,128)(2,1)} %w_hbm.3, ...), custom_call_target="tpu_custom_call" | custom-call | tf_op jit(solution)/shard_map/pallas_call | solution.py:223
  88.0 2.2 %collective-permute-start.23 = (bf16[256,128]{1,0:T(8,128)(2,1)S(1)}, bf16[256,128]{1,0:T(8,128)(2,1)S(1)}, u32[]{:S(2)}, u32[]{:S(2)}) collective-permute-start(bf16[256,128]{1,0:T(8,128)(2,1)S(1)} %get-tuple-element.63.refs_0_), channel_id=1, source_target_pairs={{0,3},{1,0},{2,1},{3,2},{4,7},{5,4},{6,5},{7,6},{8,11},{9,8},{10,9... | collective-permute-start | bytes 196616 | tf_op jit(solution)/shard_map/ppermute | solution.py:26
  91.5 3.6 %shard_map.160.slots_ref = bf16[2,8,320,128]{3,2,1,0:T(8,128)(2,1)} custom-call(s32[2]{0:T(128)} %pad_add_fusion.word_ref, bf16[8,4,256,128]{3,2,1,0:T(8,128)(2,1)} %bitcast.59), custom_call_target="tpu_custom_call" | custom-call | tf_op jit(solution)/shard_map/pallas_call | solution.py:450
  96.9 2.9 %collective-permute-start.26 = (bf16[272,128]{1,0:T(8,128)(2,1)S(1)}, bf16[272,128]{1,0:T(8,128)(2,1)S(1)}, u32[]{:S(2)}, u32[]{:S(2)}) collective-permute-start(bf16[272,128]{1,0:T(8,128)(2,1)S(1)} %get-tuple-element.68), channel_id=1, source_target_pairs={{0,3},{1,0},{2,1},{3,2},{4,7},{5,4},{6,5},{7,6},{8,11},{9,8},{10,9... | collective-permute-start | bytes 208904 | tf_op jit(solution)/shard_map/ppermute | solution.py:26
  101.9 4.2 %collective-permute-done.24.refs_0_ = bf16[272,128]{1,0:T(8,128)(2,1)S(1)} collective-permute-done((bf16[272,128]{1,0:T(8,128)(2,1)S(1)}, bf16[272,128]{1,0:T(8,128)(2,1)S(1)}, u32[]{:S(2)}, u32[]{:S(2)}) %collective-permute-start.24) | collective-permute-done | bytes 69664 | tf_op jit(solution)/shard_map/ppermute | solution.py:26
  107.3 10.7 %all-gather.2 = bf16[2176,128]{1,0:T(8,128)(2,1)S(1)} all-gather(bf16[272,128]{1,0:T(8,128)(2,1)S(1)} %get-tuple-element.74), channel_id=4, replica_groups=mesh['grp'=2,'sp'=4,'ch'=4] {'grp','sp'}, dimensions={0}, use_global_device_ids=true | all-gather | bytes 626688 | tf_op jit(solution)/shard_map/all_gather | solution.py:766
  118.0 3.7 %shard_map.157.slots_ref = bf16[2,8,320,128]{3,2,1,0:T(8,128)(2,1)} custom-call(s32[2]{0:T(128)} %pad_add_fusion.word_ref, bf16[8,4,256,128]{3,2,1,0:T(8,128)(2,1)} %bitcast.60), custom_call_target="tpu_custom_call" | custom-call | tf_op jit(solution)/shard_map/pallas_call | solution.py:450
  124.6 5.9 %shard_map.163 = (bf16[27,64,128]{2,1,0:T(8,128)(2,1)}, f32[2,27,64,128]{3,2,1,0:T(8,128)}, f32[2,27,64,128]{3,2,1,0:T(8,128)}, f32[8,128]{1,0:T(8,128)S(1)}) custom-call(s32[1]{0:T(128)} %bitcast.6.word_ref.place_ref, bf16[2,8,320,128]{3,2,1,0:T(8,128)(2,1)S(1)} %copy-done.5, bf16[8,272,128]{2,1,0:T(8,128)(2,1)S(1)} %bitcast.49, ...), custom_call_target="tpu_custom_call" | custom-call | tf_op jit(solution)/shard_map/pallas_call | solution.py:566
  131.6 4.5 %shard_map.164 = (f32[256,128]{1,0:T(8,128)S(1)}, bf16[256,128]{1,0:T(8,128)(2,1)}, bf16[256,128]{1,0:T(8,128)(2,1)}, bf16[256,128]{1,0:T(8,128)(2,1)}) custom-call(s32[2]{0:T(128)S(1)} %pad_add_fusion.1.own_ref, bf16[8,272,128]{2,1,0:T(8,128)(2,1)S(1)} %bitcast.51, bf16[8,272,128]{2,1,0:T(8,128)(2,1)S(1)} %bitcast.52, bf16[8,272,128]{2,1,0:T(8,128)(2,1)S(1)} %bitcast.53, ...), custom_call_target="tpu_custom_call" | custom-call | tf_op jit(solution)/shard_map/pallas_call | solution.py:309
  136.1 1.9 convert_add_fusion
  138.0 1.7 fusion
  139.8 2.7 %collective-permute-start.28 = (bf16[256,128]{1,0:T(8,128)(2,1)}, bf16[256,128]{1,0:T(8,128)(2,1)S(1)}, u32[]{:S(2)}, u32[]{:S(2)}) collective-permute-start(bf16[256,128]{1,0:T(8,128)(2,1)} %get-tuple-element.78), channel_id=1, source_target_pairs={{0,2},{1,3},{2,0},{3,1},{4,6},{5,7},{6,4},{7,5},{8,10},{9,11},{10,... | collective-permute-start | bytes 196616 | tf_op jit(solution)/shard_map/ppermute | solution.py:26
  143.6 3.2 %collective-permute-done.27.refs_0_ = bf16[256,128]{1,0:T(8,128)(2,1)S(1)} collective-permute-done((bf16[256,128]{1,0:T(8,128)(2,1)}, bf16[256,128]{1,0:T(8,128)(2,1)S(1)}, u32[]{:S(2)}, u32[]{:S(2)}) %collective-permute-start.27) | collective-permute-done | bytes 65568 | tf_op jit(solution)/shard_map/ppermute | solution.py:26
  146.7 1.8 collective-permute-done.28.refs_1_
  148.5 1.5 shard_map.165
  151.1 1.8 collective-permute-start.32
  152.9 11.7 %all-gather.3 = bf16[2048,128]{1,0:T(8,128)(2,1)S(1)} all-gather(bf16[256,128]{1,0:T(8,128)(2,1)S(1)} %get-tuple-element.82), channel_id=5, replica_groups=mesh['grp'=2,'sp'=4,'ch'=4] {'grp','sp'}, dimensions={0}, use_global_device_ids=true | all-gather | bytes 589824 | tf_op jit(solution)/shard_map/all_gather | solution.py:769
  165.6 5.6 %shard_map.166 = (bf16[31,64,128]{2,1,0:T(8,128)(2,1)S(1)}, f32[2,27,64,128]{3,2,1,0:T(8,128)}, f32[2,27,64,128]{3,2,1,0:T(8,128)}, f32[8,128]{1,0:T(8,128)}, f32[64,512]{1,0:T(8,128)}, /*index=5*/f32[64,512]{1,0:T(8,128)}) custom-call(s32[1]{0:T(128)} %bitcast.6.word_ref.place_ref, ...), custom_call_target="tpu_custom_call", output_to_operand_aliasing={{1}: (11, {}), {2}: (12, {})} | custom-call | tf_op jit(solution)/shard_map/pallas_call | solution.py:566
  173.3 2.0 copy-done.6
  175.3 3.3 %shard_map.167.refs_6_ = bf16[2,27,512,128]{3,2,1,0:T(8,128)(2,1)} custom-call(bf16[8,27,64,128]{3,2,1,0:T(8,128)(2,1)S(1)} %bitcast.55), custom_call_target="tpu_custom_call" | custom-call | tf_op jit(solution)/shard_map/pallas_call | solution.py:611
  178.6 6.5 %collective-permute-done.33.refs_1_ = bf16[31,64,128]{2,1,0:T(8,128)(2,1)S(1)} collective-permute-done((bf16[31,64,128]{2,1,0:T(8,128)(2,1)S(1)}, bf16[31,64,128]{2,1,0:T(8,128)(2,1)S(1)}, u32[]{:S(2)}, u32[]{:S(2)}) %collective-permute-start.33) | collective-permute-done | bytes 507936 | tf_op jit(solution)/shard_map/ppermute | solution.py:623
  188.5 1.9 shard_map.168
  190.4 4.2 %collective-permute-done.39.refs_1_ = bf16[16,64,128]{2,1,0:T(8,128)(2,1)S(1)} collective-permute-done((bf16[16,64,128]{2,1,0:T(8,128)(2,1)S(1)}, bf16[16,64,128]{2,1,0:T(8,128)(2,1)S(1)}, u32[]{:S(2)}, u32[]{:S(2)}) %collective-permute-start.39) | collective-permute-done | bytes 262176 | tf_op jit(solution)/shard_map/ppermute | solution.py:623
  (132 shorter events, 39.4 us)
Async XLA Ops:
  7.2 78.0 %all-gather.11.cloned.1.call-start = ((), (), s32[]{:S(2)}) async-start(), calls=%async_computation.1 | async-start | bytes 2359296 | tf_op jit(solution)/shard_map/all_gather | solution.py:745
  9.3 7.5 %collective-permute-start = (f32[4,2,16,256]{3,2,1,0:T(8,128)S(1)}, f32[4,2,16,256]{3,2,1,0:T(8,128)S(1)}, u32[]{:S(2)}, u32[]{:S(2)}) collective-permute-start(f32[4,2,16,256]{3,2,1,0:T(8,128)S(1)} %get-tuple-element.55), channel_id=1, source_target_pairs={{0,4},{4,8},{8,12},{12,16},{16,20},{20,24},{24,28},{28,0},{1,5},{5... | collective-permute-start | bytes 393224 | tf_op jit(solution)/shard_map/ppermute | solution.py:26
  9.8 13.5 %collective-permute-start.5 = (bf16[64,2048]{1,0:T(8,128)(2,1)S(1)}, bf16[64,2048]{1,0:T(8,128)(2,1)S(1)}, u32[]{:S(2)}, u32[]{:S(2)}) collective-permute-start(bf16[64,2048]{1,0:T(8,128)(2,1)S(1)} %shard_map.152.refs_0_), channel_id=1, source_target_pairs={{0,3},{1,0},{2,1},{3,2},{4,7},{5,4},{6,5},{7,6},{8,11},{9,8},{10,9... | collective-permute-start | bytes 786440 | tf_op jit(solution)/shard_map/ppermute | solution.py:26
  14.5 12.8 %collective-permute-start.4 = (bf16[64,2048]{1,0:T(8,128)(2,1)S(1)}, bf16[64,2048]{1,0:T(8,128)(2,1)S(1)}, u32[]{:S(2)}, u32[]{:S(2)}) collective-permute-start(bf16[64,2048]{1,0:T(8,128)(2,1)S(1)} %shard_map.152.refs_0_), channel_id=1, source_target_pairs={{0,1},{1,2},{2,3},{3,0},{4,5},{5,6},{6,7},{7,4},{8,9},{9,10},{10,1... | collective-permute-start | bytes 786440 | tf_op jit(solution)/shard_map/ppermute | solution.py:26
  14.5 4.8 %collective-permute-start.1 = (f32[4,2,16,256]{3,2,1,0:T(8,128)S(1)}, f32[4,2,16,256]{3,2,1,0:T(8,128)S(1)}, u32[]{:S(2)}, u32[]{:S(2)}) collective-permute-start(f32[4,2,16,256]{3,2,1,0:T(8,128)S(1)} %get-tuple-element.56), channel_id=1, source_target_pairs={{0,28},{4,0},{8,4},{12,8},{16,12},{20,16},{24,20},{28,24},{1,29},{... | collective-permute-start | bytes 393224 | tf_op jit(solution)/shard_map/ppermute | solution.py:26
  19.4 10.0 %collective-permute-start.2 = (f32[4,12,2,256]{3,2,1,0:T(2,128)S(1)}, f32[4,12,2,256]{3,2,1,0:T(2,128)S(1)}, u32[]{:S(2)}, u32[]{:S(2)}) collective-permute-start(f32[4,12,2,256]{3,2,1,0:T(2,128)S(1)} %get-tuple-element.57), channel_id=1, source_target_pairs={{0,1},{1,2},{2,3},{3,0},{4,5},{5,6},{6,7},{7,4},{8,9},{9,10},{10,1... | collective-permute-start | bytes 294920 | tf_op jit(solution)/shard_map/ppermute | solution.py:26
  19.4 12.5 %collective-permute-start.3 = (f32[4,12,2,256]{3,2,1,0:T(2,128)S(1)}, f32[4,12,2,256]{3,2,1,0:T(2,128)S(1)}, u32[]{:S(2)}, u32[]{:S(2)}) collective-permute-start(f32[4,12,2,256]{3,2,1,0:T(2,128)S(1)} %get-tuple-element.58), channel_id=1, source_target_pairs={{0,3},{1,0},{2,1},{3,2},{4,7},{5,4},{6,5},{7,6},{8,11},{9,8},{10,9... | collective-permute-start | bytes 294920 | tf_op jit(solution)/shard_map/ppermute | solution.py:26
  23.3 11.9 %collective-permute-start.7 = (bf16[32,2048]{1,0:T(8,128)(2,1)S(1)}, bf16[32,2048]{1,0:T(8,128)(2,1)S(1)}, u32[]{:S(2)}, u32[]{:S(2)}) collective-permute-start(bf16[32,2048]{1,0:T(8,128)(2,1)S(1)} %slice.181), channel_id=1, source_target_pairs={{0,3},{1,0},{2,1},{3,2},{4,7},{5,4},{6,5},{7,6},{8,11},{9,8},{10,9... | collective-permute-start | bytes 393224 | tf_op jit(solution)/shard_map/ppermute | solution.py:26
  27.3 9.8 %collective-permute-start.6 = (bf16[32,2048]{1,0:T(8,128)(2,1)S(1)}, bf16[32,2048]{1,0:T(8,128)(2,1)S(1)}, u32[]{:S(2)}, u32[]{:S(2)}) collective-permute-start(bf16[32,2048]{1,0:T(8,128)(2,1)S(1)} %slice.180), channel_id=1, source_target_pairs={{0,1},{1,2},{2,3},{3,0},{4,5},{5,6},{6,7},{7,4},{8,9},{9,10},{10,1... | collective-permute-start | bytes 393224 | tf_op jit(solution)/shard_map/ppermute | solution.py:26
  37.5 7.0 %collective-permute-start.9 = (bf16[256,128]{1,0:T(8,128)(2,1)S(1)}, bf16[256,128]{1,0:T(8,128)(2,1)S(1)}, u32[]{:S(2)}, u32[]{:S(2)}) collective-permute-start(bf16[256,128]{1,0:T(8,128)(2,1)S(1)} %shard_map.153.refs_3_), channel_id=1, source_target_pairs={{0,2},{1,3},{2,0},{3,1},{4,6},{5,7},{6,4},{7,5},{8,10},{9,11},{10,... | collective-permute-start | bytes 196616 | tf_op jit(solution)/shard_map/ppermute | solution.py:26
  40.0 4.6 %collective-permute-start.10 = (bf16[256,128]{1,0:T(8,128)(2,1)S(1)}, bf16[256,128]{1,0:T(8,128)(2,1)S(1)}, u32[]{:S(2)}, u32[]{:S(2)}) collective-permute-start(bf16[256,128]{1,0:T(8,128)(2,1)S(1)} %shard_map.153.refs_3_), channel_id=1, source_target_pairs={{0,3},{1,0},{2,1},{3,2},{4,7},{5,4},{6,5},{7,6},{8,11},{9,8},{10,9... | collective-permute-start | bytes 196616 | tf_op jit(solution)/shard_map/ppermute | solution.py:26
  41.6 6.1 %collective-permute-start.8 = (bf16[256,128]{1,0:T(8,128)(2,1)S(1)}, bf16[256,128]{1,0:T(8,128)(2,1)S(1)}, u32[]{:S(2)}, u32[]{:S(2)}) collective-permute-start(bf16[256,128]{1,0:T(8,128)(2,1)S(1)} %shard_map.153.refs_3_), channel_id=1, source_target_pairs={{0,1},{1,2},{2,3},{3,0},{4,5},{5,6},{6,7},{7,4},{8,9},{9,10},{10,1... | collective-permute-start | bytes 196616 | tf_op jit(solution)/shard_map/ppermute | solution.py:26
  48.4 69.7 %all-gather.9.cloned.1.call-start = ((), (), s32[]{:S(2)}) async-start(), calls=%async_computation | async-start | bytes 2359296 | tf_op jit(solution)/shard_map/all_gather | solution.py:749
  51.1 8.1 %collective-permute-start.11 = (bf16[4,256,128]{2,1,0:T(8,128)(2,1)S(1)}, bf16[4,256,128]{2,1,0:T(8,128)(2,1)S(1)}, u32[]{:S(2)}, u32[]{:S(2)}) collective-permute-start(bf16[4,256,128]{2,1,0:T(8,128)(2,1)S(1)} %copy-done.7), channel_id=1, source_target_pairs={{0,4},{4,8},{8,12},{12,16},{16,20},{20,24},{24,28},{28,0},{1,5},{5... | collective-permute-start | bytes 786440 | tf_op jit(solution)/shard_map/ppermute | solution.py:26
  51.1 10.4 %collective-permute-start.12 = (bf16[4,256,128]{2,1,0:T(8,128)(2,1)S(1)}, bf16[4,256,128]{2,1,0:T(8,128)(2,1)S(1)}, u32[]{:S(2)}, u32[]{:S(2)}) collective-permute-start(bf16[4,256,128]{2,1,0:T(8,128)(2,1)S(1)} %copy-done.7), channel_id=1, source_target_pairs={{0,28},{4,0},{8,4},{12,8},{16,12},{20,16},{24,20},{28,24},{1,29},{... | collective-permute-start | bytes 786440 | tf_op jit(solution)/shard_map/ppermute | solution.py:26
  58.0 23.0 %copy-start.16 = (s32[1,8,32]{2,1,0:T(8,128)S(1)}, s32[1,8,32]{2,1,0:T(8,128)}, u32[]{:S(2)}) copy-start(s32[1,8,32]{2,1,0:T(8,128)} %param.17) | copy-start | bytes 3076
  64.3 6.2 %collective-permute-start.13 = (bf16[256,128]{1,0:T(8,128)(2,1)S(1)}, bf16[256,128]{1,0:T(8,128)(2,1)S(1)}, u32[]{:S(2)}, u32[]{:S(2)}) collective-permute-start(bf16[256,128]{1,0:T(8,128)(2,1)S(1)} %get-tuple-element.61.refs_3_), channel_id=1, source_target_pairs={{0,1},{1,2},{2,3},{3,0},{4,5},{5,6},{6,7},{7,4},{8,9},{9,10},{10,1... | collective-permute-start | bytes 196616 | tf_op jit(solution)/shard_map/ppermute | solution.py:26
  64.4 6.2 %collective-permute-start.14 = (bf16[256,128]{1,0:T(8,128)(2,1)S(1)}, bf16[256,128]{1,0:T(8,128)(2,1)S(1)}, u32[]{:S(2)}, u32[]{:S(2)}) collective-permute-start(bf16[256,128]{1,0:T(8,128)(2,1)S(1)} %get-tuple-element.61.refs_3_), channel_id=1, source_target_pairs={{0,2},{1,3},{2,0},{3,1},{4,6},{5,7},{6,4},{7,5},{8,10},{9,11},{10,... | collective-permute-start | bytes 196616 | tf_op jit(solution)/shard_map/ppermute | solution.py:26
  66.7 6.0 %collective-permute-start.15 = (bf16[256,128]{1,0:T(8,128)(2,1)S(1)}, bf16[256,128]{1,0:T(8,128)(2,1)S(1)}, u32[]{:S(2)}, u32[]{:S(2)}) collective-permute-start(bf16[256,128]{1,0:T(8,128)(2,1)S(1)} %get-tuple-element.61.refs_3_), channel_id=1, source_target_pairs={{0,3},{1,0},{2,1},{3,2},{4,7},{5,4},{6,5},{7,6},{8,11},{9,8},{10,9... | collective-permute-start | bytes 196616 | tf_op jit(solution)/shard_map/ppermute | solution.py:26
  73.4 99.9 %all-gather.13.cloned.1.call-start = ((), (), s32[]{:S(2)}) async-start(), calls=%async_computation.2 | async-start | bytes 3981312 | tf_op jit(solution)/shard_map/all_gather | solution.py:780
  73.4 11.7 %collective-permute-start.16 = (bf16[4,256,128]{2,1,0:T(8,128)(2,1)}, bf16[4,256,128]{2,1,0:T(8,128)(2,1)S(1)}, u32[]{:S(2)}, u32[]{:S(2)}) collective-permute-start(bf16[4,256,128]{2,1,0:T(8,128)(2,1)} %pad_maximum_fusion.8.refs_0_), channel_id=1, source_target_pairs={{0,4},{4,8},{8,12},{12,16},{16,20},{20,24},{24,28},{28,0},{1,5},{5... | collective-permute-start | bytes 786440 | tf_op jit(solution)/shard_map/ppermute | solution.py:26
  74.5 10.6 %collective-permute-start.20 = (bf16[4,256,128]{2,1,0:T(8,128)(2,1)}, bf16[4,256,128]{2,1,0:T(8,128)(2,1)S(1)}, u32[]{:S(2)}, u32[]{:S(2)}) collective-permute-start(bf16[4,256,128]{2,1,0:T(8,128)(2,1)} %pad_maximum_fusion.8.refs_0_), channel_id=1, source_target_pairs={{0,28},{4,0},{8,4},{12,8},{16,12},{20,16},{24,20},{28,24},{1,29},{... | collective-permute-start | bytes 786440 | tf_op jit(solution)/shard_map/ppermute | solution.py:26
  76.1 7.8 %collective-permute-start.17 = (bf16[64,512]{1,0:T(8,128)(2,1)S(1)}, bf16[64,512]{1,0:T(8,128)(2,1)S(1)}, u32[]{:S(2)}, u32[]{:S(2)}) collective-permute-start(bf16[64,512]{1,0:T(8,128)(2,1)S(1)} %get-tuple-element.124), channel_id=1, source_target_pairs={{0,1},{1,2},{2,3},{3,0},{4,5},{5,6},{6,7},{7,4},{8,9},{9,10},{10,1... | collective-permute-start | bytes 196616 | tf_op jit(solution)/shard_map/ppermute | solution.py:26
  78.2 6.3 %collective-permute-start.18 = (bf16[64,512]{1,0:T(8,128)(2,1)S(1)}, bf16[64,512]{1,0:T(8,128)(2,1)S(1)}, u32[]{:S(2)}, u32[]{:S(2)}) collective-permute-start(bf16[64,512]{1,0:T(8,128)(2,1)S(1)} %get-tuple-element.123), channel_id=1, source_target_pairs={{0,2},{1,3},{2,0},{3,1},{4,6},{5,7},{6,4},{7,5},{8,10},{9,11},{10,... | collective-permute-start | bytes 196616 | tf_op jit(solution)/shard_map/ppermute | solution.py:26
  80.5 4.6 %collective-permute-start.19 = (bf16[64,512]{1,0:T(8,128)(2,1)S(1)}, bf16[64,512]{1,0:T(8,128)(2,1)S(1)}, u32[]{:S(2)}, u32[]{:S(2)}) collective-permute-start(bf16[64,512]{1,0:T(8,128)(2,1)S(1)} %get-tuple-element.122), channel_id=1, source_target_pairs={{0,3},{1,0},{2,1},{3,2},{4,7},{5,4},{6,5},{7,6},{8,11},{9,8},{10,9... | collective-permute-start | bytes 196616 | tf_op jit(solution)/shard_map/ppermute | solution.py:26
  88.0 7.2 %collective-permute-start.23 = (bf16[256,128]{1,0:T(8,128)(2,1)S(1)}, bf16[256,128]{1,0:T(8,128)(2,1)S(1)}, u32[]{:S(2)}, u32[]{:S(2)}) collective-permute-start(bf16[256,128]{1,0:T(8,128)(2,1)S(1)} %get-tuple-element.63.refs_0_), channel_id=1, source_target_pairs={{0,3},{1,0},{2,1},{3,2},{4,7},{5,4},{6,5},{7,6},{8,11},{9,8},{10,9... | collective-permute-start | bytes 196616 | tf_op jit(solution)/shard_map/ppermute | solution.py:26
  90.1 6.1 %collective-permute-start.21 = (bf16[256,128]{1,0:T(8,128)(2,1)S(1)}, bf16[256,128]{1,0:T(8,128)(2,1)S(1)}, u32[]{:S(2)}, u32[]{:S(2)}) collective-permute-start(bf16[256,128]{1,0:T(8,128)(2,1)S(1)} %get-tuple-element.63.refs_0_), channel_id=1, source_target_pairs={{0,1},{1,2},{2,3},{3,0},{4,5},{5,6},{6,7},{7,4},{8,9},{9,10},{10,1... | collective-permute-start | bytes 196616 | tf_op jit(solution)/shard_map/ppermute | solution.py:26
  90.1 6.1 %collective-permute-start.22 = (bf16[256,128]{1,0:T(8,128)(2,1)S(1)}, bf16[256,128]{1,0:T(8,128)(2,1)S(1)}, u32[]{:S(2)}, u32[]{:S(2)}) collective-permute-start(bf16[256,128]{1,0:T(8,128)(2,1)S(1)} %get-tuple-element.63.refs_0_), channel_id=1, source_target_pairs={{0,2},{1,3},{2,0},{3,1},{4,6},{5,7},{6,4},{7,5},{8,10},{9,11},{10,... | collective-permute-start | bytes 196616 | tf_op jit(solution)/shard_map/ppermute | solution.py:26
  96.9 5.0 %collective-permute-start.26 = (bf16[272,128]{1,0:T(8,128)(2,1)S(1)}, bf16[272,128]{1,0:T(8,128)(2,1)S(1)}, u32[]{:S(2)}, u32[]{:S(2)}) collective-permute-start(bf16[272,128]{1,0:T(8,128)(2,1)S(1)} %get-tuple-element.68), channel_id=1, source_target_pairs={{0,3},{1,0},{2,1},{3,2},{4,7},{5,4},{6,5},{7,6},{8,11},{9,8},{10,9... | collective-permute-start | bytes 208904 | tf_op jit(solution)/shard_map/ppermute | solution.py:26
  99.8 6.2 %collective-permute-start.24 = (bf16[272,128]{1,0:T(8,128)(2,1)S(1)}, bf16[272,128]{1,0:T(8,128)(2,1)S(1)}, u32[]{:S(2)}, u32[]{:S(2)}) collective-permute-start(bf16[272,128]{1,0:T(8,128)(2,1)S(1)} %get-tuple-element.66), channel_id=1, source_target_pairs={{0,1},{1,2},{2,3},{3,0},{4,5},{5,6},{6,7},{7,4},{8,9},{9,10},{10,1... | collective-permute-start | bytes 208904 | tf_op jit(solution)/shard_map/ppermute | solution.py:26
  99.9 7.4 %collective-permute-start.25 = (bf16[272,128]{1,0:T(8,128)(2,1)S(1)}, bf16[272,128]{1,0:T(8,128)(2,1)S(1)}, u32[]{:S(2)}, u32[]{:S(2)}) collective-permute-start(bf16[272,128]{1,0:T(8,128)(2,1)S(1)} %get-tuple-element.67), channel_id=1, source_target_pairs={{0,2},{1,3},{2,0},{3,1},{4,6},{5,7},{6,4},{7,5},{8,10},{9,11},{10,... | collective-permute-start | bytes 208904 | tf_op jit(solution)/shard_map/ppermute | solution.py:26
  131.1 5.0 %collective-permute-start.30 = (bf16[4,64,512]{2,1,0:T(8,128)(2,1)S(1)}, bf16[4,64,512]{2,1,0:T(8,128)(2,1)}, u32[]{:S(2)}, u32[]{:S(2)}) collective-permute-start(bf16[4,64,512]{2,1,0:T(8,128)(2,1)S(1)} %dynamic-slice_bitcast_fusion), channel_id=1, source_target_pairs={{0,4},{4,0},{8,12},{12,8},{16,20},{20,16},{24,28},{28,24},{1,5},{5... | collective-permute-start | bytes 786440 | tf_op jit(solution)/shard_map/ppermute | solution.py:623
  136.1 28.6 %copy-start.11 = (f32[64,512]{1,0:T(8,128)S(1)}, f32[64,512]{1,0:T(8,128)}, u32[]{:S(2)}) copy-start(f32[64,512]{1,0:T(8,128)} %refs_2_.5) | copy-start | bytes 393220
  139.6 10.4 %collective-permute-start.31 = (bf16[2,64,512]{2,1,0:T(8,128)(2,1)}, bf16[2,64,512]{2,1,0:T(8,128)(2,1)}, u32[]{:S(2)}, u32[]{:S(2)}) collective-permute-start(bf16[2,64,512]{2,1,0:T(8,128)(2,1)} %fusion), channel_id=1, source_target_pairs={{0,8},{4,12},{8,0},{12,4},{16,24},{20,28},{24,16},{28,20},{1,9},{5... | collective-permute-start | bytes 393224 | tf_op jit(solution)/shard_map/ppermute | solution.py:623
  139.7 7.0 %collective-permute-start.27 = (bf16[256,128]{1,0:T(8,128)(2,1)}, bf16[256,128]{1,0:T(8,128)(2,1)S(1)}, u32[]{:S(2)}, u32[]{:S(2)}) collective-permute-start(bf16[256,128]{1,0:T(8,128)(2,1)} %get-tuple-element.77), channel_id=1, source_target_pairs={{0,1},{1,2},{2,3},{3,0},{4,5},{5,6},{6,7},{7,4},{8,9},{9,10},{10,1... | collective-permute-start | bytes 196616 | tf_op jit(solution)/shard_map/ppermute | solution.py:26
  139.8 8.7 %collective-permute-start.28 = (bf16[256,128]{1,0:T(8,128)(2,1)}, bf16[256,128]{1,0:T(8,128)(2,1)S(1)}, u32[]{:S(2)}, u32[]{:S(2)}) collective-permute-start(bf16[256,128]{1,0:T(8,128)(2,1)} %get-tuple-element.78), channel_id=1, source_target_pairs={{0,2},{1,3},{2,0},{3,1},{4,6},{5,7},{6,4},{7,5},{8,10},{9,11},{10,... | collective-permute-start | bytes 196616 | tf_op jit(solution)/shard_map/ppermute | solution.py:26
  142.5 6.0 %collective-permute-start.29 = (bf16[256,128]{1,0:T(8,128)(2,1)}, bf16[256,128]{1,0:T(8,128)(2,1)}, u32[]{:S(2)}, u32[]{:S(2)}) collective-permute-start(bf16[256,128]{1,0:T(8,128)(2,1)} %get-tuple-element.79), channel_id=1, source_target_pairs={{0,3},{1,0},{2,1},{3,2},{4,7},{5,4},{6,5},{7,6},{8,11},{9,8},{10,9... | collective-permute-start | bytes 196616 | tf_op jit(solution)/shard_map/ppermute | solution.py:26
  143.6 21.1 %copy-start.4 = (bf16[2,8,320,128]{3,2,1,0:T(8,128)(2,1)S(1)}, bf16[2,8,320,128]{3,2,1,0:T(8,128)(2,1)}, u32[]{:S(2)}) copy-start(bf16[2,8,320,128]{3,2,1,0:T(8,128)(2,1)} %shard_map.160.slots_ref) | copy-start | bytes 3932164
  151.1 13.5 %collective-permute-start.32 = (bf16[1,64,512]{2,1,0:T(8,128)(2,1)S(1)}, bf16[1,64,512]{2,1,0:T(8,128)(2,1)S(1)}, u32[]{:S(2)}, u32[]{:S(2)}) collective-permute-start(bf16[1,64,512]{2,1,0:T(8,128)(2,1)S(1)} %dynamic-slice_convert_fusion), channel_id=1, source_target_pairs={{0,16},{4,20},{8,24},{12,28},{16,0},{20,4},{24,8},{28,12},{1,17},{... | collective-permute-start | bytes 196616 | tf_op jit(solution)/shard_map/ppermute | solution.py:623
  171.2 13.9 %collective-permute-start.33 = (bf16[31,64,128]{2,1,0:T(8,128)(2,1)S(1)}, bf16[31,64,128]{2,1,0:T(8,128)(2,1)S(1)}, u32[]{:S(2)}, u32[]{:S(2)}) collective-permute-start(bf16[31,64,128]{2,1,0:T(8,128)(2,1)S(1)} %get-tuple-element.88.refs_0_), channel_id=1, source_target_pairs={{0,8},{4,12},{8,0},{12,4},{16,24},{20,28},{24,16},{28,20},{1,9},{5... | collective-permute-start | bytes 1523720 | tf_op jit(solution)/shard_map/ppermute | solution.py:623
  172.2 13.5 %collective-permute-start.34 = (bf16[31,64,128]{2,1,0:T(8,128)(2,1)S(1)}, bf16[31,64,128]{2,1,0:T(8,128)(2,1)S(1)}, u32[]{:S(2)}, u32[]{:S(2)}) collective-permute-start(bf16[31,64,128]{2,1,0:T(8,128)(2,1)S(1)} %get-tuple-element.88.refs_0_), channel_id=1, source_target_pairs={{0,16},{4,20},{8,24},{12,28},{16,0},{20,4},{24,8},{28,12},{1,17},{... | collective-permute-start | bytes 1523720 | tf_op jit(solution)/shard_map/ppermute | solution.py:623
  173.2 15.2 %collective-permute-start.36 = (bf16[31,64,128]{2,1,0:T(8,128)(2,1)S(1)}, bf16[31,64,128]{2,1,0:T(8,128)(2,1)S(1)}, u32[]{:S(2)}, u32[]{:S(2)}) collective-permute-start(bf16[31,64,128]{2,1,0:T(8,128)(2,1)S(1)} %get-tuple-element.88.refs_0_), channel_id=1, source_target_pairs={{0,4},{4,0},{8,12},{12,8},{16,20},{20,16},{24,28},{28,24},{1,5},{5... | collective-permute-start | bytes 1523720 | tf_op jit(solution)/shard_map/ppermute | solution.py:623
  185.8 2.7 %collective-permute-start.37 = (bf16[31,64,128]{2,1,0:T(8,128)(2,1)S(1)}, bf16[31,64,128]{2,1,0:T(8,128)(2,1)S(1)}, u32[]{:S(2)}, u32[]{:S(2)}) collective-permute-start(bf16[31,64,128]{2,1,0:T(8,128)(2,1)S(1)} %collective-permute-done.33.refs_1_), channel_id=1, source_target_pairs={{0,4},{4,0},{8,12},{12,8},{16,20},{20,16},{24,28},{28,24},{1,5},{5... | collective-permute-start | bytes 1523720 | tf_op jit(solution)/shard_map/ppermute | solution.py:623
  185.8 2.7 %collective-permute-start.38 = (bf16[31,64,128]{2,1,0:T(8,128)(2,1)S(1)}, bf16[31,64,128]{2,1,0:T(8,128)(2,1)S(1)}, u32[]{:S(2)}, u32[]{:S(2)}) collective-permute-start(bf16[31,64,128]{2,1,0:T(8,128)(2,1)S(1)} %collective-permute-done.34.refs_2_), channel_id=1, source_target_pairs={{0,4},{4,0},{8,12},{12,8},{16,20},{20,16},{24,28},{28,24},{1,5},{5... | collective-permute-start | bytes 1523720 | tf_op jit(solution)/shard_map/ppermute | solution.py:623
  186.3 8.3 %collective-permute-start.39 = (bf16[16,64,128]{2,1,0:T(8,128)(2,1)S(1)}, bf16[16,64,128]{2,1,0:T(8,128)(2,1)S(1)}, u32[]{:S(2)}, u32[]{:S(2)}) collective-permute-start(bf16[16,64,128]{2,1,0:T(8,128)(2,1)S(1)} %slice.155), channel_id=1, source_target_pairs={{0,16},{4,20},{8,24},{12,28},{16,0},{20,4},{24,8},{28,12},{1,17},{... | collective-permute-start | bytes 786440 | tf_op jit(solution)/shard_map/ppermute | solution.py:623
  187.4 7.6 %collective-permute-start.35 = (bf16[15,64,128]{2,1,0:T(8,128)(2,1)S(1)}, bf16[15,64,128]{2,1,0:T(8,128)(2,1)S(1)}, u32[]{:S(2)}, u32[]{:S(2)}) collective-permute-start(bf16[15,64,128]{2,1,0:T(8,128)(2,1)S(1)} %slice.154), channel_id=1, source_target_pairs={{0,8},{4,12},{8,0},{12,4},{16,24},{20,28},{24,16},{28,20},{1,9},{5... | collective-permute-start | bytes 737288 | tf_op jit(solution)/shard_map/ppermute | solution.py:623
  194.6 2.0 collective-permute-start.41
  195.1 1.5 collective-permute-start.40
  (14 other events, 55.6 us)
Sparse Core Ops, SparseCore 0:
  48.5 27.6 all-gather.10
  78.7 27.6 all-gather.8
  131.2 37.4 all-gather.12

commit v3 on v2

--- a/solution.py
+++ b/solution.py
@@ -598,7 +598,7 @@
         ),
         out_shape=outs,
         input_output_aliases={first: 1, first + 1: 2} if kept else {},
-        compiler_params=BIG,
+        compiler_params=FULL,
     )(axis_word(SPLIT), slots, errors, counted, *states, *dec, *kept)
 
 

time: 205 us -> 199 us (0.971)
  local copies, waits for them, and re-layouts: 13.1 us -> 7.15 us
  other arithmetic: 7.69 us -> 5.53 us
    unnamed x36 -> x22, local copies, waits for them, and re-layouts: 8.86 us -> 4.57 us
    add x2, other arithmetic: 2.92 us -> 0.11 us  [halved(): block = keep.astype(FLOAT) + sent.astype(FLOAT)]
    pallas_call x2, Pallas kernels: 11.4 us -> 14.2 us  [kernel_step(): pl.pallas_call(kernel, grid_spec=pltpu.PrefetchScalarGridSpec(num_scalar_...]
  transfers between devices with their start and end apart: 45 -> 45, of which waited for: 25 -> 25; matrix products, arithmetic and copies ran while one was open for 6% -> 4% of each run, Pallas kernels for 15% -> 16%
where the time goes in v3:
time: 199 us; the launch traced here: 198 us
  starting transfers between devices  53.3 us (27%)
  waiting for transfers between devices  49.9 us (25%)
  Pallas kernels  44.7 us (22%)
  blocking collectives  23.1 us (12%)
  between operations  14.2 us (7%)
  local copies, waits for them, and re-layouts  7.15 us (4%)
  other arithmetic  5.53 us (3%)
    ppermute x30, starting transfers between devices, shift(): lax.ppermute(block, axis, [(i, (i + by) % count) for i in range(count)])  45.4 us
    ppermute x30, waiting for transfers between devices, shift(): lax.ppermute(block, axis, [(i, (i + by) % count) for i in range(count)])  37.6 us
    pallas_call x2, Pallas kernels, kernel_step(): pl.pallas_call(kernel, grid_spec=pltpu.PrefetchScalarGridSpec(num_scalar_...  14.2 us
    ppermute x12, waiting for transfers between devices, cross(): return lax.ppermute(block, SPLIT, [(i, i ^ mask) for i in range(count)])  12.3 us
    all_gather x1, blocking collectives, body(): errors_two = lax.all_gather(d_pre_two, SPLIT, axis=0)  11.7 us
    all_gather x1, blocking collectives, body(): errors_one = lax.all_gather(d_pre_one, SPLIT, axis=0)  11.4 us
    pallas_call x4, Pallas kernels, conv_planes(): pl.pallas_call(kernel, grid=(1,), out_shape=outs, in_specs=[pl.BlockSpec(...  9.34 us
    ppermute x12, starting transfers between devices, cross(): return lax.ppermute(block, SPLIT, [(i, i ^ mask) for i in range(count)])  7.81 us
  transfers between devices with their start and end apart: 45, of which 25 were waited for; matrix products, arithmetic and copies ran while one was open for 4% of the time, Pallas kernels for 16%

profile of v3, /device:TPU:0, one launch (start us, length us, event | category | flops | bytes accessed | tf_op | source)
XLA Modules:
  0.0 198.2 jit_solution(11006981126519781043)
XLA Ops:
  9.8 4.7 %collective-permute-start.5 = (bf16[64,2048]{1,0:T(8,128)(2,1)S(1)}, bf16[64,2048]{1,0:T(8,128)(2,1)S(1)}, u32[]{:S(2)}, u32[]{:S(2)}) collective-permute-start(bf16[64,2048]{1,0:T(8,128)(2,1)S(1)} %shard_map.152.refs_0_), channel_id=1, source_target_pairs={{0,3},{1,0},{2,1},{3,2},{4,7},{5,4},{6,5},{7,6},{8,11},{9,8},{10,9... | collective-permute-start | bytes 786440 | tf_op jit(solution)/shard_map/ppermute | solution.py:26
  14.5 2.3 %collective-permute-start.1 = (f32[4,2,16,256]{3,2,1,0:T(8,128)S(1)}, f32[4,2,16,256]{3,2,1,0:T(8,128)S(1)}, u32[]{:S(2)}, u32[]{:S(2)}) collective-permute-start(f32[4,2,16,256]{3,2,1,0:T(8,128)S(1)} %get-tuple-element.56), channel_id=1, source_target_pairs={{0,28},{4,0},{8,4},{12,8},{16,12},{20,16},{24,20},{28,24},{1,29},{... | collective-permute-start | bytes 393224 | tf_op jit(solution)/shard_map/ppermute | solution.py:26
  16.8 2.4 %collective-permute-done.1 = f32[4,2,16,256]{3,2,1,0:T(8,128)S(1)} collective-permute-done((f32[4,2,16,256]{3,2,1,0:T(8,128)S(1)}, f32[4,2,16,256]{3,2,1,0:T(8,128)S(1)}, u32[]{:S(2)}, u32[]{:S(2)}) %collective-permute-start.1) | collective-permute-done | bytes 131104 | tf_op jit(solution)/shard_map/ppermute | solution.py:26
  19.4 3.8 %collective-permute-start.3 = (f32[4,12,2,256]{3,2,1,0:T(2,128)S(1)}, f32[4,12,2,256]{3,2,1,0:T(2,128)S(1)}, u32[]{:S(2)}, u32[]{:S(2)}) collective-permute-start(f32[4,12,2,256]{3,2,1,0:T(2,128)S(1)} %get-tuple-element.58), channel_id=1, source_target_pairs={{0,3},{1,0},{2,1},{3,2},{4,7},{5,4},{6,5},{7,6},{8,11},{9,8},{10,9... | collective-permute-start | bytes 294920 | tf_op jit(solution)/shard_map/ppermute | solution.py:26
  23.3 1.8 collective-permute-start.7
  25.1 2.2 %collective-permute-done.4.refs_1_ = bf16[64,2048]{1,0:T(8,128)(2,1)S(1)} collective-permute-done((bf16[64,2048]{1,0:T(8,128)(2,1)S(1)}, bf16[64,2048]{1,0:T(8,128)(2,1)S(1)}, u32[]{:S(2)}, u32[]{:S(2)}) %collective-permute-start.4) | collective-permute-done | bytes 262176 | tf_op jit(solution)/shard_map/ppermute | solution.py:26
  27.3 1.5 collective-permute-start.6
  29.4 2.5 %collective-permute-done.3 = f32[4,12,2,256]{3,2,1,0:T(2,128)S(1)} collective-permute-done((f32[4,12,2,256]{3,2,1,0:T(2,128)S(1)}, f32[4,12,2,256]{3,2,1,0:T(2,128)S(1)}, u32[]{:S(2)}, u32[]{:S(2)}) %collective-permute-start.3) | collective-permute-done | bytes 98336 | tf_op jit(solution)/shard_map/ppermute | solution.py:26
  32.1 3.1 %collective-permute-done.7.refs_4_ = bf16[32,2048]{1,0:T(8,128)(2,1)S(1)} collective-permute-done((bf16[32,2048]{1,0:T(8,128)(2,1)S(1)}, bf16[32,2048]{1,0:T(8,128)(2,1)S(1)}, u32[]{:S(2)}, u32[]{:S(2)}) %collective-permute-start.7) | collective-permute-done | bytes 131104 | tf_op jit(solution)/shard_map/ppermute | solution.py:26
  35.2 1.8 collective-permute-done.6.refs_3_
  37.5 2.5 %collective-permute-start.9 = (bf16[256,128]{1,0:T(8,128)(2,1)S(1)}, bf16[256,128]{1,0:T(8,128)(2,1)S(1)}, u32[]{:S(2)}, u32[]{:S(2)}) collective-permute-start(bf16[256,128]{1,0:T(8,128)(2,1)S(1)} %shard_map.153.refs_3_), channel_id=1, source_target_pairs={{0,2},{1,3},{2,0},{3,1},{4,6},{5,7},{6,4},{7,5},{8,10},{9,11},{10,... | collective-permute-start | bytes 196616 | tf_op jit(solution)/shard_map/ppermute | solution.py:26
  40.0 1.5 collective-permute-start.10
  42.0 2.5 %collective-permute-done.9 = bf16[256,128]{1,0:T(8,128)(2,1)S(1)} collective-permute-done((bf16[256,128]{1,0:T(8,128)(2,1)S(1)}, bf16[256,128]{1,0:T(8,128)(2,1)S(1)}, u32[]{:S(2)}, u32[]{:S(2)}) %collective-permute-start.9) | collective-permute-done | bytes 65568 | tf_op jit(solution)/shard_map/ppermute | solution.py:26
  44.6 3.0 %collective-permute-done.8 = bf16[256,128]{1,0:T(8,128)(2,1)S(1)} collective-permute-done((bf16[256,128]{1,0:T(8,128)(2,1)S(1)}, bf16[256,128]{1,0:T(8,128)(2,1)S(1)}, u32[]{:S(2)}, u32[]{:S(2)}) %collective-permute-start.8) | collective-permute-done | bytes 65568 | tf_op jit(solution)/shard_map/ppermute | solution.py:26
  51.1 2.6 %collective-permute-start.12 = (bf16[4,256,128]{2,1,0:T(8,128)(2,1)S(1)}, bf16[4,256,128]{2,1,0:T(8,128)(2,1)S(1)}, u32[]{:S(2)}, u32[]{:S(2)}) collective-permute-start(bf16[4,256,128]{2,1,0:T(8,128)(2,1)S(1)} %copy-done.4), channel_id=1, source_target_pairs={{0,28},{4,0},{8,4},{12,8},{16,12},{20,16},{24,20},{28,24},{1,29},{... | collective-permute-start | bytes 786440 | tf_op jit(solution)/shard_map/ppermute | solution.py:26
  53.8 1.4 convert_subtract_fusion
  56.1 1.9 shard_map.154.refs_4_
  59.2 2.3 %collective-permute-done.12.refs_1_ = bf16[4,256,128]{2,1,0:T(8,128)(2,1)S(1)} collective-permute-done((bf16[4,256,128]{2,1,0:T(8,128)(2,1)S(1)}, bf16[4,256,128]{2,1,0:T(8,128)(2,1)S(1)}, u32[]{:S(2)}, u32[]{:S(2)}) %collective-permute-start.12) | collective-permute-done | bytes 262176 | tf_op jit(solution)/shard_map/ppermute | solution.py:26
  61.5 2.8 %shard_map.156 = (f32[256,128]{1,0:T(8,128)S(1)}, bf16[256,128]{1,0:T(8,128)(2,1)S(1)}) custom-call(s32[1]{0:T(128)} %bitcast.7.own_ref, bf16[4,256,128]{2,1,0:T(8,128)(2,1)S(1)} %collective-permute-done.11.refs_0_, bf16[4,256,128]{2,1,0:T(8,128)(2,1)S(1)} %collective-permute-done.12.refs_1_, bf16[2,27,512,128]{3,2,1,0:T(8,128)(2,1)} %w_hbm.3, ...), custom_call_target="tpu_custom_call" | custom-call | tf_op jit(solution)/shard_map/pallas_call | solution.py:223
  64.4 2.3 %collective-permute-start.14 = (bf16[256,128]{1,0:T(8,128)(2,1)S(1)}, bf16[256,128]{1,0:T(8,128)(2,1)S(1)}, u32[]{:S(2)}, u32[]{:S(2)}) collective-permute-start(bf16[256,128]{1,0:T(8,128)(2,1)S(1)} %get-tuple-element.61.refs_3_), channel_id=1, source_target_pairs={{0,2},{1,3},{2,0},{3,1},{4,6},{5,7},{6,4},{7,5},{8,10},{9,11},{10,... | collective-permute-start | bytes 196616 | tf_op jit(solution)/shard_map/ppermute | solution.py:26
  66.7 2.8 %collective-permute-start.15 = (bf16[256,128]{1,0:T(8,128)(2,1)S(1)}, bf16[256,128]{1,0:T(8,128)(2,1)S(1)}, u32[]{:S(2)}, u32[]{:S(2)}) collective-permute-start(bf16[256,128]{1,0:T(8,128)(2,1)S(1)} %get-tuple-element.61.refs_3_), channel_id=1, source_target_pairs={{0,3},{1,0},{2,1},{3,2},{4,7},{5,4},{6,5},{7,6},{8,11},{9,8},{10,9... | collective-permute-start | bytes 196616 | tf_op jit(solution)/shard_map/ppermute | solution.py:26
  70.5 2.1 %collective-permute-done.15 = bf16[256,128]{1,0:T(8,128)(2,1)S(1)} collective-permute-done((bf16[256,128]{1,0:T(8,128)(2,1)S(1)}, bf16[256,128]{1,0:T(8,128)(2,1)S(1)}, u32[]{:S(2)}, u32[]{:S(2)}) %collective-permute-start.15) | collective-permute-done | bytes 65568 | tf_op jit(solution)/shard_map/ppermute | solution.py:26
  74.5 1.6 collective-permute-start.20
  76.1 2.0 %collective-permute-start.17 = (bf16[64,512]{1,0:T(8,128)(2,1)S(1)}, bf16[64,512]{1,0:T(8,128)(2,1)S(1)}, u32[]{:S(2)}, u32[]{:S(2)}) collective-permute-start(bf16[64,512]{1,0:T(8,128)(2,1)S(1)} %get-tuple-element.124), channel_id=1, source_target_pairs={{0,1},{1,2},{2,3},{3,0},{4,5},{5,6},{6,7},{7,4},{8,9},{9,10},{10,1... | collective-permute-start | bytes 196616 | tf_op jit(solution)/shard_map/ppermute | solution.py:26
  78.2 2.3 %collective-permute-start.18 = (bf16[64,512]{1,0:T(8,128)(2,1)S(1)}, bf16[64,512]{1,0:T(8,128)(2,1)S(1)}, u32[]{:S(2)}, u32[]{:S(2)}) collective-permute-start(bf16[64,512]{1,0:T(8,128)(2,1)S(1)} %get-tuple-element.123), channel_id=1, source_target_pairs={{0,2},{1,3},{2,0},{3,1},{4,6},{5,7},{6,4},{7,5},{8,10},{9,11},{10,... | collective-permute-start | bytes 196616 | tf_op jit(solution)/shard_map/ppermute | solution.py:26
  82.0 1.9 shard_map.158.refs_4_
  85.1 2.8 %shard_map.159 = (f32[256,128]{1,0:T(8,128)S(1)}, bf16[256,128]{1,0:T(8,128)(2,1)S(1)}) custom-call(s32[1]{0:T(128)} %bitcast.7.own_ref, bf16[4,256,128]{2,1,0:T(8,128)(2,1)S(1)} %collective-permute-done.16.refs_0_, bf16[4,256,128]{2,1,0:T(8,128)(2,1)S(1)} %collective-permute-done.20.refs_1_, bf16[2,27,512,128]{3,2,1,0:T(8,128)(2,1)} %w_hbm.3, ...), custom_call_target="tpu_custom_call" | custom-call | tf_op jit(solution)/shard_map/pallas_call | solution.py:223
  88.0 2.2 %collective-permute-start.23 = (bf16[256,128]{1,0:T(8,128)(2,1)S(1)}, bf16[256,128]{1,0:T(8,128)(2,1)S(1)}, u32[]{:S(2)}, u32[]{:S(2)}) collective-permute-start(bf16[256,128]{1,0:T(8,128)(2,1)S(1)} %get-tuple-element.63.refs_0_), channel_id=1, source_target_pairs={{0,3},{1,0},{2,1},{3,2},{4,7},{5,4},{6,5},{7,6},{8,11},{9,8},{10,9... | collective-permute-start | bytes 196616 | tf_op jit(solution)/shard_map/ppermute | solution.py:26
  91.5 3.6 %shard_map.160.slots_ref = bf16[2,8,320,128]{3,2,1,0:T(8,128)(2,1)} custom-call(s32[2]{0:T(128)} %pad_add_fusion.word_ref, bf16[8,4,256,128]{3,2,1,0:T(8,128)(2,1)} %bitcast.59), custom_call_target="tpu_custom_call" | custom-call | tf_op jit(solution)/shard_map/pallas_call | solution.py:450
  96.9 2.9 %collective-permute-start.26 = (bf16[272,128]{1,0:T(8,128)(2,1)S(1)}, bf16[272,128]{1,0:T(8,128)(2,1)S(1)}, u32[]{:S(2)}, u32[]{:S(2)}) collective-permute-start(bf16[272,128]{1,0:T(8,128)(2,1)S(1)} %get-tuple-element.68), channel_id=1, source_target_pairs={{0,3},{1,0},{2,1},{3,2},{4,7},{5,4},{6,5},{7,6},{8,11},{9,8},{10,9... | collective-permute-start | bytes 208904 | tf_op jit(solution)/shard_map/ppermute | solution.py:26
  101.9 4.2 %collective-permute-done.24.refs_0_ = bf16[272,128]{1,0:T(8,128)(2,1)S(1)} collective-permute-done((bf16[272,128]{1,0:T(8,128)(2,1)S(1)}, bf16[272,128]{1,0:T(8,128)(2,1)S(1)}, u32[]{:S(2)}, u32[]{:S(2)}) %collective-permute-start.24) | collective-permute-done | bytes 69664 | tf_op jit(solution)/shard_map/ppermute | solution.py:26
  107.3 11.7 %all-gather.2 = bf16[2176,128]{1,0:T(8,128)(2,1)} all-gather(bf16[272,128]{1,0:T(8,128)(2,1)S(1)} %get-tuple-element.74), channel_id=4, replica_groups=mesh['grp'=2,'sp'=4,'ch'=4] {'grp','sp'}, dimensions={0}, use_global_device_ids=true | all-gather | bytes 626688 | tf_op jit(solution)/shard_map/all_gather | solution.py:766
  119.0 3.6 %shard_map.157.slots_ref = bf16[2,8,320,128]{3,2,1,0:T(8,128)(2,1)} custom-call(s32[2]{0:T(128)} %pad_add_fusion.word_ref, bf16[8,4,256,128]{3,2,1,0:T(8,128)(2,1)} %bitcast.60), custom_call_target="tpu_custom_call" | custom-call | tf_op jit(solution)/shard_map/pallas_call | solution.py:450
  122.7 7.0 %shard_map.163 = (bf16[27,64,128]{2,1,0:T(8,128)(2,1)}, f32[2,27,64,128]{3,2,1,0:T(8,128)}, f32[2,27,64,128]{3,2,1,0:T(8,128)}, f32[8,128]{1,0:T(8,128)}) custom-call(s32[1]{0:T(128)} %bitcast.6.word_ref.place_ref, bf16[2,8,320,128]{3,2,1,0:T(8,128)(2,1)} %shard_map.157.slots_ref, bf16[8,272,128]{2,1,0:T(8,128)(2,1)} %bitcast.49, ...), custom_call_target="tpu_custom_call" | custom-call | tf_op jit(solution)/shard_map/pallas_call | solution.py:566
  130.2 3.8 %shard_map.164 = (f32[256,128]{1,0:T(8,128)S(1)}, bf16[256,128]{1,0:T(8,128)(2,1)S(1)}, bf16[256,128]{1,0:T(8,128)(2,1)S(1)}, bf16[256,128]{1,0:T(8,128)(2,1)S(1)}) custom-call(s32[2]{0:T(128)S(1)} %pad_add_fusion.1.own_ref, bf16[8,272,128]{2,1,0:T(8,128)(2,1)S(1)} %bitcast.52, bf16[8,272,128]{2,1,0:T(8,128)(2,1)S(1)} %bitcast.53, ...), custom_call_target="tpu_custom_call" | custom-call | tf_op jit(solution)/shard_map/pallas_call | solution.py:309
  134.8 2.7 %collective-permute-start.28 = (bf16[256,128]{1,0:T(8,128)(2,1)S(1)}, bf16[256,128]{1,0:T(8,128)(2,1)S(1)}, u32[]{:S(2)}, u32[]{:S(2)}) collective-permute-start(bf16[256,128]{1,0:T(8,128)(2,1)S(1)} %get-tuple-element.78), channel_id=1, source_target_pairs={{0,2},{1,3},{2,0},{3,1},{4,6},{5,7},{6,4},{7,5},{8,10},{9,11},{10,... | collective-permute-start | bytes 196616 | tf_op jit(solution)/shard_map/ppermute | solution.py:26
  138.6 2.9 %collective-permute-done.27.refs_0_ = bf16[256,128]{1,0:T(8,128)(2,1)S(1)} collective-permute-done((bf16[256,128]{1,0:T(8,128)(2,1)S(1)}, bf16[256,128]{1,0:T(8,128)(2,1)S(1)}, u32[]{:S(2)}, u32[]{:S(2)}) %collective-permute-start.27) | collective-permute-done | bytes 65568 | tf_op jit(solution)/shard_map/ppermute | solution.py:26
  141.5 1.6 collective-permute-done.28.refs_1_
  143.9 1.5 collective-permute-start.32
  145.4 11.4 %all-gather.3 = bf16[2048,128]{1,0:T(8,128)(2,1)} all-gather(bf16[256,128]{1,0:T(8,128)(2,1)S(1)} %get-tuple-element.82), channel_id=5, replica_groups=mesh['grp'=2,'sp'=4,'ch'=4] {'grp','sp'}, dimensions={0}, use_global_device_ids=true | all-gather | bytes 589824 | tf_op jit(solution)/shard_map/all_gather | solution.py:769
  157.5 7.2 %shard_map.166 = (bf16[31,64,128]{2,1,0:T(8,128)(2,1)}, f32[2,27,64,128]{3,2,1,0:T(8,128)}, f32[2,27,64,128]{3,2,1,0:T(8,128)}, f32[8,128]{1,0:T(8,128)}, f32[64,512]{1,0:T(8,128)}, /*index=5*/f32[64,512]{1,0:T(8,128)}) custom-call(s32[1]{0:T(128)} %bitcast.6.word_ref.place_ref, ...), custom_call_target="tpu_custom_call", output_to_operand_aliasing={{1}: (11, {}), {2}: (12, {})} | custom-call | tf_op jit(solution)/shard_map/pallas_call | solution.py:566
  164.7 1.5 collective-permute-start.33
  166.8 2.0 %copy-done.3 = bf16[216,64,128]{2,1,0:T(8,128)(2,1)S(1)} copy-done((bf16[216,64,128]{2,1,0:T(8,128)(2,1)S(1)}, bf16[216,64,128]{2,1,0:T(8,128)(2,1)}, u32[]{:S(2)}) %copy-start.3) | copy-done | bytes 3538968
  168.8 3.3 %shard_map.167.refs_6_ = bf16[2,27,512,128]{3,2,1,0:T(8,128)(2,1)} custom-call(bf16[8,27,64,128]{3,2,1,0:T(8,128)(2,1)S(1)} %bitcast.55), custom_call_target="tpu_custom_call" | custom-call | tf_op jit(solution)/shard_map/pallas_call | solution.py:611
  172.1 6.7 %collective-permute-done.33.refs_1_ = bf16[31,64,128]{2,1,0:T(8,128)(2,1)S(1)} collective-permute-done((bf16[31,64,128]{2,1,0:T(8,128)(2,1)}, bf16[31,64,128]{2,1,0:T(8,128)(2,1)S(1)}, u32[]{:S(2)}, u32[]{:S(2)}) %collective-permute-start.33) | collective-permute-done | bytes 507936 | tf_op jit(solution)/shard_map/ppermute | solution.py:623
  181.2 1.5 collective-permute-start.35
  182.7 1.9 shard_map.168
  184.6 4.2 %collective-permute-done.39.refs_1_ = bf16[16,64,128]{2,1,0:T(8,128)(2,1)S(1)} collective-permute-done((bf16[16,64,128]{2,1,0:T(8,128)(2,1)S(1)}, bf16[16,64,128]{2,1,0:T(8,128)(2,1)S(1)}, u32[]{:S(2)}, u32[]{:S(2)}) %collective-permute-start.39) | collective-permute-done | bytes 262176 | tf_op jit(solution)/shard_map/ppermute | solution.py:623
  (118 shorter events, 32.0 us)
Async XLA Ops:
  7.2 78.0 %all-gather.11.cloned.1.call-start = ((), (), s32[]{:S(2)}) async-start(), calls=%async_computation.1 | async-start | bytes 2359296 | tf_op jit(solution)/shard_map/all_gather | solution.py:745
  9.3 7.5 %collective-permute-start = (f32[4,2,16,256]{3,2,1,0:T(8,128)S(1)}, f32[4,2,16,256]{3,2,1,0:T(8,128)S(1)}, u32[]{:S(2)}, u32[]{:S(2)}) collective-permute-start(f32[4,2,16,256]{3,2,1,0:T(8,128)S(1)} %get-tuple-element.55), channel_id=1, source_target_pairs={{0,4},{4,8},{8,12},{12,16},{16,20},{20,24},{24,28},{28,0},{1,5},{5... | collective-permute-start | bytes 393224 | tf_op jit(solution)/shard_map/ppermute | solution.py:26
  9.8 13.5 %collective-permute-start.5 = (bf16[64,2048]{1,0:T(8,128)(2,1)S(1)}, bf16[64,2048]{1,0:T(8,128)(2,1)S(1)}, u32[]{:S(2)}, u32[]{:S(2)}) collective-permute-start(bf16[64,2048]{1,0:T(8,128)(2,1)S(1)} %shard_map.152.refs_0_), channel_id=1, source_target_pairs={{0,3},{1,0},{2,1},{3,2},{4,7},{5,4},{6,5},{7,6},{8,11},{9,8},{10,9... | collective-permute-start | bytes 786440 | tf_op jit(solution)/shard_map/ppermute | solution.py:26
  14.5 12.8 %collective-permute-start.4 = (bf16[64,2048]{1,0:T(8,128)(2,1)S(1)}, bf16[64,2048]{1,0:T(8,128)(2,1)S(1)}, u32[]{:S(2)}, u32[]{:S(2)}) collective-permute-start(bf16[64,2048]{1,0:T(8,128)(2,1)S(1)} %shard_map.152.refs_0_), channel_id=1, source_target_pairs={{0,1},{1,2},{2,3},{3,0},{4,5},{5,6},{6,7},{7,4},{8,9},{9,10},{10,1... | collective-permute-start | bytes 786440 | tf_op jit(solution)/shard_map/ppermute | solution.py:26
  14.5 4.8 %collective-permute-start.1 = (f32[4,2,16,256]{3,2,1,0:T(8,128)S(1)}, f32[4,2,16,256]{3,2,1,0:T(8,128)S(1)}, u32[]{:S(2)}, u32[]{:S(2)}) collective-permute-start(f32[4,2,16,256]{3,2,1,0:T(8,128)S(1)} %get-tuple-element.56), channel_id=1, source_target_pairs={{0,28},{4,0},{8,4},{12,8},{16,12},{20,16},{24,20},{28,24},{1,29},{... | collective-permute-start | bytes 393224 | tf_op jit(solution)/shard_map/ppermute | solution.py:26
  16.8 20.2 %copy-start.7 = (bf16[2048,128]{1,0:T(8,128)(2,1)S(1)}, bf16[2048,128]{1,0:T(8,128)(2,1)}, u32[]{:S(2)}) copy-start(bf16[2048,128]{1,0:T(8,128)(2,1)} %refs_5_.1) | copy-start | bytes 1572868
  19.4 10.0 %collective-permute-start.2 = (f32[4,12,2,256]{3,2,1,0:T(2,128)S(1)}, f32[4,12,2,256]{3,2,1,0:T(2,128)S(1)}, u32[]{:S(2)}, u32[]{:S(2)}) collective-permute-start(f32[4,12,2,256]{3,2,1,0:T(2,128)S(1)} %get-tuple-element.57), channel_id=1, source_target_pairs={{0,1},{1,2},{2,3},{3,0},{4,5},{5,6},{6,7},{7,4},{8,9},{9,10},{10,1... | collective-permute-start | bytes 294920 | tf_op jit(solution)/shard_map/ppermute | solution.py:26
  19.4 12.5 %collective-permute-start.3 = (f32[4,12,2,256]{3,2,1,0:T(2,128)S(1)}, f32[4,12,2,256]{3,2,1,0:T(2,128)S(1)}, u32[]{:S(2)}, u32[]{:S(2)}) collective-permute-start(f32[4,12,2,256]{3,2,1,0:T(2,128)S(1)} %get-tuple-element.58), channel_id=1, source_target_pairs={{0,3},{1,0},{2,1},{3,2},{4,7},{5,4},{6,5},{7,6},{8,11},{9,8},{10,9... | collective-permute-start | bytes 294920 | tf_op jit(solution)/shard_map/ppermute | solution.py:26
  23.3 11.9 %collective-permute-start.7 = (bf16[32,2048]{1,0:T(8,128)(2,1)S(1)}, bf16[32,2048]{1,0:T(8,128)(2,1)S(1)}, u32[]{:S(2)}, u32[]{:S(2)}) collective-permute-start(bf16[32,2048]{1,0:T(8,128)(2,1)S(1)} %slice.181), channel_id=1, source_target_pairs={{0,3},{1,0},{2,1},{3,2},{4,7},{5,4},{6,5},{7,6},{8,11},{9,8},{10,9... | collective-permute-start | bytes 393224 | tf_op jit(solution)/shard_map/ppermute | solution.py:26
  27.3 9.8 %collective-permute-start.6 = (bf16[32,2048]{1,0:T(8,128)(2,1)S(1)}, bf16[32,2048]{1,0:T(8,128)(2,1)S(1)}, u32[]{:S(2)}, u32[]{:S(2)}) collective-permute-start(bf16[32,2048]{1,0:T(8,128)(2,1)S(1)} %slice.180), channel_id=1, source_target_pairs={{0,1},{1,2},{2,3},{3,0},{4,5},{5,6},{6,7},{7,4},{8,9},{9,10},{10,1... | collective-permute-start | bytes 393224 | tf_op jit(solution)/shard_map/ppermute | solution.py:26
  37.5 7.0 %collective-permute-start.9 = (bf16[256,128]{1,0:T(8,128)(2,1)S(1)}, bf16[256,128]{1,0:T(8,128)(2,1)S(1)}, u32[]{:S(2)}, u32[]{:S(2)}) collective-permute-start(bf16[256,128]{1,0:T(8,128)(2,1)S(1)} %shard_map.153.refs_3_), channel_id=1, source_target_pairs={{0,2},{1,3},{2,0},{3,1},{4,6},{5,7},{6,4},{7,5},{8,10},{9,11},{10,... | collective-permute-start | bytes 196616 | tf_op jit(solution)/shard_map/ppermute | solution.py:26
  40.0 4.6 %collective-permute-start.10 = (bf16[256,128]{1,0:T(8,128)(2,1)S(1)}, bf16[256,128]{1,0:T(8,128)(2,1)S(1)}, u32[]{:S(2)}, u32[]{:S(2)}) collective-permute-start(bf16[256,128]{1,0:T(8,128)(2,1)S(1)} %shard_map.153.refs_3_), channel_id=1, source_target_pairs={{0,3},{1,0},{2,1},{3,2},{4,7},{5,4},{6,5},{7,6},{8,11},{9,8},{10,9... | collective-permute-start | bytes 196616 | tf_op jit(solution)/shard_map/ppermute | solution.py:26
  41.6 6.1 %collective-permute-start.8 = (bf16[256,128]{1,0:T(8,128)(2,1)S(1)}, bf16[256,128]{1,0:T(8,128)(2,1)S(1)}, u32[]{:S(2)}, u32[]{:S(2)}) collective-permute-start(bf16[256,128]{1,0:T(8,128)(2,1)S(1)} %shard_map.153.refs_3_), channel_id=1, source_target_pairs={{0,1},{1,2},{2,3},{3,0},{4,5},{5,6},{6,7},{7,4},{8,9},{9,10},{10,1... | collective-permute-start | bytes 196616 | tf_op jit(solution)/shard_map/ppermute | solution.py:26
  48.4 70.6 %all-gather.9.cloned.1.call-start = ((), (), s32[]{:S(2)}) async-start(), calls=%async_computation | async-start | bytes 2359296 | tf_op jit(solution)/shard_map/all_gather | solution.py:749
  51.1 8.1 %collective-permute-start.11 = (bf16[4,256,128]{2,1,0:T(8,128)(2,1)S(1)}, bf16[4,256,128]{2,1,0:T(8,128)(2,1)S(1)}, u32[]{:S(2)}, u32[]{:S(2)}) collective-permute-start(bf16[4,256,128]{2,1,0:T(8,128)(2,1)S(1)} %copy-done.4), channel_id=1, source_target_pairs={{0,4},{4,8},{8,12},{12,16},{16,20},{20,24},{24,28},{28,0},{1,5},{5... | collective-permute-start | bytes 786440 | tf_op jit(solution)/shard_map/ppermute | solution.py:26
  51.1 10.4 %collective-permute-start.12 = (bf16[4,256,128]{2,1,0:T(8,128)(2,1)S(1)}, bf16[4,256,128]{2,1,0:T(8,128)(2,1)S(1)}, u32[]{:S(2)}, u32[]{:S(2)}) collective-permute-start(bf16[4,256,128]{2,1,0:T(8,128)(2,1)S(1)} %copy-done.4), channel_id=1, source_target_pairs={{0,28},{4,0},{8,4},{12,8},{16,12},{20,16},{24,20},{28,24},{1,29},{... | collective-permute-start | bytes 786440 | tf_op jit(solution)/shard_map/ppermute | solution.py:26
  58.0 23.0 %copy-start.9 = (s32[1,8,32]{2,1,0:T(8,128)S(1)}, s32[1,8,32]{2,1,0:T(8,128)}, u32[]{:S(2)}) copy-start(s32[1,8,32]{2,1,0:T(8,128)} %param.17) | copy-start | bytes 3076
  64.3 6.2 %collective-permute-start.13 = (bf16[256,128]{1,0:T(8,128)(2,1)S(1)}, bf16[256,128]{1,0:T(8,128)(2,1)S(1)}, u32[]{:S(2)}, u32[]{:S(2)}) collective-permute-start(bf16[256,128]{1,0:T(8,128)(2,1)S(1)} %get-tuple-element.61.refs_3_), channel_id=1, source_target_pairs={{0,1},{1,2},{2,3},{3,0},{4,5},{5,6},{6,7},{7,4},{8,9},{9,10},{10,1... | collective-permute-start | bytes 196616 | tf_op jit(solution)/shard_map/ppermute | solution.py:26
  64.4 6.2 %collective-permute-start.14 = (bf16[256,128]{1,0:T(8,128)(2,1)S(1)}, bf16[256,128]{1,0:T(8,128)(2,1)S(1)}, u32[]{:S(2)}, u32[]{:S(2)}) collective-permute-start(bf16[256,128]{1,0:T(8,128)(2,1)S(1)} %get-tuple-element.61.refs_3_), channel_id=1, source_target_pairs={{0,2},{1,3},{2,0},{3,1},{4,6},{5,7},{6,4},{7,5},{8,10},{9,11},{10,... | collective-permute-start | bytes 196616 | tf_op jit(solution)/shard_map/ppermute | solution.py:26
  66.7 6.0 %collective-permute-start.15 = (bf16[256,128]{1,0:T(8,128)(2,1)S(1)}, bf16[256,128]{1,0:T(8,128)(2,1)S(1)}, u32[]{:S(2)}, u32[]{:S(2)}) collective-permute-start(bf16[256,128]{1,0:T(8,128)(2,1)S(1)} %get-tuple-element.61.refs_3_), channel_id=1, source_target_pairs={{0,3},{1,0},{2,1},{3,2},{4,7},{5,4},{6,5},{7,6},{8,11},{9,8},{10,9... | collective-permute-start | bytes 196616 | tf_op jit(solution)/shard_map/ppermute | solution.py:26
  73.4 93.5 %all-gather.13.cloned.1.call-start = ((), (), s32[]{:S(2)}) async-start(), calls=%async_computation.2 | async-start | bytes 3981312 | tf_op jit(solution)/shard_map/all_gather | solution.py:780
  73.4 11.7 %collective-permute-start.16 = (bf16[4,256,128]{2,1,0:T(8,128)(2,1)}, bf16[4,256,128]{2,1,0:T(8,128)(2,1)S(1)}, u32[]{:S(2)}, u32[]{:S(2)}) collective-permute-start(bf16[4,256,128]{2,1,0:T(8,128)(2,1)} %pad_maximum_fusion.8.refs_0_), channel_id=1, source_target_pairs={{0,4},{4,8},{8,12},{12,16},{16,20},{20,24},{24,28},{28,0},{1,5},{5... | collective-permute-start | bytes 786440 | tf_op jit(solution)/shard_map/ppermute | solution.py:26
  74.5 10.6 %collective-permute-start.20 = (bf16[4,256,128]{2,1,0:T(8,128)(2,1)}, bf16[4,256,128]{2,1,0:T(8,128)(2,1)S(1)}, u32[]{:S(2)}, u32[]{:S(2)}) collective-permute-start(bf16[4,256,128]{2,1,0:T(8,128)(2,1)} %pad_maximum_fusion.8.refs_0_), channel_id=1, source_target_pairs={{0,28},{4,0},{8,4},{12,8},{16,12},{20,16},{24,20},{28,24},{1,29},{... | collective-permute-start | bytes 786440 | tf_op jit(solution)/shard_map/ppermute | solution.py:26
  76.1 7.8 %collective-permute-start.17 = (bf16[64,512]{1,0:T(8,128)(2,1)S(1)}, bf16[64,512]{1,0:T(8,128)(2,1)S(1)}, u32[]{:S(2)}, u32[]{:S(2)}) collective-permute-start(bf16[64,512]{1,0:T(8,128)(2,1)S(1)} %get-tuple-element.124), channel_id=1, source_target_pairs={{0,1},{1,2},{2,3},{3,0},{4,5},{5,6},{6,7},{7,4},{8,9},{9,10},{10,1... | collective-permute-start | bytes 196616 | tf_op jit(solution)/shard_map/ppermute | solution.py:26
  78.2 6.3 %collective-permute-start.18 = (bf16[64,512]{1,0:T(8,128)(2,1)S(1)}, bf16[64,512]{1,0:T(8,128)(2,1)S(1)}, u32[]{:S(2)}, u32[]{:S(2)}) collective-permute-start(bf16[64,512]{1,0:T(8,128)(2,1)S(1)} %get-tuple-element.123), channel_id=1, source_target_pairs={{0,2},{1,3},{2,0},{3,1},{4,6},{5,7},{6,4},{7,5},{8,10},{9,11},{10,... | collective-permute-start | bytes 196616 | tf_op jit(solution)/shard_map/ppermute | solution.py:26
  80.5 4.6 %collective-permute-start.19 = (bf16[64,512]{1,0:T(8,128)(2,1)S(1)}, bf16[64,512]{1,0:T(8,128)(2,1)S(1)}, u32[]{:S(2)}, u32[]{:S(2)}) collective-permute-start(bf16[64,512]{1,0:T(8,128)(2,1)S(1)} %get-tuple-element.122), channel_id=1, source_target_pairs={{0,3},{1,0},{2,1},{3,2},{4,7},{5,4},{6,5},{7,6},{8,11},{9,8},{10,9... | collective-permute-start | bytes 196616 | tf_op jit(solution)/shard_map/ppermute | solution.py:26
  88.0 7.2 %collective-permute-start.23 = (bf16[256,128]{1,0:T(8,128)(2,1)S(1)}, bf16[256,128]{1,0:T(8,128)(2,1)S(1)}, u32[]{:S(2)}, u32[]{:S(2)}) collective-permute-start(bf16[256,128]{1,0:T(8,128)(2,1)S(1)} %get-tuple-element.63.refs_0_), channel_id=1, source_target_pairs={{0,3},{1,0},{2,1},{3,2},{4,7},{5,4},{6,5},{7,6},{8,11},{9,8},{10,9... | collective-permute-start | bytes 196616 | tf_op jit(solution)/shard_map/ppermute | solution.py:26
  90.1 6.1 %collective-permute-start.21 = (bf16[256,128]{1,0:T(8,128)(2,1)S(1)}, bf16[256,128]{1,0:T(8,128)(2,1)S(1)}, u32[]{:S(2)}, u32[]{:S(2)}) collective-permute-start(bf16[256,128]{1,0:T(8,128)(2,1)S(1)} %get-tuple-element.63.refs_0_), channel_id=1, source_target_pairs={{0,1},{1,2},{2,3},{3,0},{4,5},{5,6},{6,7},{7,4},{8,9},{9,10},{10,1... | collective-permute-start | bytes 196616 | tf_op jit(solution)/shard_map/ppermute | solution.py:26
  90.1 6.1 %collective-permute-start.22 = (bf16[256,128]{1,0:T(8,128)(2,1)S(1)}, bf16[256,128]{1,0:T(8,128)(2,1)S(1)}, u32[]{:S(2)}, u32[]{:S(2)}) collective-permute-start(bf16[256,128]{1,0:T(8,128)(2,1)S(1)} %get-tuple-element.63.refs_0_), channel_id=1, source_target_pairs={{0,2},{1,3},{2,0},{3,1},{4,6},{5,7},{6,4},{7,5},{8,10},{9,11},{10,... | collective-permute-start | bytes 196616 | tf_op jit(solution)/shard_map/ppermute | solution.py:26
  96.9 5.0 %collective-permute-start.26 = (bf16[272,128]{1,0:T(8,128)(2,1)S(1)}, bf16[272,128]{1,0:T(8,128)(2,1)S(1)}, u32[]{:S(2)}, u32[]{:S(2)}) collective-permute-start(bf16[272,128]{1,0:T(8,128)(2,1)S(1)} %get-tuple-element.68), channel_id=1, source_target_pairs={{0,3},{1,0},{2,1},{3,2},{4,7},{5,4},{6,5},{7,6},{8,11},{9,8},{10,9... | collective-permute-start | bytes 208904 | tf_op jit(solution)/shard_map/ppermute | solution.py:26
  99.8 6.2 %collective-permute-start.24 = (bf16[272,128]{1,0:T(8,128)(2,1)S(1)}, bf16[272,128]{1,0:T(8,128)(2,1)S(1)}, u32[]{:S(2)}, u32[]{:S(2)}) collective-permute-start(bf16[272,128]{1,0:T(8,128)(2,1)S(1)} %get-tuple-element.66), channel_id=1, source_target_pairs={{0,1},{1,2},{2,3},{3,0},{4,5},{5,6},{6,7},{7,4},{8,9},{9,10},{10,1... | collective-permute-start | bytes 208904 | tf_op jit(solution)/shard_map/ppermute | solution.py:26
  99.9 7.4 %collective-permute-start.25 = (bf16[272,128]{1,0:T(8,128)(2,1)S(1)}, bf16[272,128]{1,0:T(8,128)(2,1)S(1)}, u32[]{:S(2)}, u32[]{:S(2)}) collective-permute-start(bf16[272,128]{1,0:T(8,128)(2,1)S(1)} %get-tuple-element.67), channel_id=1, source_target_pairs={{0,2},{1,3},{2,0},{3,1},{4,6},{5,7},{6,4},{7,5},{8,10},{9,11},{10,... | collective-permute-start | bytes 208904 | tf_op jit(solution)/shard_map/ppermute | solution.py:26
  129.7 4.3 %collective-permute-start.30 = (bf16[4,64,512]{2,1,0:T(8,128)(2,1)S(1)}, bf16[4,64,512]{2,1,0:T(8,128)(2,1)S(1)}, u32[]{:S(2)}, u32[]{:S(2)}) collective-permute-start(bf16[4,64,512]{2,1,0:T(8,128)(2,1)S(1)} %dynamic-slice_bitcast_fusion), channel_id=1, source_target_pairs={{0,4},{4,0},{8,12},{12,8},{16,20},{20,16},{24,28},{28,24},{1,5},{5... | collective-permute-start | bytes 786440 | tf_op jit(solution)/shard_map/ppermute | solution.py:623
  134.1 9.7 %collective-permute-start.31 = (bf16[2,64,512]{2,1,0:T(8,128)(2,1)S(1)}, bf16[2,64,512]{2,1,0:T(8,128)(2,1)S(1)}, u32[]{:S(2)}, u32[]{:S(2)}) collective-permute-start(bf16[2,64,512]{2,1,0:T(8,128)(2,1)S(1)} %fusion), channel_id=1, source_target_pairs={{0,8},{4,12},{8,0},{12,4},{16,24},{20,28},{24,16},{28,20},{1,9},{5... | collective-permute-start | bytes 393224 | tf_op jit(solution)/shard_map/ppermute | solution.py:623
  134.8 6.8 %collective-permute-start.27 = (bf16[256,128]{1,0:T(8,128)(2,1)S(1)}, bf16[256,128]{1,0:T(8,128)(2,1)S(1)}, u32[]{:S(2)}, u32[]{:S(2)}) collective-permute-start(bf16[256,128]{1,0:T(8,128)(2,1)S(1)} %get-tuple-element.77), channel_id=1, source_target_pairs={{0,1},{1,2},{2,3},{3,0},{4,5},{5,6},{6,7},{7,4},{8,9},{9,10},{10,1... | collective-permute-start | bytes 196616 | tf_op jit(solution)/shard_map/ppermute | solution.py:26
  134.8 8.3 %collective-permute-start.28 = (bf16[256,128]{1,0:T(8,128)(2,1)S(1)}, bf16[256,128]{1,0:T(8,128)(2,1)S(1)}, u32[]{:S(2)}, u32[]{:S(2)}) collective-permute-start(bf16[256,128]{1,0:T(8,128)(2,1)S(1)} %get-tuple-element.78), channel_id=1, source_target_pairs={{0,2},{1,3},{2,0},{3,1},{4,6},{5,7},{6,4},{7,5},{8,10},{9,11},{10,... | collective-permute-start | bytes 196616 | tf_op jit(solution)/shard_map/ppermute | solution.py:26
  137.5 5.6 %collective-permute-start.29 = (bf16[256,128]{1,0:T(8,128)(2,1)S(1)}, bf16[256,128]{1,0:T(8,128)(2,1)S(1)}, u32[]{:S(2)}, u32[]{:S(2)}) collective-permute-start(bf16[256,128]{1,0:T(8,128)(2,1)S(1)} %get-tuple-element.79), channel_id=1, source_target_pairs={{0,3},{1,0},{2,1},{3,2},{4,7},{5,4},{6,5},{7,6},{8,11},{9,8},{10,9... | collective-permute-start | bytes 196616 | tf_op jit(solution)/shard_map/ppermute | solution.py:26
  143.9 12.9 %collective-permute-start.32 = (bf16[1,64,512]{2,1,0:T(8,128)(2,1)S(1)}, bf16[1,64,512]{2,1,0:T(8,128)(2,1)S(1)}, u32[]{:S(2)}, u32[]{:S(2)}) collective-permute-start(bf16[1,64,512]{2,1,0:T(8,128)(2,1)S(1)} %dynamic-slice_convert_fusion), channel_id=1, source_target_pairs={{0,16},{4,20},{8,24},{12,28},{16,0},{20,4},{24,8},{28,12},{1,17},{... | collective-permute-start | bytes 196616 | tf_op jit(solution)/shard_map/ppermute | solution.py:623
  164.7 14.1 %collective-permute-start.33 = (bf16[31,64,128]{2,1,0:T(8,128)(2,1)}, bf16[31,64,128]{2,1,0:T(8,128)(2,1)S(1)}, u32[]{:S(2)}, u32[]{:S(2)}) collective-permute-start(bf16[31,64,128]{2,1,0:T(8,128)(2,1)} %get-tuple-element.88.refs_0_), channel_id=1, source_target_pairs={{0,8},{4,12},{8,0},{12,4},{16,24},{20,28},{24,16},{28,20},{1,9},{5... | collective-permute-start | bytes 1523720 | tf_op jit(solution)/shard_map/ppermute | solution.py:623
  166.2 13.7 %collective-permute-start.34 = (bf16[31,64,128]{2,1,0:T(8,128)(2,1)}, bf16[31,64,128]{2,1,0:T(8,128)(2,1)S(1)}, u32[]{:S(2)}, u32[]{:S(2)}) collective-permute-start(bf16[31,64,128]{2,1,0:T(8,128)(2,1)} %get-tuple-element.88.refs_0_), channel_id=1, source_target_pairs={{0,16},{4,20},{8,24},{12,28},{16,0},{20,4},{24,8},{28,12},{1,17},{... | collective-permute-start | bytes 1523720 | tf_op jit(solution)/shard_map/ppermute | solution.py:623
  166.8 15.8 %collective-permute-start.36 = (bf16[31,64,128]{2,1,0:T(8,128)(2,1)}, bf16[31,64,128]{2,1,0:T(8,128)(2,1)S(1)}, u32[]{:S(2)}, u32[]{:S(2)}) collective-permute-start(bf16[31,64,128]{2,1,0:T(8,128)(2,1)} %get-tuple-element.88.refs_0_), channel_id=1, source_target_pairs={{0,4},{4,0},{8,12},{12,8},{16,20},{20,16},{24,28},{28,24},{1,5},{5... | collective-permute-start | bytes 1523720 | tf_op jit(solution)/shard_map/ppermute | solution.py:623
  168.8 13.8 %copy-start.8 = (bf16[31,64,128]{2,1,0:T(8,128)(2,1)S(1)}, bf16[31,64,128]{2,1,0:T(8,128)(2,1)}, u32[]{:S(2)}) copy-start(bf16[31,64,128]{2,1,0:T(8,128)(2,1)} %get-tuple-element.88.refs_0_) | copy-start | bytes 1523716
  179.9 2.7 %collective-permute-start.37 = (bf16[31,64,128]{2,1,0:T(8,128)(2,1)S(1)}, bf16[31,64,128]{2,1,0:T(8,128)(2,1)S(1)}, u32[]{:S(2)}, u32[]{:S(2)}) collective-permute-start(bf16[31,64,128]{2,1,0:T(8,128)(2,1)S(1)} %collective-permute-done.33.refs_1_), channel_id=1, source_target_pairs={{0,4},{4,0},{8,12},{12,8},{16,20},{20,16},{24,28},{28,24},{1,5},{5... | collective-permute-start | bytes 1523720 | tf_op jit(solution)/shard_map/ppermute | solution.py:623
  179.9 2.7 %collective-permute-start.38 = (bf16[31,64,128]{2,1,0:T(8,128)(2,1)S(1)}, bf16[31,64,128]{2,1,0:T(8,128)(2,1)S(1)}, u32[]{:S(2)}, u32[]{:S(2)}) collective-permute-start(bf16[31,64,128]{2,1,0:T(8,128)(2,1)S(1)} %collective-permute-done.34.refs_2_), channel_id=1, source_target_pairs={{0,4},{4,0},{8,12},{12,8},{16,20},{20,16},{24,28},{28,24},{1,5},{5... | collective-permute-start | bytes 1523720 | tf_op jit(solution)/shard_map/ppermute | solution.py:623
  180.5 8.3 %collective-permute-start.39 = (bf16[16,64,128]{2,1,0:T(8,128)(2,1)S(1)}, bf16[16,64,128]{2,1,0:T(8,128)(2,1)S(1)}, u32[]{:S(2)}, u32[]{:S(2)}) collective-permute-start(bf16[16,64,128]{2,1,0:T(8,128)(2,1)S(1)} %slice.155), channel_id=1, source_target_pairs={{0,16},{4,20},{8,24},{12,28},{16,0},{20,4},{24,8},{28,12},{1,17},{... | collective-permute-start | bytes 786440 | tf_op jit(solution)/shard_map/ppermute | solution.py:623
  181.2 7.6 %collective-permute-start.35 = (bf16[15,64,128]{2,1,0:T(8,128)(2,1)S(1)}, bf16[15,64,128]{2,1,0:T(8,128)(2,1)S(1)}, u32[]{:S(2)}, u32[]{:S(2)}) collective-permute-start(bf16[15,64,128]{2,1,0:T(8,128)(2,1)S(1)} %slice.154), channel_id=1, source_target_pairs={{0,8},{4,12},{8,0},{12,4},{16,24},{20,28},{24,16},{28,20},{1,9},{5... | collective-permute-start | bytes 737288 | tf_op jit(solution)/shard_map/ppermute | solution.py:623
  188.8 1.9 collective-permute-start.41
  188.8 1.8 collective-permute-start.40
  (7 other events, 24.3 us)
Sparse Core Ops, SparseCore 0:
  48.5 27.6 all-gather.10
  78.7 27.6 all-gather.8
  129.8 34.0 all-gather.12

commit v4 on v3

--- a/solution.py
+++ b/solution.py
@@ -420,6 +420,26 @@
     )(axis_word("ch"), *arrays)
 
 
+def fill_slots(word_ref, held, slots, rows, rows_z):
+    each, planes, _, lane = slots.shape
+    points = held.shape[1]
+    offset = lax.rem(word_ref[0] * rows, lane)
+    lanes = lax.broadcasted_iota(jnp.int32, (points, lane), 1)
+
+    def prepare(plane, carry):
+        own = held[plane].astype(FLOAT)
+        for slot in range(each):
+            moved = pltpu.roll(own, lax.rem(slot * rows - offset + lane, lane), 1)
+            inside = (lanes >= slot * rows) & (lanes < (slot + 1) * rows)
+            moved = jnp.where(inside, moved, 0.0).astype(HALF)
+            slots[slot, plane, rows_z : rows_z + points] = moved
+            slots[slot, plane, :rows_z] = moved[points - rows_z :]
+            slots[slot, plane, rows_z + points :] = moved[:rows_z]
+        return carry
+
+    lax.fori_loop(0, planes, prepare, 0)
+
+
 def spread_slots(every, rows, rows_y, rows_z):
     planes, count, points, lane = every.shape
     each = lane // rows
@@ -427,22 +447,8 @@
     def kernel(word_ref, every_ref, slots, held, sem):
         read = pltpu.make_async_copy(every_ref.at[:, word_ref[1]], held, sem)
         read.start()
-        offset = lax.rem(word_ref[0] * rows, lane)
-        lanes = lax.broadcasted_iota(jnp.int32, (points, lane), 1)
         read.wait()
-
-        def prepare(plane, carry):
-            own = held[plane].astype(FLOAT)
-            for slot in range(each):
-                moved = pltpu.roll(own, lax.rem(slot * rows - offset + lane, lane), 1)
-                inside = (lanes >= slot * rows) & (lanes < (slot + 1) * rows)
-                moved = jnp.where(inside, moved, 0.0).astype(HALF)
-                slots[slot, plane, rows_z : rows_z + points] = moved
-                slots[slot, plane, :rows_z] = moved[points - rows_z :]
-                slots[slot, plane, rows_z + points :] = moved[:rows_z]
-            return carry
-
-        lax.fori_loop(0, planes, prepare, 0)
+        fill_slots(word_ref, held, slots, rows, rows_z)
 
     shape = (each, planes, points + 2 * rows_z, lane)
     place = axis_word(SPLIT)
@@ -459,9 +465,14 @@
 
 
 def kernel_step(slots, errors, counted, states, layer, kept, dec, rows_y, rows_z):
-    each, planes, _, lane = slots.shape
     points, cols = rows_y * rows_z, errors.shape[2]
     rows = states[1].shape[2]
+    raw = slots.shape[2] == points
+    if raw:
+        planes, _, _, lane = slots.shape
+        each = lane // rows
+    else:
+        each, planes, _, lane = slots.shape
     blocks = -(-9 // each)
     solo = 2 * bool(dec)
     more = dec[1].shape[1] // cols if dec else 0
@@ -471,7 +482,10 @@
         dec_refs = refs[: len(dec)]
         refs = refs[len(dec) + len(kept) :]
         new_w, m_out, v_out, loss_ref, *dec_outs = refs[: 4 + solo]
-        w_ref, m_ref, v_ref, new_m, new_v, total, sems, out_sems = refs[4 + solo :]
+        w_ref, m_ref, v_ref, new_m, new_v, total, sems, out_sems, *rest = refs[4 + solo :]
+        if raw:
+            first_read = pltpu.make_async_copy(slots_ref.at[:, word_ref[1]], rest[1], rest[2])
+            first_read.start()
         reads = [
             pltpu.make_async_copy(
                 w_hbm.at[layer, :, pl.ds(pl.multiple_of(word_ref[0] * rows, rows), rows)],
@@ -484,6 +498,10 @@
         for read in reads:
             read.start()
         total[...] = jnp.zeros_like(total)
+        if raw:
+            slots_ref = rest[0]
+            first_read.wait()
+            fill_slots(word_ref, rest[1], slots_ref, rows, rows_z)
 
         def gather(plane, carry):
             left = []
@@ -552,6 +570,15 @@
 
     any_spec = pl.BlockSpec(memory_space=pl.ANY)
     hbm_spec = pl.BlockSpec(memory_space=pltpu.HBM)
+    place, count = axis_word(SPLIT), lax.axis_size("ch")
+    word = jnp.concatenate([place, (axis_word("ch") - place * rows // lane + count) % count])
+    raw_scratch = []
+    if raw:
+        raw_scratch = [
+            pltpu.VMEM((each, planes, points + 2 * rows_z, lane), HALF),
+            pltpu.VMEM((planes, points, lane), HALF),
+            pltpu.SemaphoreType.DMA,
+        ]
     dec_specs = []
     if dec:
         flat = whole_spec(dec[2].shape)
@@ -569,7 +596,7 @@
             num_scalar_prefetch=1,
             grid=(1,),
             in_specs=[
-                whole_spec(slots.shape),
+                hbm_spec if raw else whole_spec(slots.shape),
                 whole_spec(errors.shape),
                 pl.BlockSpec((planes, 16, cols), lambda step, word: (0, points // 16, 0)),
                 hbm_spec,
@@ -594,12 +621,13 @@
                 pltpu.VMEM((blocks * lane, 3 * cols), FLOAT),
                 pltpu.SemaphoreType.DMA((3,)),
                 pltpu.SemaphoreType.DMA((2 * 27 // chunk,)),
-            ],
+            ]
+            + raw_scratch,
         ),
         out_shape=outs,
         input_output_aliases={first: 1, first + 1: 2} if kept else {},
         compiler_params=FULL,
-    )(axis_word(SPLIT), slots, errors, counted, *states, *dec, *kept)
+    )(word, slots, errors, counted, *states, *dec, *kept)
 
 
 def settle(gathered, shape, layer):
@@ -762,7 +790,6 @@
     pieces = sent(pieces)
     pieces[-1] = after(pieces[-1], send)
     d_act_two, d_pre_two = step_back(back, pieces, pre_two, sums)
-    slots_two = spread_slots(rows_two, conv_rows, rows_y, rows_z)
     errors_two = lax.all_gather(d_pre_two, SPLIT, axis=0)
     back, *pieces = conv_back(errors_two, conv_w, 1, rows_y, rows_z, count)
     _, d_pre_one = step_back(back, sent(pieces), pre_one, d_act_two)
@@ -772,7 +799,7 @@
     states = (conv_w, conv_m, conv_v)
     dec = (grad_dec, dec_w, dec_m, dec_v)
     two_shard, m_next, v_next, loss = kernel_step(
-        slots_two, errors_two, errors_two, states, 1, (), (), rows_y, rows_z
+        rows_two, errors_two, errors_two, states, 1, (), (), rows_y, rows_z
     )
     one_shard, m_next, v_next, _, dec_m_next, dec_v_next = kernel_step(
         slots_one, errors_one, errors_two, states, 0, (m_next, v_next), dec, rows_y, rows_z

time: 199 us -> 198 us (level)
    pallas_call x2 -> x1, Pallas kernels: 7.26 us -> 3.62 us  [spread_slots(): pl.pallas_call(kernel, grid=(1,), in_specs=[pl.BlockSpec(memory_space=plt...]
    pallas_call x2, Pallas kernels: 14.2 us -> 17.4 us  [kernel_step(): pl.pallas_call(kernel, grid_spec=pltpu.PrefetchScalarGridSpec(num_scalar_...]
where the time goes in v4:
time: 198 us
  starting transfers between devices  53.3 us (27%)
  waiting for transfers between devices  49.9 us (25%)
  Pallas kernels  44.2 us (22%)
  blocking collectives  23.2 us (12%)
  between operations  14.2 us (7%)
  local copies, waits for them, and re-layouts  7.15 us (4%)
  other arithmetic  5.59 us (3%)
    ppermute x30, starting transfers between devices, shift(): lax.ppermute(block, axis, [(i, (i + by) % count) for i in range(count)])  45.4 us
    ppermute x30, waiting for transfers between devices, shift(): lax.ppermute(block, axis, [(i, (i + by) % count) for i in range(count)])  37.5 us
    pallas_call x2, Pallas kernels, kernel_step(): pl.pallas_call(kernel, grid_spec=pltpu.PrefetchScalarGridSpec(num_scalar_...  17.4 us
    ppermute x12, waiting for transfers between devices, cross(): return lax.ppermute(block, SPLIT, [(i, i ^ mask) for i in range(count)])  12.3 us
    all_gather x1, blocking collectives, body(): errors_two = lax.all_gather(d_pre_two, SPLIT, axis=0)  11.7 us
    all_gather x1, blocking collectives, body(): errors_one = lax.all_gather(d_pre_one, SPLIT, axis=0)  11.4 us
    pallas_call x4, Pallas kernels, conv_planes(): pl.pallas_call(kernel, grid=(1,), out_shape=outs, in_specs=[pl.BlockSpec(...  9.34 us
    ppermute x12, starting transfers between devices, cross(): return lax.ppermute(block, SPLIT, [(i, i ^ mask) for i in range(count)])  7.78 us
  transfers between devices with their start and end apart: 45, of which 25 were waited for; matrix products, arithmetic and copies ran while one was open for 4% of the time, Pallas kernels for 16%

profile of v4, /device:TPU:0, one launch (start us, length us, event | category | flops | bytes accessed | tf_op | source)
XLA Modules:
  0.0 197.8 jit_solution(11970455929865587731)
XLA Ops:
  9.8 4.7 %collective-permute-start.5 = (bf16[64,2048]{1,0:T(8,128)(2,1)S(1)}, bf16[64,2048]{1,0:T(8,128)(2,1)S(1)}, u32[]{:S(2)}, u32[]{:S(2)}) collective-permute-start(bf16[64,2048]{1,0:T(8,128)(2,1)S(1)} %shard_map.152.refs_0_), channel_id=1, source_target_pairs={{0,3},{1,0},{2,1},{3,2},{4,7},{5,4},{6,5},{7,6},{8,11},{9,8},{10,9... | collective-permute-start | bytes 786440 | tf_op jit(solution)/shard_map/ppermute | solution.py:26
  14.5 2.3 %collective-permute-start.1 = (f32[4,2,16,256]{3,2,1,0:T(8,128)S(1)}, f32[4,2,16,256]{3,2,1,0:T(8,128)S(1)}, u32[]{:S(2)}, u32[]{:S(2)}) collective-permute-start(f32[4,2,16,256]{3,2,1,0:T(8,128)S(1)} %get-tuple-element.56), channel_id=1, source_target_pairs={{0,28},{4,0},{8,4},{12,8},{16,12},{20,16},{24,20},{28,24},{1,29},{... | collective-permute-start | bytes 393224 | tf_op jit(solution)/shard_map/ppermute | solution.py:26
  16.8 2.4 %collective-permute-done.1 = f32[4,2,16,256]{3,2,1,0:T(8,128)S(1)} collective-permute-done((f32[4,2,16,256]{3,2,1,0:T(8,128)S(1)}, f32[4,2,16,256]{3,2,1,0:T(8,128)S(1)}, u32[]{:S(2)}, u32[]{:S(2)}) %collective-permute-start.1) | collective-permute-done | bytes 131104 | tf_op jit(solution)/shard_map/ppermute | solution.py:26
  19.4 3.8 %collective-permute-start.3 = (f32[4,12,2,256]{3,2,1,0:T(2,128)S(1)}, f32[4,12,2,256]{3,2,1,0:T(2,128)S(1)}, u32[]{:S(2)}, u32[]{:S(2)}) collective-permute-start(f32[4,12,2,256]{3,2,1,0:T(2,128)S(1)} %get-tuple-element.58), channel_id=1, source_target_pairs={{0,3},{1,0},{2,1},{3,2},{4,7},{5,4},{6,5},{7,6},{8,11},{9,8},{10,9... | collective-permute-start | bytes 294920 | tf_op jit(solution)/shard_map/ppermute | solution.py:26
  23.3 1.8 collective-permute-start.7
  25.1 2.2 %collective-permute-done.4.refs_1_ = bf16[64,2048]{1,0:T(8,128)(2,1)S(1)} collective-permute-done((bf16[64,2048]{1,0:T(8,128)(2,1)S(1)}, bf16[64,2048]{1,0:T(8,128)(2,1)S(1)}, u32[]{:S(2)}, u32[]{:S(2)}) %collective-permute-start.4) | collective-permute-done | bytes 262176 | tf_op jit(solution)/shard_map/ppermute | solution.py:26
  27.3 1.5 collective-permute-start.6
  29.4 2.5 %collective-permute-done.3 = f32[4,12,2,256]{3,2,1,0:T(2,128)S(1)} collective-permute-done((f32[4,12,2,256]{3,2,1,0:T(2,128)S(1)}, f32[4,12,2,256]{3,2,1,0:T(2,128)S(1)}, u32[]{:S(2)}, u32[]{:S(2)}) %collective-permute-start.3) | collective-permute-done | bytes 98336 | tf_op jit(solution)/shard_map/ppermute | solution.py:26
  32.1 3.1 %collective-permute-done.7.refs_4_ = bf16[32,2048]{1,0:T(8,128)(2,1)S(1)} collective-permute-done((bf16[32,2048]{1,0:T(8,128)(2,1)S(1)}, bf16[32,2048]{1,0:T(8,128)(2,1)S(1)}, u32[]{:S(2)}, u32[]{:S(2)}) %collective-permute-start.7) | collective-permute-done | bytes 131104 | tf_op jit(solution)/shard_map/ppermute | solution.py:26
  35.2 1.8 collective-permute-done.6.refs_3_
  37.5 2.5 %collective-permute-start.9 = (bf16[256,128]{1,0:T(8,128)(2,1)S(1)}, bf16[256,128]{1,0:T(8,128)(2,1)S(1)}, u32[]{:S(2)}, u32[]{:S(2)}) collective-permute-start(bf16[256,128]{1,0:T(8,128)(2,1)S(1)} %shard_map.153.refs_3_), channel_id=1, source_target_pairs={{0,2},{1,3},{2,0},{3,1},{4,6},{5,7},{6,4},{7,5},{8,10},{9,11},{10,... | collective-permute-start | bytes 196616 | tf_op jit(solution)/shard_map/ppermute | solution.py:26
  40.0 1.5 collective-permute-start.10
  42.0 2.5 %collective-permute-done.9 = bf16[256,128]{1,0:T(8,128)(2,1)S(1)} collective-permute-done((bf16[256,128]{1,0:T(8,128)(2,1)S(1)}, bf16[256,128]{1,0:T(8,128)(2,1)S(1)}, u32[]{:S(2)}, u32[]{:S(2)}) %collective-permute-start.9) | collective-permute-done | bytes 65568 | tf_op jit(solution)/shard_map/ppermute | solution.py:26
  44.6 3.0 %collective-permute-done.8 = bf16[256,128]{1,0:T(8,128)(2,1)S(1)} collective-permute-done((bf16[256,128]{1,0:T(8,128)(2,1)S(1)}, bf16[256,128]{1,0:T(8,128)(2,1)S(1)}, u32[]{:S(2)}, u32[]{:S(2)}) %collective-permute-start.8) | collective-permute-done | bytes 65568 | tf_op jit(solution)/shard_map/ppermute | solution.py:26
  51.1 2.6 %collective-permute-start.12 = (bf16[4,256,128]{2,1,0:T(8,128)(2,1)S(1)}, bf16[4,256,128]{2,1,0:T(8,128)(2,1)S(1)}, u32[]{:S(2)}, u32[]{:S(2)}) collective-permute-start(bf16[4,256,128]{2,1,0:T(8,128)(2,1)S(1)} %copy-done.4), channel_id=1, source_target_pairs={{0,28},{4,0},{8,4},{12,8},{16,12},{20,16},{24,20},{28,24},{1,29},{... | collective-permute-start | bytes 786440 | tf_op jit(solution)/shard_map/ppermute | solution.py:26
  53.8 1.4 convert_subtract_fusion
  56.1 1.9 shard_map.154.refs_4_
  58.0 1.2 collective-permute-done.11.refs_0_
  59.2 2.3 %collective-permute-done.12.refs_1_ = bf16[4,256,128]{2,1,0:T(8,128)(2,1)S(1)} collective-permute-done((bf16[4,256,128]{2,1,0:T(8,128)(2,1)S(1)}, bf16[4,256,128]{2,1,0:T(8,128)(2,1)S(1)}, u32[]{:S(2)}, u32[]{:S(2)}) %collective-permute-start.12) | collective-permute-done | bytes 262176 | tf_op jit(solution)/shard_map/ppermute | solution.py:26
  61.5 2.8 %shard_map.156 = (f32[256,128]{1,0:T(8,128)S(1)}, bf16[256,128]{1,0:T(8,128)(2,1)S(1)}) custom-call(s32[1]{0:T(128)} %bitcast.7.own_ref, bf16[4,256,128]{2,1,0:T(8,128)(2,1)S(1)} %collective-permute-done.11.refs_0_, bf16[4,256,128]{2,1,0:T(8,128)(2,1)S(1)} %collective-permute-done.12.refs_1_, bf16[2,27,512,128]{3,2,1,0:T(8,128)(2,1)} %w_hbm.3, ...), custom_call_target="tpu_custom_call" | custom-call | tf_op jit(solution)/shard_map/pallas_call | solution.py:223
  64.4 2.3 %collective-permute-start.14 = (bf16[256,128]{1,0:T(8,128)(2,1)S(1)}, bf16[256,128]{1,0:T(8,128)(2,1)S(1)}, u32[]{:S(2)}, u32[]{:S(2)}) collective-permute-start(bf16[256,128]{1,0:T(8,128)(2,1)S(1)} %get-tuple-element.61.refs_3_), channel_id=1, source_target_pairs={{0,2},{1,3},{2,0},{3,1},{4,6},{5,7},{6,4},{7,5},{8,10},{9,11},{10,... | collective-permute-start | bytes 196616 | tf_op jit(solution)/shard_map/ppermute | solution.py:26
  66.7 2.8 %collective-permute-start.15 = (bf16[256,128]{1,0:T(8,128)(2,1)S(1)}, bf16[256,128]{1,0:T(8,128)(2,1)S(1)}, u32[]{:S(2)}, u32[]{:S(2)}) collective-permute-start(bf16[256,128]{1,0:T(8,128)(2,1)S(1)} %get-tuple-element.61.refs_3_), channel_id=1, source_target_pairs={{0,3},{1,0},{2,1},{3,2},{4,7},{5,4},{6,5},{7,6},{8,11},{9,8},{10,9... | collective-permute-start | bytes 196616 | tf_op jit(solution)/shard_map/ppermute | solution.py:26
  70.5 2.1 %collective-permute-done.15 = bf16[256,128]{1,0:T(8,128)(2,1)S(1)} collective-permute-done((bf16[256,128]{1,0:T(8,128)(2,1)S(1)}, bf16[256,128]{1,0:T(8,128)(2,1)S(1)}, u32[]{:S(2)}, u32[]{:S(2)}) %collective-permute-start.15) | collective-permute-done | bytes 65568 | tf_op jit(solution)/shard_map/ppermute | solution.py:26
  74.5 1.6 collective-permute-start.20
  76.1 2.0 %collective-permute-start.17 = (bf16[64,512]{1,0:T(8,128)(2,1)S(1)}, bf16[64,512]{1,0:T(8,128)(2,1)S(1)}, u32[]{:S(2)}, u32[]{:S(2)}) collective-permute-start(bf16[64,512]{1,0:T(8,128)(2,1)S(1)} %get-tuple-element.124), channel_id=1, source_target_pairs={{0,1},{1,2},{2,3},{3,0},{4,5},{5,6},{6,7},{7,4},{8,9},{9,10},{10,1... | collective-permute-start | bytes 196616 | tf_op jit(solution)/shard_map/ppermute | solution.py:26
  78.2 2.3 %collective-permute-start.18 = (bf16[64,512]{1,0:T(8,128)(2,1)S(1)}, bf16[64,512]{1,0:T(8,128)(2,1)S(1)}, u32[]{:S(2)}, u32[]{:S(2)}) collective-permute-start(bf16[64,512]{1,0:T(8,128)(2,1)S(1)} %get-tuple-element.123), channel_id=1, source_target_pairs={{0,2},{1,3},{2,0},{3,1},{4,6},{5,7},{6,4},{7,5},{8,10},{9,11},{10,... | collective-permute-start | bytes 196616 | tf_op jit(solution)/shard_map/ppermute | solution.py:26
  82.0 1.9 shard_map.157.refs_4_
  85.1 2.8 %shard_map.158 = (f32[256,128]{1,0:T(8,128)S(1)}, bf16[256,128]{1,0:T(8,128)(2,1)S(1)}) custom-call(s32[1]{0:T(128)} %bitcast.7.own_ref, bf16[4,256,128]{2,1,0:T(8,128)(2,1)S(1)} %collective-permute-done.16.refs_0_, bf16[4,256,128]{2,1,0:T(8,128)(2,1)S(1)} %collective-permute-done.20.refs_1_, bf16[2,27,512,128]{3,2,1,0:T(8,128)(2,1)} %w_hbm.3, ...), custom_call_target="tpu_custom_call" | custom-call | tf_op jit(solution)/shard_map/pallas_call | solution.py:223
  88.0 2.2 %collective-permute-start.23 = (bf16[256,128]{1,0:T(8,128)(2,1)S(1)}, bf16[256,128]{1,0:T(8,128)(2,1)S(1)}, u32[]{:S(2)}, u32[]{:S(2)}) collective-permute-start(bf16[256,128]{1,0:T(8,128)(2,1)S(1)} %get-tuple-element.63.refs_0_), channel_id=1, source_target_pairs={{0,3},{1,0},{2,1},{3,2},{4,7},{5,4},{6,5},{7,6},{8,11},{9,8},{10,9... | collective-permute-start | bytes 196616 | tf_op jit(solution)/shard_map/ppermute | solution.py:26
  91.6 3.6 %shard_map.159.slots_ref = bf16[2,8,320,128]{3,2,1,0:T(8,128)(2,1)} custom-call(s32[2]{0:T(128)} %pad_add_fusion.word_ref, bf16[8,4,256,128]{3,2,1,0:T(8,128)(2,1)} %bitcast.59), custom_call_target="tpu_custom_call" | custom-call | tf_op jit(solution)/shard_map/pallas_call | solution.py:456
  96.9 2.9 %collective-permute-start.26 = (bf16[272,128]{1,0:T(8,128)(2,1)S(1)}, bf16[272,128]{1,0:T(8,128)(2,1)S(1)}, u32[]{:S(2)}, u32[]{:S(2)}) collective-permute-start(bf16[272,128]{1,0:T(8,128)(2,1)S(1)} %get-tuple-element.68), channel_id=1, source_target_pairs={{0,3},{1,0},{2,1},{3,2},{4,7},{5,4},{6,5},{7,6},{8,11},{9,8},{10,9... | collective-permute-start | bytes 208904 | tf_op jit(solution)/shard_map/ppermute | solution.py:26
  101.9 4.2 %collective-permute-done.24.refs_0_ = bf16[272,128]{1,0:T(8,128)(2,1)S(1)} collective-permute-done((bf16[272,128]{1,0:T(8,128)(2,1)S(1)}, bf16[272,128]{1,0:T(8,128)(2,1)S(1)}, u32[]{:S(2)}, u32[]{:S(2)}) %collective-permute-start.24) | collective-permute-done | bytes 69664 | tf_op jit(solution)/shard_map/ppermute | solution.py:26
  107.3 11.7 %all-gather.2 = bf16[2176,128]{1,0:T(8,128)(2,1)} all-gather(bf16[272,128]{1,0:T(8,128)(2,1)S(1)} %get-tuple-element.74), channel_id=4, replica_groups=mesh['grp'=2,'sp'=4,'ch'=4] {'grp','sp'}, dimensions={0}, use_global_device_ids=true | all-gather | bytes 626688 | tf_op jit(solution)/shard_map/all_gather | solution.py:793
  119.1 9.5 %shard_map.162 = (bf16[27,64,128]{2,1,0:T(8,128)(2,1)}, f32[2,27,64,128]{3,2,1,0:T(8,128)}, f32[2,27,64,128]{3,2,1,0:T(8,128)}, f32[8,128]{1,0:T(8,128)}) custom-call(s32[2]{0:T(128)} %pad_add_fusion.word_ref, bf16[8,4,256,128]{3,2,1,0:T(8,128)(2,1)} %bitcast.62, bf16[8,272,128]{2,1,0:T(8,128)(2,1)} %bitcast.49, bf16[8,272,128]{2,1,0:T(8,128)(2,1)} %bitcast.50, ...), custom_call_target="tpu_custom_call" | custom-call | tf_op jit(solution)/shard_map/pallas_call | solution.py:593
  129.1 3.8 %shard_map.163 = (f32[256,128]{1,0:T(8,128)S(1)}, bf16[256,128]{1,0:T(8,128)(2,1)S(1)}, bf16[256,128]{1,0:T(8,128)(2,1)S(1)}, bf16[256,128]{1,0:T(8,128)(2,1)S(1)}) custom-call(s32[2]{0:T(128)S(1)} %pad_add_fusion.1.own_ref, bf16[8,272,128]{2,1,0:T(8,128)(2,1)S(1)} %bitcast.52, bf16[8,272,128]{2,1,0:T(8,128)(2,1)S(1)} %bitcast.53, ...), custom_call_target="tpu_custom_call" | custom-call | tf_op jit(solution)/shard_map/pallas_call | solution.py:309
  133.7 2.7 %collective-permute-start.28 = (bf16[256,128]{1,0:T(8,128)(2,1)S(1)}, bf16[256,128]{1,0:T(8,128)(2,1)S(1)}, u32[]{:S(2)}, u32[]{:S(2)}) collective-permute-start(bf16[256,128]{1,0:T(8,128)(2,1)S(1)} %get-tuple-element.78), channel_id=1, source_target_pairs={{0,2},{1,3},{2,0},{3,1},{4,6},{5,7},{6,4},{7,5},{8,10},{9,11},{10,... | collective-permute-start | bytes 196616 | tf_op jit(solution)/shard_map/ppermute | solution.py:26
  137.6 2.9 %collective-permute-done.27.refs_0_ = bf16[256,128]{1,0:T(8,128)(2,1)S(1)} collective-permute-done((bf16[256,128]{1,0:T(8,128)(2,1)S(1)}, bf16[256,128]{1,0:T(8,128)(2,1)S(1)}, u32[]{:S(2)}, u32[]{:S(2)}) %collective-permute-start.27) | collective-permute-done | bytes 65568 | tf_op jit(solution)/shard_map/ppermute | solution.py:26
  140.5 1.6 collective-permute-done.28.refs_1_
  142.9 1.5 collective-permute-start.32
  144.4 11.4 %all-gather.3 = bf16[2048,128]{1,0:T(8,128)(2,1)} all-gather(bf16[256,128]{1,0:T(8,128)(2,1)S(1)} %get-tuple-element.82), channel_id=5, replica_groups=mesh['grp'=2,'sp'=4,'ch'=4] {'grp','sp'}, dimensions={0}, use_global_device_ids=true | all-gather | bytes 589824 | tf_op jit(solution)/shard_map/all_gather | solution.py:796
  156.5 7.8 %shard_map.165 = (bf16[31,64,128]{2,1,0:T(8,128)(2,1)}, f32[2,27,64,128]{3,2,1,0:T(8,128)}, f32[2,27,64,128]{3,2,1,0:T(8,128)}, f32[8,128]{1,0:T(8,128)}, f32[64,512]{1,0:T(8,128)}, /*index=5*/f32[64,512]{1,0:T(8,128)}) custom-call(s32[2]{0:T(128)} %pad_add_fusion.word_ref, ...), custom_call_target="tpu_custom_call", output_to_operand_aliasing={{1}: (11, {}), {2}: (12, {})} | custom-call | tf_op jit(solution)/shard_map/pallas_call | solution.py:593
  164.3 1.5 collective-permute-start.33
  166.4 2.0 %copy-done.3 = bf16[216,64,128]{2,1,0:T(8,128)(2,1)S(1)} copy-done((bf16[216,64,128]{2,1,0:T(8,128)(2,1)S(1)}, bf16[216,64,128]{2,1,0:T(8,128)(2,1)}, u32[]{:S(2)}) %copy-start.3) | copy-done | bytes 3538968
  168.4 3.3 %shard_map.166.refs_6_ = bf16[2,27,512,128]{3,2,1,0:T(8,128)(2,1)} custom-call(bf16[8,27,64,128]{3,2,1,0:T(8,128)(2,1)S(1)} %bitcast.55), custom_call_target="tpu_custom_call" | custom-call | tf_op jit(solution)/shard_map/pallas_call | solution.py:639
  171.7 6.7 %collective-permute-done.33.refs_1_ = bf16[31,64,128]{2,1,0:T(8,128)(2,1)S(1)} collective-permute-done((bf16[31,64,128]{2,1,0:T(8,128)(2,1)}, bf16[31,64,128]{2,1,0:T(8,128)(2,1)S(1)}, u32[]{:S(2)}, u32[]{:S(2)}) %collective-permute-start.33) | collective-permute-done | bytes 507936 | tf_op jit(solution)/shard_map/ppermute | solution.py:651
  180.8 1.5 collective-permute-start.35
  182.3 1.9 shard_map.167
  184.2 4.2 %collective-permute-done.39.refs_1_ = bf16[16,64,128]{2,1,0:T(8,128)(2,1)S(1)} collective-permute-done((bf16[16,64,128]{2,1,0:T(8,128)(2,1)S(1)}, bf16[16,64,128]{2,1,0:T(8,128)(2,1)S(1)}, u32[]{:S(2)}, u32[]{:S(2)}) %collective-permute-start.39) | collective-permute-done | bytes 262176 | tf_op jit(solution)/shard_map/ppermute | solution.py:651
  (117 shorter events, 30.8 us)
Async XLA Ops:
  7.2 78.0 %all-gather.11.cloned.1.call-start = ((), (), s32[]{:S(2)}) async-start(), calls=%async_computation.1 | async-start | bytes 2359296 | tf_op jit(solution)/shard_map/all_gather | solution.py:773
  9.3 7.5 %collective-permute-start = (f32[4,2,16,256]{3,2,1,0:T(8,128)S(1)}, f32[4,2,16,256]{3,2,1,0:T(8,128)S(1)}, u32[]{:S(2)}, u32[]{:S(2)}) collective-permute-start(f32[4,2,16,256]{3,2,1,0:T(8,128)S(1)} %get-tuple-element.55), channel_id=1, source_target_pairs={{0,4},{4,8},{8,12},{12,16},{16,20},{20,24},{24,28},{28,0},{1,5},{5... | collective-permute-start | bytes 393224 | tf_op jit(solution)/shard_map/ppermute | solution.py:26
  9.8 13.5 %collective-permute-start.5 = (bf16[64,2048]{1,0:T(8,128)(2,1)S(1)}, bf16[64,2048]{1,0:T(8,128)(2,1)S(1)}, u32[]{:S(2)}, u32[]{:S(2)}) collective-permute-start(bf16[64,2048]{1,0:T(8,128)(2,1)S(1)} %shard_map.152.refs_0_), channel_id=1, source_target_pairs={{0,3},{1,0},{2,1},{3,2},{4,7},{5,4},{6,5},{7,6},{8,11},{9,8},{10,9... | collective-permute-start | bytes 786440 | tf_op jit(solution)/shard_map/ppermute | solution.py:26
  14.5 12.8 %collective-permute-start.4 = (bf16[64,2048]{1,0:T(8,128)(2,1)S(1)}, bf16[64,2048]{1,0:T(8,128)(2,1)S(1)}, u32[]{:S(2)}, u32[]{:S(2)}) collective-permute-start(bf16[64,2048]{1,0:T(8,128)(2,1)S(1)} %shard_map.152.refs_0_), channel_id=1, source_target_pairs={{0,1},{1,2},{2,3},{3,0},{4,5},{5,6},{6,7},{7,4},{8,9},{9,10},{10,1... | collective-permute-start | bytes 786440 | tf_op jit(solution)/shard_map/ppermute | solution.py:26
  14.5 4.8 %collective-permute-start.1 = (f32[4,2,16,256]{3,2,1,0:T(8,128)S(1)}, f32[4,2,16,256]{3,2,1,0:T(8,128)S(1)}, u32[]{:S(2)}, u32[]{:S(2)}) collective-permute-start(f32[4,2,16,256]{3,2,1,0:T(8,128)S(1)} %get-tuple-element.56), channel_id=1, source_target_pairs={{0,28},{4,0},{8,4},{12,8},{16,12},{20,16},{24,20},{28,24},{1,29},{... | collective-permute-start | bytes 393224 | tf_op jit(solution)/shard_map/ppermute | solution.py:26
  16.8 20.2 %copy-start.7 = (bf16[2048,128]{1,0:T(8,128)(2,1)S(1)}, bf16[2048,128]{1,0:T(8,128)(2,1)}, u32[]{:S(2)}) copy-start(bf16[2048,128]{1,0:T(8,128)(2,1)} %refs_5_.1) | copy-start | bytes 1572868
  19.4 10.0 %collective-permute-start.2 = (f32[4,12,2,256]{3,2,1,0:T(2,128)S(1)}, f32[4,12,2,256]{3,2,1,0:T(2,128)S(1)}, u32[]{:S(2)}, u32[]{:S(2)}) collective-permute-start(f32[4,12,2,256]{3,2,1,0:T(2,128)S(1)} %get-tuple-element.57), channel_id=1, source_target_pairs={{0,1},{1,2},{2,3},{3,0},{4,5},{5,6},{6,7},{7,4},{8,9},{9,10},{10,1... | collective-permute-start | bytes 294920 | tf_op jit(solution)/shard_map/ppermute | solution.py:26
  19.4 12.5 %collective-permute-start.3 = (f32[4,12,2,256]{3,2,1,0:T(2,128)S(1)}, f32[4,12,2,256]{3,2,1,0:T(2,128)S(1)}, u32[]{:S(2)}, u32[]{:S(2)}) collective-permute-start(f32[4,12,2,256]{3,2,1,0:T(2,128)S(1)} %get-tuple-element.58), channel_id=1, source_target_pairs={{0,3},{1,0},{2,1},{3,2},{4,7},{5,4},{6,5},{7,6},{8,11},{9,8},{10,9... | collective-permute-start | bytes 294920 | tf_op jit(solution)/shard_map/ppermute | solution.py:26
  23.3 11.9 %collective-permute-start.7 = (bf16[32,2048]{1,0:T(8,128)(2,1)S(1)}, bf16[32,2048]{1,0:T(8,128)(2,1)S(1)}, u32[]{:S(2)}, u32[]{:S(2)}) collective-permute-start(bf16[32,2048]{1,0:T(8,128)(2,1)S(1)} %slice.181), channel_id=1, source_target_pairs={{0,3},{1,0},{2,1},{3,2},{4,7},{5,4},{6,5},{7,6},{8,11},{9,8},{10,9... | collective-permute-start | bytes 393224 | tf_op jit(solution)/shard_map/ppermute | solution.py:26
  27.3 9.8 %collective-permute-start.6 = (bf16[32,2048]{1,0:T(8,128)(2,1)S(1)}, bf16[32,2048]{1,0:T(8,128)(2,1)S(1)}, u32[]{:S(2)}, u32[]{:S(2)}) collective-permute-start(bf16[32,2048]{1,0:T(8,128)(2,1)S(1)} %slice.180), channel_id=1, source_target_pairs={{0,1},{1,2},{2,3},{3,0},{4,5},{5,6},{6,7},{7,4},{8,9},{9,10},{10,1... | collective-permute-start | bytes 393224 | tf_op jit(solution)/shard_map/ppermute | solution.py:26
  37.5 7.0 %collective-permute-start.9 = (bf16[256,128]{1,0:T(8,128)(2,1)S(1)}, bf16[256,128]{1,0:T(8,128)(2,1)S(1)}, u32[]{:S(2)}, u32[]{:S(2)}) collective-permute-start(bf16[256,128]{1,0:T(8,128)(2,1)S(1)} %shard_map.153.refs_3_), channel_id=1, source_target_pairs={{0,2},{1,3},{2,0},{3,1},{4,6},{5,7},{6,4},{7,5},{8,10},{9,11},{10,... | collective-permute-start | bytes 196616 | tf_op jit(solution)/shard_map/ppermute | solution.py:26
  40.0 4.6 %collective-permute-start.10 = (bf16[256,128]{1,0:T(8,128)(2,1)S(1)}, bf16[256,128]{1,0:T(8,128)(2,1)S(1)}, u32[]{:S(2)}, u32[]{:S(2)}) collective-permute-start(bf16[256,128]{1,0:T(8,128)(2,1)S(1)} %shard_map.153.refs_3_), channel_id=1, source_target_pairs={{0,3},{1,0},{2,1},{3,2},{4,7},{5,4},{6,5},{7,6},{8,11},{9,8},{10,9... | collective-permute-start | bytes 196616 | tf_op jit(solution)/shard_map/ppermute | solution.py:26
  41.6 6.1 %collective-permute-start.8 = (bf16[256,128]{1,0:T(8,128)(2,1)S(1)}, bf16[256,128]{1,0:T(8,128)(2,1)S(1)}, u32[]{:S(2)}, u32[]{:S(2)}) collective-permute-start(bf16[256,128]{1,0:T(8,128)(2,1)S(1)} %shard_map.153.refs_3_), channel_id=1, source_target_pairs={{0,1},{1,2},{2,3},{3,0},{4,5},{5,6},{6,7},{7,4},{8,9},{9,10},{10,1... | collective-permute-start | bytes 196616 | tf_op jit(solution)/shard_map/ppermute | solution.py:26
  48.4 70.7 %all-gather.9.cloned.1.call-start = ((), (), s32[]{:S(2)}) async-start(), calls=%async_computation | async-start | bytes 2359296 | tf_op jit(solution)/shard_map/all_gather | solution.py:777
  51.1 8.1 %collective-permute-start.11 = (bf16[4,256,128]{2,1,0:T(8,128)(2,1)S(1)}, bf16[4,256,128]{2,1,0:T(8,128)(2,1)S(1)}, u32[]{:S(2)}, u32[]{:S(2)}) collective-permute-start(bf16[4,256,128]{2,1,0:T(8,128)(2,1)S(1)} %copy-done.4), channel_id=1, source_target_pairs={{0,4},{4,8},{8,12},{12,16},{16,20},{20,24},{24,28},{28,0},{1,5},{5... | collective-permute-start | bytes 786440 | tf_op jit(solution)/shard_map/ppermute | solution.py:26
  51.1 10.4 %collective-permute-start.12 = (bf16[4,256,128]{2,1,0:T(8,128)(2,1)S(1)}, bf16[4,256,128]{2,1,0:T(8,128)(2,1)S(1)}, u32[]{:S(2)}, u32[]{:S(2)}) collective-permute-start(bf16[4,256,128]{2,1,0:T(8,128)(2,1)S(1)} %copy-done.4), channel_id=1, source_target_pairs={{0,28},{4,0},{8,4},{12,8},{16,12},{20,16},{24,20},{28,24},{1,29},{... | collective-permute-start | bytes 786440 | tf_op jit(solution)/shard_map/ppermute | solution.py:26
  58.0 23.0 %copy-start.9 = (s32[1,8,32]{2,1,0:T(8,128)S(1)}, s32[1,8,32]{2,1,0:T(8,128)}, u32[]{:S(2)}) copy-start(s32[1,8,32]{2,1,0:T(8,128)} %param.17) | copy-start | bytes 3076
  64.3 6.2 %collective-permute-start.13 = (bf16[256,128]{1,0:T(8,128)(2,1)S(1)}, bf16[256,128]{1,0:T(8,128)(2,1)S(1)}, u32[]{:S(2)}, u32[]{:S(2)}) collective-permute-start(bf16[256,128]{1,0:T(8,128)(2,1)S(1)} %get-tuple-element.61.refs_3_), channel_id=1, source_target_pairs={{0,1},{1,2},{2,3},{3,0},{4,5},{5,6},{6,7},{7,4},{8,9},{9,10},{10,1... | collective-permute-start | bytes 196616 | tf_op jit(solution)/shard_map/ppermute | solution.py:26
  64.4 6.2 %collective-permute-start.14 = (bf16[256,128]{1,0:T(8,128)(2,1)S(1)}, bf16[256,128]{1,0:T(8,128)(2,1)S(1)}, u32[]{:S(2)}, u32[]{:S(2)}) collective-permute-start(bf16[256,128]{1,0:T(8,128)(2,1)S(1)} %get-tuple-element.61.refs_3_), channel_id=1, source_target_pairs={{0,2},{1,3},{2,0},{3,1},{4,6},{5,7},{6,4},{7,5},{8,10},{9,11},{10,... | collective-permute-start | bytes 196616 | tf_op jit(solution)/shard_map/ppermute | solution.py:26
  66.7 6.0 %collective-permute-start.15 = (bf16[256,128]{1,0:T(8,128)(2,1)S(1)}, bf16[256,128]{1,0:T(8,128)(2,1)S(1)}, u32[]{:S(2)}, u32[]{:S(2)}) collective-permute-start(bf16[256,128]{1,0:T(8,128)(2,1)S(1)} %get-tuple-element.61.refs_3_), channel_id=1, source_target_pairs={{0,3},{1,0},{2,1},{3,2},{4,7},{5,4},{6,5},{7,6},{8,11},{9,8},{10,9... | collective-permute-start | bytes 196616 | tf_op jit(solution)/shard_map/ppermute | solution.py:26
  73.4 93.0 %all-gather.13.cloned.1.call-start = ((), (), s32[]{:S(2)}) async-start(), calls=%async_computation.2 | async-start | bytes 3981312 | tf_op jit(solution)/shard_map/all_gather | solution.py:807
  73.4 11.7 %collective-permute-start.16 = (bf16[4,256,128]{2,1,0:T(8,128)(2,1)}, bf16[4,256,128]{2,1,0:T(8,128)(2,1)S(1)}, u32[]{:S(2)}, u32[]{:S(2)}) collective-permute-start(bf16[4,256,128]{2,1,0:T(8,128)(2,1)} %pad_maximum_fusion.8.refs_0_), channel_id=1, source_target_pairs={{0,4},{4,8},{8,12},{12,16},{16,20},{20,24},{24,28},{28,0},{1,5},{5... | collective-permute-start | bytes 786440 | tf_op jit(solution)/shard_map/ppermute | solution.py:26
  74.5 10.6 %collective-permute-start.20 = (bf16[4,256,128]{2,1,0:T(8,128)(2,1)}, bf16[4,256,128]{2,1,0:T(8,128)(2,1)S(1)}, u32[]{:S(2)}, u32[]{:S(2)}) collective-permute-start(bf16[4,256,128]{2,1,0:T(8,128)(2,1)} %pad_maximum_fusion.8.refs_0_), channel_id=1, source_target_pairs={{0,28},{4,0},{8,4},{12,8},{16,12},{20,16},{24,20},{28,24},{1,29},{... | collective-permute-start | bytes 786440 | tf_op jit(solution)/shard_map/ppermute | solution.py:26
  76.1 7.8 %collective-permute-start.17 = (bf16[64,512]{1,0:T(8,128)(2,1)S(1)}, bf16[64,512]{1,0:T(8,128)(2,1)S(1)}, u32[]{:S(2)}, u32[]{:S(2)}) collective-permute-start(bf16[64,512]{1,0:T(8,128)(2,1)S(1)} %get-tuple-element.124), channel_id=1, source_target_pairs={{0,1},{1,2},{2,3},{3,0},{4,5},{5,6},{6,7},{7,4},{8,9},{9,10},{10,1... | collective-permute-start | bytes 196616 | tf_op jit(solution)/shard_map/ppermute | solution.py:26
  78.2 6.3 %collective-permute-start.18 = (bf16[64,512]{1,0:T(8,128)(2,1)S(1)}, bf16[64,512]{1,0:T(8,128)(2,1)S(1)}, u32[]{:S(2)}, u32[]{:S(2)}) collective-permute-start(bf16[64,512]{1,0:T(8,128)(2,1)S(1)} %get-tuple-element.123), channel_id=1, source_target_pairs={{0,2},{1,3},{2,0},{3,1},{4,6},{5,7},{6,4},{7,5},{8,10},{9,11},{10,... | collective-permute-start | bytes 196616 | tf_op jit(solution)/shard_map/ppermute | solution.py:26
  80.5 4.6 %collective-permute-start.19 = (bf16[64,512]{1,0:T(8,128)(2,1)S(1)}, bf16[64,512]{1,0:T(8,128)(2,1)S(1)}, u32[]{:S(2)}, u32[]{:S(2)}) collective-permute-start(bf16[64,512]{1,0:T(8,128)(2,1)S(1)} %get-tuple-element.122), channel_id=1, source_target_pairs={{0,3},{1,0},{2,1},{3,2},{4,7},{5,4},{6,5},{7,6},{8,11},{9,8},{10,9... | collective-permute-start | bytes 196616 | tf_op jit(solution)/shard_map/ppermute | solution.py:26
  88.0 7.2 %collective-permute-start.23 = (bf16[256,128]{1,0:T(8,128)(2,1)S(1)}, bf16[256,128]{1,0:T(8,128)(2,1)S(1)}, u32[]{:S(2)}, u32[]{:S(2)}) collective-permute-start(bf16[256,128]{1,0:T(8,128)(2,1)S(1)} %get-tuple-element.63.refs_0_), channel_id=1, source_target_pairs={{0,3},{1,0},{2,1},{3,2},{4,7},{5,4},{6,5},{7,6},{8,11},{9,8},{10,9... | collective-permute-start | bytes 196616 | tf_op jit(solution)/shard_map/ppermute | solution.py:26
  90.1 6.1 %collective-permute-start.21 = (bf16[256,128]{1,0:T(8,128)(2,1)S(1)}, bf16[256,128]{1,0:T(8,128)(2,1)S(1)}, u32[]{:S(2)}, u32[]{:S(2)}) collective-permute-start(bf16[256,128]{1,0:T(8,128)(2,1)S(1)} %get-tuple-element.63.refs_0_), channel_id=1, source_target_pairs={{0,1},{1,2},{2,3},{3,0},{4,5},{5,6},{6,7},{7,4},{8,9},{9,10},{10,1... | collective-permute-start | bytes 196616 | tf_op jit(solution)/shard_map/ppermute | solution.py:26
  90.1 6.1 %collective-permute-start.22 = (bf16[256,128]{1,0:T(8,128)(2,1)S(1)}, bf16[256,128]{1,0:T(8,128)(2,1)S(1)}, u32[]{:S(2)}, u32[]{:S(2)}) collective-permute-start(bf16[256,128]{1,0:T(8,128)(2,1)S(1)} %get-tuple-element.63.refs_0_), channel_id=1, source_target_pairs={{0,2},{1,3},{2,0},{3,1},{4,6},{5,7},{6,4},{7,5},{8,10},{9,11},{10,... | collective-permute-start | bytes 196616 | tf_op jit(solution)/shard_map/ppermute | solution.py:26
  96.9 5.0 %collective-permute-start.26 = (bf16[272,128]{1,0:T(8,128)(2,1)S(1)}, bf16[272,128]{1,0:T(8,128)(2,1)S(1)}, u32[]{:S(2)}, u32[]{:S(2)}) collective-permute-start(bf16[272,128]{1,0:T(8,128)(2,1)S(1)} %get-tuple-element.68), channel_id=1, source_target_pairs={{0,3},{1,0},{2,1},{3,2},{4,7},{5,4},{6,5},{7,6},{8,11},{9,8},{10,9... | collective-permute-start | bytes 208904 | tf_op jit(solution)/shard_map/ppermute | solution.py:26
  99.8 6.2 %collective-permute-start.24 = (bf16[272,128]{1,0:T(8,128)(2,1)S(1)}, bf16[272,128]{1,0:T(8,128)(2,1)S(1)}, u32[]{:S(2)}, u32[]{:S(2)}) collective-permute-start(bf16[272,128]{1,0:T(8,128)(2,1)S(1)} %get-tuple-element.66), channel_id=1, source_target_pairs={{0,1},{1,2},{2,3},{3,0},{4,5},{5,6},{6,7},{7,4},{8,9},{9,10},{10,1... | collective-permute-start | bytes 208904 | tf_op jit(solution)/shard_map/ppermute | solution.py:26
  99.9 7.4 %collective-permute-start.25 = (bf16[272,128]{1,0:T(8,128)(2,1)S(1)}, bf16[272,128]{1,0:T(8,128)(2,1)S(1)}, u32[]{:S(2)}, u32[]{:S(2)}) collective-permute-start(bf16[272,128]{1,0:T(8,128)(2,1)S(1)} %get-tuple-element.67), channel_id=1, source_target_pairs={{0,2},{1,3},{2,0},{3,1},{4,6},{5,7},{6,4},{7,5},{8,10},{9,11},{10,... | collective-permute-start | bytes 208904 | tf_op jit(solution)/shard_map/ppermute | solution.py:26
  128.6 4.3 %collective-permute-start.30 = (bf16[4,64,512]{2,1,0:T(8,128)(2,1)S(1)}, bf16[4,64,512]{2,1,0:T(8,128)(2,1)S(1)}, u32[]{:S(2)}, u32[]{:S(2)}) collective-permute-start(bf16[4,64,512]{2,1,0:T(8,128)(2,1)S(1)} %dynamic-slice_bitcast_fusion), channel_id=1, source_target_pairs={{0,4},{4,0},{8,12},{12,8},{16,20},{20,16},{24,28},{28,24},{1,5},{5... | collective-permute-start | bytes 786440 | tf_op jit(solution)/shard_map/ppermute | solution.py:651
  133.1 9.7 %collective-permute-start.31 = (bf16[2,64,512]{2,1,0:T(8,128)(2,1)S(1)}, bf16[2,64,512]{2,1,0:T(8,128)(2,1)S(1)}, u32[]{:S(2)}, u32[]{:S(2)}) collective-permute-start(bf16[2,64,512]{2,1,0:T(8,128)(2,1)S(1)} %fusion), channel_id=1, source_target_pairs={{0,8},{4,12},{8,0},{12,4},{16,24},{20,28},{24,16},{28,20},{1,9},{5... | collective-permute-start | bytes 393224 | tf_op jit(solution)/shard_map/ppermute | solution.py:651
  133.7 6.8 %collective-permute-start.27 = (bf16[256,128]{1,0:T(8,128)(2,1)S(1)}, bf16[256,128]{1,0:T(8,128)(2,1)S(1)}, u32[]{:S(2)}, u32[]{:S(2)}) collective-permute-start(bf16[256,128]{1,0:T(8,128)(2,1)S(1)} %get-tuple-element.77), channel_id=1, source_target_pairs={{0,1},{1,2},{2,3},{3,0},{4,5},{5,6},{6,7},{7,4},{8,9},{9,10},{10,1... | collective-permute-start | bytes 196616 | tf_op jit(solution)/shard_map/ppermute | solution.py:26
  133.7 8.4 %collective-permute-start.28 = (bf16[256,128]{1,0:T(8,128)(2,1)S(1)}, bf16[256,128]{1,0:T(8,128)(2,1)S(1)}, u32[]{:S(2)}, u32[]{:S(2)}) collective-permute-start(bf16[256,128]{1,0:T(8,128)(2,1)S(1)} %get-tuple-element.78), channel_id=1, source_target_pairs={{0,2},{1,3},{2,0},{3,1},{4,6},{5,7},{6,4},{7,5},{8,10},{9,11},{10,... | collective-permute-start | bytes 196616 | tf_op jit(solution)/shard_map/ppermute | solution.py:26
  136.5 5.6 %collective-permute-start.29 = (bf16[256,128]{1,0:T(8,128)(2,1)S(1)}, bf16[256,128]{1,0:T(8,128)(2,1)S(1)}, u32[]{:S(2)}, u32[]{:S(2)}) collective-permute-start(bf16[256,128]{1,0:T(8,128)(2,1)S(1)} %get-tuple-element.79), channel_id=1, source_target_pairs={{0,3},{1,0},{2,1},{3,2},{4,7},{5,4},{6,5},{7,6},{8,11},{9,8},{10,9... | collective-permute-start | bytes 196616 | tf_op jit(solution)/shard_map/ppermute | solution.py:26
  142.9 12.9 %collective-permute-start.32 = (bf16[1,64,512]{2,1,0:T(8,128)(2,1)S(1)}, bf16[1,64,512]{2,1,0:T(8,128)(2,1)S(1)}, u32[]{:S(2)}, u32[]{:S(2)}) collective-permute-start(bf16[1,64,512]{2,1,0:T(8,128)(2,1)S(1)} %dynamic-slice_convert_fusion), channel_id=1, source_target_pairs={{0,16},{4,20},{8,24},{12,28},{16,0},{20,4},{24,8},{28,12},{1,17},{... | collective-permute-start | bytes 196616 | tf_op jit(solution)/shard_map/ppermute | solution.py:651
  164.3 14.1 %collective-permute-start.33 = (bf16[31,64,128]{2,1,0:T(8,128)(2,1)}, bf16[31,64,128]{2,1,0:T(8,128)(2,1)S(1)}, u32[]{:S(2)}, u32[]{:S(2)}) collective-permute-start(bf16[31,64,128]{2,1,0:T(8,128)(2,1)} %get-tuple-element.88.refs_0_), channel_id=1, source_target_pairs={{0,8},{4,12},{8,0},{12,4},{16,24},{20,28},{24,16},{28,20},{1,9},{5... | collective-permute-start | bytes 1523720 | tf_op jit(solution)/shard_map/ppermute | solution.py:651
  165.8 13.7 %collective-permute-start.34 = (bf16[31,64,128]{2,1,0:T(8,128)(2,1)}, bf16[31,64,128]{2,1,0:T(8,128)(2,1)S(1)}, u32[]{:S(2)}, u32[]{:S(2)}) collective-permute-start(bf16[31,64,128]{2,1,0:T(8,128)(2,1)} %get-tuple-element.88.refs_0_), channel_id=1, source_target_pairs={{0,16},{4,20},{8,24},{12,28},{16,0},{20,4},{24,8},{28,12},{1,17},{... | collective-permute-start | bytes 1523720 | tf_op jit(solution)/shard_map/ppermute | solution.py:651
  166.4 15.9 %collective-permute-start.36 = (bf16[31,64,128]{2,1,0:T(8,128)(2,1)}, bf16[31,64,128]{2,1,0:T(8,128)(2,1)S(1)}, u32[]{:S(2)}, u32[]{:S(2)}) collective-permute-start(bf16[31,64,128]{2,1,0:T(8,128)(2,1)} %get-tuple-element.88.refs_0_), channel_id=1, source_target_pairs={{0,4},{4,0},{8,12},{12,8},{16,20},{20,16},{24,28},{28,24},{1,5},{5... | collective-permute-start | bytes 1523720 | tf_op jit(solution)/shard_map/ppermute | solution.py:651
  168.4 13.9 %copy-start.8 = (bf16[31,64,128]{2,1,0:T(8,128)(2,1)S(1)}, bf16[31,64,128]{2,1,0:T(8,128)(2,1)}, u32[]{:S(2)}) copy-start(bf16[31,64,128]{2,1,0:T(8,128)(2,1)} %get-tuple-element.88.refs_0_) | copy-start | bytes 1523716
  179.5 2.7 %collective-permute-start.37 = (bf16[31,64,128]{2,1,0:T(8,128)(2,1)S(1)}, bf16[31,64,128]{2,1,0:T(8,128)(2,1)S(1)}, u32[]{:S(2)}, u32[]{:S(2)}) collective-permute-start(bf16[31,64,128]{2,1,0:T(8,128)(2,1)S(1)} %collective-permute-done.33.refs_1_), channel_id=1, source_target_pairs={{0,4},{4,0},{8,12},{12,8},{16,20},{20,16},{24,28},{28,24},{1,5},{5... | collective-permute-start | bytes 1523720 | tf_op jit(solution)/shard_map/ppermute | solution.py:651
  179.5 2.7 %collective-permute-start.38 = (bf16[31,64,128]{2,1,0:T(8,128)(2,1)S(1)}, bf16[31,64,128]{2,1,0:T(8,128)(2,1)S(1)}, u32[]{:S(2)}, u32[]{:S(2)}) collective-permute-start(bf16[31,64,128]{2,1,0:T(8,128)(2,1)S(1)} %collective-permute-done.34.refs_2_), channel_id=1, source_target_pairs={{0,4},{4,0},{8,12},{12,8},{16,20},{20,16},{24,28},{28,24},{1,5},{5... | collective-permute-start | bytes 1523720 | tf_op jit(solution)/shard_map/ppermute | solution.py:651
  180.1 8.3 %collective-permute-start.39 = (bf16[16,64,128]{2,1,0:T(8,128)(2,1)S(1)}, bf16[16,64,128]{2,1,0:T(8,128)(2,1)S(1)}, u32[]{:S(2)}, u32[]{:S(2)}) collective-permute-start(bf16[16,64,128]{2,1,0:T(8,128)(2,1)S(1)} %slice.155), channel_id=1, source_target_pairs={{0,16},{4,20},{8,24},{12,28},{16,0},{20,4},{24,8},{28,12},{1,17},{... | collective-permute-start | bytes 786440 | tf_op jit(solution)/shard_map/ppermute | solution.py:651
  180.8 7.6 %collective-permute-start.35 = (bf16[15,64,128]{2,1,0:T(8,128)(2,1)S(1)}, bf16[15,64,128]{2,1,0:T(8,128)(2,1)S(1)}, u32[]{:S(2)}, u32[]{:S(2)}) collective-permute-start(bf16[15,64,128]{2,1,0:T(8,128)(2,1)S(1)} %slice.154), channel_id=1, source_target_pairs={{0,8},{4,12},{8,0},{12,4},{16,24},{20,28},{24,16},{28,20},{1,9},{5... | collective-permute-start | bytes 737288 | tf_op jit(solution)/shard_map/ppermute | solution.py:651
  188.3 1.9 collective-permute-start.41
  188.4 1.8 collective-permute-start.40
  (7 other events, 26.8 us)
Sparse Core Ops, SparseCore 0:
  48.5 27.6 all-gather.10
  78.7 27.6 all-gather.8
  128.8 34.0 all-gather.12
